TPU v7x, 32 devices: a whole 2x2x4 slice. The times are simulated.
32 devices in a mesh: dom: 8 (over y, x, core), tile: 4 (over z).
Axes of the slice: x: 2, y: 2, z: 4, core: 2. Of those that a mesh axis runs over, the one named last changes fastest.
Arguments:
- vorticity: float32 [32, 2, 64, 2048], P('dom', None, 'tile'), may hold values from -6 to 6
- streamfunction: float32 [32, 2, 64, 2048], P('dom', None, 'tile'), may hold values from -6 to 6
- model_noise: float32 [2, 32, 2, 64, 2048], P(None, 'dom', None, 'tile'), may hold values from -3 to 3
- offspring: int32 [2, 32], replicated, may hold values from 0 to 8, as said below
- footprint: float32 [8, 16, 1024, 1024], P('tile', 'dom'), may hold values from -0.1875 to 0.1875
- observed: float32 [8, 16, 1024], P('tile', 'dom'), may hold values from -6 to 6
- precision: float32 [8, 16, 1024], P('tile', 'dom'), may hold values from 0.002 to 0.02
- block_rows: int32 [8, 16], P('tile', 'dom'), may hold values from 0 to 8
Outputs:
- vorticity_out: float32 [32, 2, 64, 2048], P('dom', None, 'tile')
- streamfunction_out: float32 [32, 2, 64, 2048], P('dom', None, 'tile')
- mean_loglik: float32 [2, 32], replicated
- weights: float32 [2, 32], replicated
Inputs may be any that keep to these rules, and one draw needn't show every extreme that they name: Each row sums to 32; in each row exactly one member has 8 offspring.
All inputs are finite; a program needn't handle non-finite values.
Results may differ from a plain program's by a relative error of at most 0.00055.
Values sent between devices are 32-bit elements; how exact they have to be, the bound alone decides.
No kernel may reach another device: no remote copies, remote signals or barrier semaphores. Data moves between devices by JAX's collectives and lax.ppermute only.
A program may use at most 192 MiB of HBM per device.

v0:
```python
import functools

import jax
import jax.numpy as jnp
from jax import lax
from jax.experimental import pallas as pl
from jax.experimental.pallas import tpu as pltpu
from jax.sharding import PartitionSpec as P

STEPS = 6
CYCLES = 2
BW = 128
BR = 8
ROWS = 16
MEM = 4
LAYERS = 2
SUB = 8
SEG = 16
F32 = jnp.float32
VMEM_LIMIT = 56 * 1024 * 1024
DRAG_STEP = 0.1 * 0.2


def lanes():
    return lax.broadcasted_iota(jnp.int32, (SUB, BW), 1)


def lane_roll(x, shift):
    return pltpu.roll(x, shift % BW, axis=1)


def ring_row(blocks, load, other, emit, drag):
    lane = lanes()
    at_last, at_first = lane == BW - 1, lane == 0
    cur = (load(1, 0, 0), load(0, 0, 0))
    left = tuple(lane_roll(v, -1) for v in cur)
    right = tuple(lane_roll(v, 1) for v in cur)
    first_left = left
    before = tuple(lane_roll(load(f, blocks - 1, 0), 1) for f in (1, 0))
    for b in range(blocks):
        if b + 1 < blocks:
            nxt = (load(1, b + 1, 0), load(0, b + 1, 0))
            nxt_left = tuple(lane_roll(v, -1) for v in nxt)
            nxt_right = tuple(lane_roll(v, 1) for v in nxt)
        else:
            nxt, nxt_left, nxt_right = None, first_left, None
        psi, q = cur
        psi_e, q_e = (jnp.where(at_last, n, c) for n, c in zip(nxt_left, left))
        psi_w, q_w = (jnp.where(at_first, p, c) for p, c in zip(before, right))
        psi_n, psi_s = load(1, b, 1), load(1, b, -1)
        q_n, q_s = load(0, b, 1), load(0, b, -1)
        around = (psi_n + psi_s) + (psi_e + psi_w)
        along = psi_e - psi_w
        psi_new = (around + other(b, psi) - q) * 0.2
        change = along * ((q_n - q_s) + 1.0) - (psi_n - psi_s) * (q_e - q_w)
        q_new = q - 0.025 * change
        if drag is not None:
            q_new = q_new - drag * (around - 4.0 * psi)
        emit(b, q_new, psi_new)
        before = right
        cur, left, right = nxt, nxt_left, nxt_right


def halo_pack(take, rows):
    segment = ((lanes() + SEG // 2) // SEG) % SUB
    lower = lanes() < BW // 2
    packed = None
    for j in range(rows):
        before, after = take(j)
        edge = lane_roll(jnp.where(lower, after, before), SEG * j)
        packed = edge if packed is None else jnp.where(segment == j, edge, packed)
    return packed


def pack_state(q_ref, p_ref, n_ref, main_ref, up_ref, down_ref, *, blocks):
    for b in range(blocks):
        cols = slice(b * BW, (b + 1) * BW)
        for m in range(MEM):
            for l in range(LAYERS):
                for g in range(ROWS // SUB):
                    rows = slice(g * SUB, (g + 1) * SUB)
                    start = g * SUB * 16 + l * MEM + m
                    main_ref[b, pl.ds(start, SUB, stride=16), :] = (
                        q_ref[m, l, rows, cols] + n_ref[0, m, l, rows, cols]
                    )
                    main_ref[b, pl.ds(start + SUB, SUB, stride=16), :] = p_ref[m, l, rows, cols]
        up_ref[b] = main_ref[b, (ROWS - STEPS) * 16 :, :]
        down_ref[b] = main_ref[b, : STEPS * 16, :]


def pack_noise(n_ref, out_ref, work, edges, *, groups, per):
    blocks = groups * per
    for b in range(blocks):
        for m in range(MEM):
            for l in range(LAYERS):
                for g in range(ROWS // SUB):
                    work[b, pl.ds(g * SUB * SUB + l * MEM + m, SUB, stride=SUB), :] = n_ref[
                        0, m, l, g * SUB : (g + 1) * SUB, b * BW : (b + 1) * BW
                    ]
    for d in range(groups):
        for h in range(2):
            def take(j):
                row = slice((h * SUB + j) * SUB, (h * SUB + j + 1) * SUB)
                return work[(d * per - 1) % blocks, row, :], work[(d * per + per) % blocks, row, :]

            edges[d, h * 16 : h * 16 + SUB, :] = halo_pack(take, SUB)
            edges[d, h * 16 + SUB : (h + 1) * 16, :] = jnp.zeros((SUB, BW), F32)
        for m in range(MEM):
            for c in range(per):
                for v in range(4):
                    out_ref[d, m, c * 4 + v] = work[d * per + c, pl.ds(v * 32 + m, SUB, stride=MEM), :]
            out_ref[d, m, per * 4] = edges[d, pl.ds(m, SUB, stride=MEM), :]


def clear_wall(buf, row, planes, edge):
    zero = jnp.zeros((STEPS * row, BW), F32)

    @pl.when(edge[0] == 0)
    def _():
        for b in range(planes):
            buf[b, : STEPS * row, :] = zero

    @pl.when(edge[0] == edge[1] - 1)
    def _():
        for b in range(planes):
            buf[b, (STEPS + ROWS) * row :, :] = zero


def row_range(edge, step):
    low = jnp.where(edge[0] == 0, STEPS, step + 1)
    high = jnp.where(edge[0] == edge[1] - 1, STEPS + ROWS, 2 * STEPS + ROWS - 1 - step)
    return low, high


def advance_members(edge, main_ref, up_ref, down_ref, out_ref, first, second, edges, *, groups, per):
    blocks = groups * per
    row = 2 * SUB
    for b in range(blocks):
        first[b, : STEPS * row, :] = up_ref[b]
        first[b, STEPS * row : (STEPS + ROWS) * row, :] = main_ref[b]
        first[b, (STEPS + ROWS) * row :, :] = down_ref[b]
    clear_wall(second, row, blocks, edge)
    drag = jnp.where(lax.broadcasted_iota(jnp.int32, (SUB, BW), 0) >= MEM, DRAG_STEP, 0.0).astype(F32)
    src, dst = first, second
    for step in range(STEPS):
        def body(i, _, src=src, dst=dst):
            def at(f, di):
                return pl.ds(pl.multiple_of((i + di) * row + f * SUB, SUB), SUB)

            def emit(b, q_new, psi_new):
                dst[b, at(0, 0), :] = q_new
                dst[b, at(1, 0), :] = psi_new

            ring_row(
                blocks,
                lambda f, b, di: src[b, at(f, di), :],
                lambda b, psi: pltpu.roll(psi, MEM, axis=0),
                emit,
                drag,
            )
            return 0

        low, high = row_range(edge, step)
        lax.fori_loop(low, high, body, 0)
        src, dst = dst, src
    base = STEPS * row
    for d in range(groups):
        for h in range(2):
            for f in range(2):
                def take(j):
                    s = base + (h * SUB + j) * row + f * SUB
                    rows = slice(s, s + SUB)
                    return src[(d * per - 1) % blocks, rows, :], src[(d * per + per) % blocks, rows, :]

                edges[d, (h * 2 + f) * SUB : (h * 2 + f + 1) * SUB, :] = halo_pack(take, SUB)
        for m in range(MEM):
            for c in range(per):
                for v in range(8):
                    out_ref[d, m, c * 8 + v] = src[
                        d * per + c, pl.ds(base + v * 32 + m, SUB, stride=MEM), :
                    ]
            out_ref[d, m, per * 8] = edges[d, pl.ds(m, SUB, stride=MEM), :]


def resample(
    parent, x_ref, n_ref, main_ref, edge_ref, up_ref, down_ref, z_ref, noise, *, members, per
):
    size = per * 8 + 1
    row = 4 * members

    def one(k, _):
        p = parent[k]
        for c in range(per):
            for v in range(8):
                main_ref[c, pl.ds(v * 8 * members + k, SUB, stride=members), :] = x_ref[p, c * 8 + v]
            for v in range(4):
                noise[c, pl.ds(v * 8 * members + k, SUB, stride=members), :] = n_ref[k, c * 4 + v]
            for g in range(2):
                for r in range(SUB):
                    j = g * SUB + r
                    z_ref[c, pl.ds(j * members + k, 1), :] = x_ref[
                        k, c * 8 + j // 2, (j % 2) * 4 + 2 : (j % 2) * 4 + 3, :
                    ]
        edge_ref[pl.ds(k, SUB, stride=members), :] = x_ref[p, size - 1] + n_ref[k, per * 4]
        return 0

    lax.fori_loop(0, members, one, 0)
    for c in range(per):
        for r in range(ROWS):
            s = slice(r * row, r * row + 2 * members)
            main_ref[c, s, :] = main_ref[c, s, :] + noise[c, r * 2 * members : (r + 1) * 2 * members, :]
        for r in range(STEPS):
            up_ref[c * STEPS + r] = main_ref[c, (ROWS - STEPS + r) * row : (ROWS - STEPS + r + 1) * row, :]
            down_ref[c * STEPS + r] = main_ref[c, r * row : (r + 1) * row, :]
    up_ref[per * STEPS] = edge_ref[row:, :]
    down_ref[per * STEPS] = edge_ref[:row, :]


def advance_columns(
    edge, parent, main_ref, edge_ref, up_ref, down_ref, out_ref, z_ref, first, second, *, members, per
):
    row = 4 * members
    top = (STEPS + ROWS) * row
    for c in range(per):
        for r in range(STEPS):
            first[c, r * row : (r + 1) * row, :] = up_ref[c * STEPS + r]
            first[c, top + r * row : top + (r + 1) * row, :] = down_ref[c * STEPS + r]
        first[c, STEPS * row : top, :] = main_ref[c]
    for j in range(SUB):
        for h in range(2):
            s = (STEPS + h * SUB + j) * row
            first[per, s : s + row, :] = lane_roll(edge_ref[h * row : (h + 1) * row, :], -SEG * j)
        if j >= SUB - STEPS:
            s = (j - (SUB - STEPS)) * row
            first[per, s : s + row, :] = lane_roll(up_ref[per * STEPS], -SEG * j)
        if j < STEPS:
            s = top + j * row
            first[per, s : s + row, :] = lane_roll(down_ref[per * STEPS], -SEG * j)
    clear_wall(second, row, per + 1, edge)
    src, dst = first, second
    for step in range(STEPS):
        def body(i, _, src=src, dst=dst):
            for g in range(members // SUB):
                for l in range(LAYERS):
                    def at(f, layer, di):
                        s = (i + di) * row + (f * 2 + layer) * members + g * SUB
                        return pl.ds(pl.multiple_of(s, SUB), SUB)

                    def emit(b, q_new, psi_new):
                        dst[b, at(0, l, 0), :] = q_new
                        dst[b, at(1, l, 0), :] = psi_new

                    ring_row(
                        per + 1,
                        lambda f, b, di: src[b, at(f, l, di), :],
                        lambda b, psi: src[b, at(1, 1 - l, 0), :],
                        emit,
                        DRAG_STEP if l == 1 else None,
                    )
            return 0

        low, high = row_range(edge, step)
        lax.fori_loop(low, high, body, 0)
        src, dst = dst, src

    def one(k, _):
        p = parent[k]
        for c in range(per):
            for v in range(8):
                out_ref[k, c * 8 + v] = src[
                    c, pl.ds(STEPS * row + v * 8 * members + p, SUB, stride=members), :
                ]
        return 0

    lax.fori_loop(0, members, one, 0)
    for c in range(per):
        for r in range(ROWS):
            s = (STEPS + r) * row + 2 * members
            z_ref[c, r * members : (r + 1) * members, :] = src[c, s : s + members, :]


def unpack_state(y_ref, q_ref, p_ref, *, per):
    for c in range(per):
        for m in range(MEM):
            for l in range(LAYERS):
                for g in range(ROWS // SUB):
                    rows, cols = slice(g * SUB, (g + 1) * SUB), slice(c * BW, (c + 1) * BW)
                    s = c * 64 + g * 32 + l
                    q_ref[m, l, rows, cols] = y_ref[0, m, pl.ds(s, SUB, stride=4), :]
                    p_ref[m, l, rows, cols] = y_ref[0, m, pl.ds(s + 2, SUB, stride=4), :]


def score(rows_ref, z_ref, f_ref, o_ref, w_ref, out_ref, patch, total, *, members, per, chunk):
    a, c, j = pl.program_id(0), pl.program_id(1), pl.program_id(2)

    @pl.when((a == 0) & (c == 0) & (j == 0))
    def _():
        total[...] = jnp.zeros_like(total)

    @pl.when(j == 0)
    def _():
        start = rows_ref[a, c]
        for r in range(BR):
            s = pl.multiple_of((start + r) * members, SUB)
            part = z_ref[c, pl.ds(s, members), :]
            high = part.astype(jnp.bfloat16)
            patch[:members, r * BW : (r + 1) * BW] = high
            patch[members:, r * BW : (r + 1) * BW] = (part - high.astype(F32)).astype(jnp.bfloat16)

    weights = f_ref[0, 0]
    high = weights.astype(jnp.bfloat16)
    low = (weights - high.astype(F32)).astype(jnp.bfloat16)
    dims = (((1,), (1,)), ((), ()))
    main = lax.dot_general(patch[...], high, dims, preferred_element_type=F32)
    rest = lax.dot_general(patch[:members, :], low, dims, preferred_element_type=F32)
    predicted = main[:members] + (main[members:] + rest)
    miss = o_ref[0, 0] - predicted
    total[...] += w_ref[0, 0] * miss * miss

    @pl.when((a == pl.num_programs(0) - 1) & (c == pl.num_programs(1) - 1) & (j == pl.num_programs(2) - 1))
    def _():
        out_ref[...] = jnp.broadcast_to(jnp.sum(total[...], axis=1, keepdims=True) * -0.5, (members, BW))


def shape(*dims):
    return jax.ShapeDtypeStruct(dims, F32)


def call(kernel, outs, scratch=(), scalars=0, name=None):
    def run(*args):
        specs = [pl.BlockSpec(memory_space=pltpu.SMEM)] * scalars
        specs += [pl.BlockSpec(memory_space=pltpu.VMEM)] * (len(args) - scalars)
        return pl.pallas_call(
            kernel,
            out_shape=outs,
            in_specs=specs,
            out_specs=[pl.BlockSpec(memory_space=pltpu.VMEM)] * len(outs),
            scratch_shapes=list(scratch),
            compiler_params=pltpu.CompilerParams(vmem_limit_bytes=VMEM_LIMIT),
            name=name,
        )(*args)

    return run


def shards(
    vorticity, streamfunction, model_noise, offspring, footprint, observed, precision, block_rows
):
    groups, tiles = lax.axis_size("dom"), lax.axis_size("tile")
    members = offspring.shape[1]
    width = vorticity.shape[3]
    blocks = width // BW
    per = blocks // groups
    bands, observations, cells = footprint.shape[0], footprint.shape[2], footprint.shape[3]

    running = jnp.cumsum(offspring, axis=1)
    slots = jnp.arange(members, dtype=jnp.int32)
    parent = jnp.sum((running[:, None, :] <= slots[None, :, None]).astype(jnp.int32), axis=2)
    parent = jnp.minimum(parent, members - 1)
    edge = jnp.stack([lax.axis_index("tile"), jnp.int32(tiles)]).astype(jnp.int32)

    up = [(i, i + 1) for i in range(tiles - 1)]
    down = [(i + 1, i) for i in range(tiles - 1)]

    fields = (MEM, LAYERS, ROWS)
    step_blocks = blocks // 4
    main, to_up, to_down = pl.pallas_call(
        functools.partial(pack_state, blocks=step_blocks),
        grid=(4,),
        in_specs=[
            pl.BlockSpec(fields + (step_blocks * BW,), lambda i: (0, 0, 0, i)),
            pl.BlockSpec(fields + (step_blocks * BW,), lambda i: (0, 0, 0, i)),
            pl.BlockSpec((1,) + fields + (step_blocks * BW,), lambda i: (0, 0, 0, 0, i)),
        ],
        out_specs=[
            pl.BlockSpec((step_blocks, ROWS * 16, BW), lambda i: (i, 0, 0)),
            pl.BlockSpec((step_blocks, STEPS * 16, BW), lambda i: (i, 0, 0)),
            pl.BlockSpec((step_blocks, STEPS * 16, BW), lambda i: (i, 0, 0)),
        ],
        out_shape=[
            shape(blocks, ROWS * 16, BW),
            shape(blocks, STEPS * 16, BW),
            shape(blocks, STEPS * 16, BW),
        ],
        name="pack_state",
    )(vorticity, streamfunction, model_noise)
    from_below = lax.ppermute(to_up, "tile", up)
    from_above = lax.ppermute(to_down, "tile", down)

    noise = pl.pallas_call(
        functools.partial(pack_noise, groups=groups, per=per),
        grid=(1,),
        in_specs=[pl.BlockSpec((1,) + fields + (width,), lambda i: (1, 0, 0, 0, 0))],
        out_specs=pl.BlockSpec((groups, MEM, per * 4 + 1, SUB, BW), lambda i: (0, 0, 0, 0, 0)),
        out_shape=shape(groups, MEM, per * 4 + 1, SUB, BW),
        scratch_shapes=[pltpu.VMEM((blocks, ROWS * SUB, BW), F32), pltpu.VMEM((groups, 32, BW), F32)],
        name="pack_noise",
    )(model_noise)
    noise = lax.all_to_all(noise, "dom", split_axis=0, concat_axis=0, tiled=True)
    noise = noise.reshape(members, per * 4 + 1, SUB, BW)

    work = (blocks, (ROWS + 2 * STEPS) * 16, BW)
    (sent,) = call(
        functools.partial(advance_members, groups=groups, per=per),
        [shape(groups, MEM, per * 8 + 1, SUB, BW)],
        [pltpu.VMEM(work, F32), pltpu.VMEM(work, F32), pltpu.VMEM((groups, 32, BW), F32)],
        scalars=1,
        name="advance_members",
    )(edge, main, from_below, from_above)
    owned = lax.all_to_all(sent, "dom", split_axis=0, concat_axis=0, tiled=True)
    owned = owned.reshape(members, per * 8 + 1, SUB, BW)

    row = 4 * members
    main, sides, to_up, to_down, surface = call(
        functools.partial(resample, members=members, per=per),
        [
            shape(per, ROWS * row, BW),
            shape(2 * row, BW),
            shape(per * STEPS + 1, row, BW),
            shape(per * STEPS + 1, row, BW),
            shape(per, ROWS * members, BW),
        ],
        [pltpu.VMEM((per, ROWS * 2 * members, BW), F32)],
        scalars=1,
        name="resample",
    )(parent[0], owned, noise)
    from_below = lax.ppermute(to_up, "tile", up)
    from_above = lax.ppermute(to_down, "tile", down)

    def likelihood(surface):
        chunk = 512
        obs = (bands, per, 1, observations)
        out = pl.pallas_call(
            functools.partial(score, members=members, per=per, chunk=chunk),
            grid=(bands, per, observations // chunk),
            in_specs=[
                pl.BlockSpec(memory_space=pltpu.SMEM),
                pl.BlockSpec((per, ROWS * members, BW), lambda a, c, j: (0, 0, 0)),
                pl.BlockSpec((1, 1, chunk, cells), lambda a, c, j: (a, c, j, 0)),
                pl.BlockSpec((1, 1, 1, chunk), lambda a, c, j: (a, c, 0, j)),
                pl.BlockSpec((1, 1, 1, chunk), lambda a, c, j: (a, c, 0, j)),
            ],
            out_specs=pl.BlockSpec((members, BW), lambda a, c, j: (0, 0)),
            out_shape=shape(members, BW),
            scratch_shapes=[
                pltpu.VMEM((2 * members, cells), jnp.bfloat16),
                pltpu.VMEM((members, chunk), F32),
            ],
            compiler_params=pltpu.CompilerParams(vmem_limit_bytes=VMEM_LIMIT),
            name="score",
        )(block_rows, surface, footprint, observed.reshape(obs), precision.reshape(obs))
        return lax.psum(out[:, 0], ("dom", "tile"))

    logs = [likelihood(surface)]

    work = (per + 1, (ROWS + 2 * STEPS) * row, BW)
    back, surface = call(
        functools.partial(advance_columns, members=members, per=per),
        [shape(members, per * 8, SUB, BW), shape(per, ROWS * members, BW)],
        [pltpu.VMEM(work, F32), pltpu.VMEM(work, F32)],
        scalars=2,
        name="advance_columns",
    )(edge, parent[1], main, sides, from_below, from_above)
    back = back.reshape(groups, MEM, per * 64, BW)
    mine = lax.all_to_all(back, "dom", split_axis=0, concat_axis=0, tiled=True)
    logs.append(likelihood(surface))

    q_out, psi_out = pl.pallas_call(
        functools.partial(unpack_state, per=per),
        grid=(groups,),
        in_specs=[pl.BlockSpec((1, MEM, per * 64, BW), lambda i: (i, 0, 0, 0))],
        out_specs=[pl.BlockSpec(fields + (per * BW,), lambda i: (0, 0, 0, i))] * 2,
        out_shape=[shape(*fields, width)] * 2,
        name="unpack_state",
    )(mine)

    loglik = jnp.stack(logs)
    total_obs = observed.size * groups * tiles
    mean_loglik = loglik / total_obs
    highest = jnp.max(loglik, axis=1, keepdims=True)
    scaled = jnp.exp(loglik - highest)
    weights = scaled / jnp.sum(scaled, axis=1, keepdims=True)
    return (q_out, psi_out, mean_loglik, weights)


def solution(mesh):
    return jax.shard_map(
        shards,
        mesh=mesh,
        in_specs=(
            P("dom", None, "tile", None),
            P("dom", None, "tile", None),
            P(None, "dom", None, "tile", None),
            P(),
            P("tile", "dom", None, None),
            P("tile", "dom", None),
            P("tile", "dom", None),
            P("tile", "dom"),
        ),
        out_specs=(P("dom", None, "tile", None), P("dom", None, "tile", None), P(), P()),
        check_vma=False,
    )
```

profile of v0, /device:TPU:0, one launch (start us, length us, event | category | flops | bytes accessed | tf_op | source)
XLA Modules:
  0.0 238.3 jit_solution(1430594285644836792)
XLA Ops:
  0.6 2.6 %pack_noise.1 = f32[8,4,9,8,128]{4,3,2,1,0:T(8,128)} custom-call(f32[2,4,2,16,2048]{4,3,2,1,0:T(8,128)} %n_ref.3), custom_call_target="tpu_custom_call" | custom-call | tf_op jit(solution)/shard_map/pack_noise/pallas_call | solution.py:390
  3.3 5.2 %all-to-all-start.1 = ((f32[8,4,9,8,128]{4,3,2,1,0:T(8,128)}), f32[8,4,9,8,128]{4,3,2,1,0:T(8,128)S(1)}, u32[]{:S(2)}, u32[]{:S(2)}) async-start(f32[8,4,9,8,128]{4,3,2,1,0:T(8,128)} %pack_noise.1), calls=%async_computation.1 | async-start | bytes 2359296 | tf_op jit(solution)/shard_map/all_to_all | solution.py:399
  8.4 4.4 %pack_state.1 = (f32[16,256,128]{2,1,0:T(8,128)}, f32[16,96,128]{2,1,0:T(8,128)}, f32[16,96,128]{2,1,0:T(8,128)}) custom-call(f32[4,2,16,2048]{3,2,1,0:T(8,128)} %q_ref.1, f32[4,2,16,2048]{3,2,1,0:T(8,128)} %p_ref.1, f32[2,4,2,16,2048]{4,3,2,1,0:T(8,128)} %n_ref.3), custom_call_target="tpu_custom_call" | custom-call | tf_op jit(solution)/shard_map/pack_state/pallas_call | solution.py:367
  12.8 3.5 %collective-permute-start = (f32[16,96,128]{2,1,0:T(8,128)}, f32[16,96,128]{2,1,0:T(8,128)S(1)}, u32[]{:S(2)}, u32[]{:S(2)}) collective-permute-start(f32[16,96,128]{2,1,0:T(8,128)} %get-tuple-element.17), channel_id=1, source_target_pairs={{0,1},{1,2},{2,3},{4,5},{5,6},{6,7},{8,9},{9,10},{10,11},{12,13},{... | collective-permute-start | bytes 2359304 | tf_op jit(solution)/shard_map/ppermute | solution.py:387
  16.3 1.3 collective-permute-start.1
  18.2 15.8 %collective-permute-done.up_ref = f32[16,96,128]{2,1,0:T(8,128)S(1)} collective-permute-done((f32[16,96,128]{2,1,0:T(8,128)}, f32[16,96,128]{2,1,0:T(8,128)S(1)}, u32[]{:S(2)}, u32[]{:S(2)}) %collective-permute-start) | collective-permute-done | bytes 786464 | tf_op jit(solution)/shard_map/ppermute | solution.py:387
  34.0 4.1 %collective-permute-done.1.down_ref = f32[16,96,128]{2,1,0:T(8,128)S(1)} collective-permute-done((f32[16,96,128]{2,1,0:T(8,128)}, f32[16,96,128]{2,1,0:T(8,128)S(1)}, u32[]{:S(2)}, u32[]{:S(2)}) %collective-permute-start.1) | collective-permute-done | bytes 786464 | tf_op jit(solution)/shard_map/ppermute | solution.py:388
  39.0 20.0 %advance_members.1 = f32[8,4,17,8,128]{4,3,2,1,0:T(8,128)} custom-call(s32[2]{0:T(128)} %pad_add_fusion.edge, f32[16,256,128]{2,1,0:T(8,128)} %get-tuple-element.16.main_ref, f32[16,96,128]{2,1,0:T(8,128)} %copy-done.5, f32[16,96,128]{2,1,0:T(8,128)} %copy-done.6), custom_call_target="tpu_custom_call" | custom-call | tf_op jit(solution)/shard_map/advance_members/pallas_call | solution.py:333
  59.0 1.0 copy-done.2
  60.0 3.8 %all-to-all-start = ((f32[8,4,17,8,128]{4,3,2,1,0:T(8,128)}), f32[8,4,17,8,128]{4,3,2,1,0:T(8,128)S(1)}, u32[]{:S(2)}, u32[]{:S(2)}) async-start(f32[8,4,17,8,128]{4,3,2,1,0:T(8,128)} %advance_members.1), calls=%async_computation | async-start | bytes 4456448 | tf_op jit(solution)/shard_map/all_to_all | solution.py:410
  64.7 27.1 %all-to-all-done = f32[8,4,17,8,128]{4,3,2,1,0:T(8,128)S(1)} async-done(((f32[8,4,17,8,128]{4,3,2,1,0:T(8,128)}), f32[8,4,17,8,128]{4,3,2,1,0:T(8,128)S(1)}, u32[]{:S(2)}, u32[]{:S(2)}) %all-to-all-start) | async-done | bytes 2228256 | tf_op jit(solution)/shard_map/all_to_all | solution.py:410
  91.9 1.4 copy-done
  93.3 8.1 %resample.1 = (f32[2,2048,128]{2,1,0:T(8,128)}, f32[256,128]{1,0:T(8,128)}, f32[13,128,128]{2,1,0:T(8,128)}, f32[13,128,128]{2,1,0:T(8,128)}, f32[2,512,128]{2,1,0:T(8,128)}) custom-call(s32[32]{0:T(128)} %get-tuple-element.32.parent, f32[32,17,8,128]{3,2,1,0:T(8,128)} %bitcast.10, f32[32,9,8,128]{3,2,1,0:T(8,128)} %bitcast.11), custom_call_target="tpu_custom_call" | custom-call | tf_op jit(solution)/shard_map/resample/pallas_call | solution.py:333
  101.4 5.6 %collective-permute-start.2 = (f32[13,128,128]{2,1,0:T(8,128)}, f32[13,128,128]{2,1,0:T(8,128)S(1)}, u32[]{:S(2)}, u32[]{:S(2)}) collective-permute-start(f32[13,128,128]{2,1,0:T(8,128)} %get-tuple-element.21), channel_id=1, source_target_pairs={{0,1},{1,2},{2,3},{4,5},{5,6},{6,7},{8,9},{9,10},{10,11},{12,13},{... | collective-permute-start | bytes 2555912 | tf_op jit(solution)/shard_map/ppermute | solution.py:427
  107.0 1.3 collective-permute-start.3
  108.3 14.4 %collective-permute-done.2.up_ref = f32[13,128,128]{2,1,0:T(8,128)S(1)} collective-permute-done((f32[13,128,128]{2,1,0:T(8,128)}, f32[13,128,128]{2,1,0:T(8,128)S(1)}, u32[]{:S(2)}, u32[]{:S(2)}) %collective-permute-start.2) | collective-permute-done | bytes 852000 | tf_op jit(solution)/shard_map/ppermute | solution.py:427
  122.6 4.1 %collective-permute-done.3.down_ref = f32[13,128,128]{2,1,0:T(8,128)S(1)} collective-permute-done((f32[13,128,128]{2,1,0:T(8,128)}, f32[13,128,128]{2,1,0:T(8,128)S(1)}, u32[]{:S(2)}, u32[]{:S(2)}) %collective-permute-start.3) | collective-permute-done | bytes 852000 | tf_op jit(solution)/shard_map/ppermute | solution.py:428
  127.6 27.9 %advance_columns.1 = (f32[32,16,8,128]{3,2,1,0:T(8,128)}, f32[2,512,128]{2,1,0:T(8,128)}) custom-call(s32[2]{0:T(128)} %pad_add_fusion.edge, s32[32]{0:T(128)} %get-tuple-element.33.parent, f32[2,2048,128]{2,1,0:T(8,128)} %get-tuple-element.19.main_ref, f32[256,128]{1,0:T(8,128)} %get-tuple-element.20.edge_ref, f32[13,128,128]{2,1,0:T(8,128)} %copy-done.3, ...), custom_call_target="tpu_custom_call" | custom-call | tf_op jit(solution)/shard_map/advance_columns/pallas_call | solution.py:333
  155.5 4.9 %all-to-all-start.2 = ((f32[8,4,128,128]{3,2,1,0:T(8,128)}), f32[8,4,128,128]{3,2,1,0:T(8,128)S(1)}, u32[]{:S(2)}, u32[]{:S(2)}) async-start(f32[8,4,128,128]{3,2,1,0:T(8,128)} %bitcast.12), calls=%async_computation.2 | async-start | bytes 4194304 | tf_op jit(solution)/shard_map/all_to_all | solution.py:465
  161.7 11.8 %score.2 = f32[32,128]{1,0:T(8,128)} custom-call(s32[2,2]{1,0:T(2,128)} %rows_ref.3, f32[2,512,128]{2,1,0:T(8,128)} %get-tuple-element.26.z_ref, f32[2,2,1024,1024]{3,2,1,0:T(8,128)} %f_ref.3, f32[2,2,1,1024]{3,2,1,0:T(1,128)} %reshape.33.o_ref, f32[2,2,1,1024]{3,2,1,0:T(1,128)} %reshape.34.w_ref), custom_call_target="tpu_custom_call" | custom-call | tf_op jit(solution)/shard_map/score/pallas_call | solution.py:433
  174.3 11.8 %score.3 = f32[32,128]{1,0:T(8,128)} custom-call(s32[2,2]{1,0:T(2,128)} %rows_ref.3, f32[2,512,128]{2,1,0:T(8,128)} %get-tuple-element.27.z_ref, f32[2,2,1024,1024]{3,2,1,0:T(8,128)} %f_ref.3, f32[2,2,1,1024]{3,2,1,0:T(1,128)} %reshape.33.o_ref, f32[2,2,1,1024]{3,2,1,0:T(1,128)} %reshape.34.w_ref), custom_call_target="tpu_custom_call" | custom-call | tf_op jit(solution)/shard_map/score/pallas_call | solution.py:433
  186.9 43.5 %all-reduce = (f32[1,32]{1,0:T(1,128)S(1)}, f32[1,32]{1,0:T(1,128)S(1)}) all-reduce(f32[1,32]{1,0:T(1,128)S(1)} %bitcast.14, f32[1,32]{1,0:T(1,128)S(1)} %bitcast.13), channel_id=1, replica_groups=mesh['dom'=8,'tile'=4] {'dom','tile'}, use_global_device_ids=true, to_apply=%region_3.4 | all-reduce | flops 64 | bytes 512 | tf_op jit(solution)/shard_map/psum | solution.py:452
  231.3 1.4 copy-done.1
  232.7 5.6 %unpack_state.1 = (f32[4,2,16,2048]{3,2,1,0:T(8,128)}, f32[4,2,16,2048]{3,2,1,0:T(8,128)}) custom-call(f32[8,4,128,128]{3,2,1,0:T(8,128)} %copy-done.1), custom_call_target="tpu_custom_call" | custom-call | tf_op jit(solution)/shard_map/unpack_state/pallas_call | solution.py:468
  (31 shorter events, 7.2 us)
Async XLA Ops:
  3.3 55.7 %all-to-all-start.1 = ((f32[8,4,9,8,128]{4,3,2,1,0:T(8,128)}), f32[8,4,9,8,128]{4,3,2,1,0:T(8,128)S(1)}, u32[]{:S(2)}, u32[]{:S(2)}) async-start(f32[8,4,9,8,128]{4,3,2,1,0:T(8,128)} %pack_noise.1), calls=%async_computation.1 | async-start | bytes 2359296 | tf_op jit(solution)/shard_map/all_to_all | solution.py:399
  12.8 21.2 %collective-permute-start = (f32[16,96,128]{2,1,0:T(8,128)}, f32[16,96,128]{2,1,0:T(8,128)S(1)}, u32[]{:S(2)}, u32[]{:S(2)}) collective-permute-start(f32[16,96,128]{2,1,0:T(8,128)} %get-tuple-element.17), channel_id=1, source_target_pairs={{0,1},{1,2},{2,3},{4,5},{5,6},{6,7},{8,9},{9,10},{10,11},{12,13},{... | collective-permute-start | bytes 2359304 | tf_op jit(solution)/shard_map/ppermute | solution.py:387
  16.3 21.8 %collective-permute-start.1 = (f32[16,96,128]{2,1,0:T(8,128)}, f32[16,96,128]{2,1,0:T(8,128)S(1)}, u32[]{:S(2)}, u32[]{:S(2)}) collective-permute-start(f32[16,96,128]{2,1,0:T(8,128)} %get-tuple-element.18), channel_id=1, source_target_pairs={{1,0},{2,1},{3,2},{5,4},{6,5},{7,6},{9,8},{10,9},{11,10},{13,12},{... | collective-permute-start | bytes 2359304 | tf_op jit(solution)/shard_map/ppermute | solution.py:388
  34.0 4.1 %copy-start.5 = (f32[16,96,128]{2,1,0:T(8,128)}, f32[16,96,128]{2,1,0:T(8,128)S(1)}, u32[]{:S(2)}) copy-start(f32[16,96,128]{2,1,0:T(8,128)S(1)} %collective-permute-done.up_ref) | copy-start | bytes 2359300
  38.1 0.9 copy-start.6
  58.9 4.9 %copy-start.9 = (s32[2,32]{1,0:T(2,128)S(1)}, s32[2,32]{1,0:T(2,128)}, u32[]{:S(2)}) copy-start(s32[2,32]{1,0:T(2,128)} %param.11) | copy-start | bytes 772
  59.0 1.0 copy-start.2
  60.0 31.9 %all-to-all-start = ((f32[8,4,17,8,128]{4,3,2,1,0:T(8,128)}), f32[8,4,17,8,128]{4,3,2,1,0:T(8,128)S(1)}, u32[]{:S(2)}, u32[]{:S(2)}) async-start(f32[8,4,17,8,128]{4,3,2,1,0:T(8,128)} %advance_members.1), calls=%async_computation | async-start | bytes 4456448 | tf_op jit(solution)/shard_map/all_to_all | solution.py:410
  91.9 1.4 copy-start
  101.4 21.3 %collective-permute-start.2 = (f32[13,128,128]{2,1,0:T(8,128)}, f32[13,128,128]{2,1,0:T(8,128)S(1)}, u32[]{:S(2)}, u32[]{:S(2)}) collective-permute-start(f32[13,128,128]{2,1,0:T(8,128)} %get-tuple-element.21), channel_id=1, source_target_pairs={{0,1},{1,2},{2,3},{4,5},{5,6},{6,7},{8,9},{9,10},{10,11},{12,13},{... | collective-permute-start | bytes 2555912 | tf_op jit(solution)/shard_map/ppermute | solution.py:427
  107.0 19.7 %collective-permute-start.3 = (f32[13,128,128]{2,1,0:T(8,128)}, f32[13,128,128]{2,1,0:T(8,128)S(1)}, u32[]{:S(2)}, u32[]{:S(2)}) collective-permute-start(f32[13,128,128]{2,1,0:T(8,128)} %get-tuple-element.22), channel_id=1, source_target_pairs={{1,0},{2,1},{3,2},{5,4},{6,5},{7,6},{9,8},{10,9},{11,10},{13,12},{... | collective-permute-start | bytes 2555912 | tf_op jit(solution)/shard_map/ppermute | solution.py:428
  122.6 4.1 %copy-start.3 = (f32[13,128,128]{2,1,0:T(8,128)}, f32[13,128,128]{2,1,0:T(8,128)S(1)}, u32[]{:S(2)}) copy-start(f32[13,128,128]{2,1,0:T(8,128)S(1)} %collective-permute-done.2.up_ref) | copy-start | bytes 2555908
  126.7 0.9 copy-start.4
  155.5 4.9 %copy-start.7 = (f32[2,2,1024]{2,1,0:T(2,128)S(1)}, f32[2,2,1024]{2,1,0:T(2,128)}, u32[]{:S(2)}) copy-start(f32[2,2,1024]{2,1,0:T(2,128)} %param.13) | copy-start | bytes 49156
  155.5 5.6 %copy-start.8 = (f32[2,2,1024]{2,1,0:T(2,128)S(1)}, f32[2,2,1024]{2,1,0:T(2,128)}, u32[]{:S(2)}) copy-start(f32[2,2,1024]{2,1,0:T(2,128)} %param.14) | copy-start | bytes 49156
  155.5 75.8 %all-to-all-start.2 = ((f32[8,4,128,128]{3,2,1,0:T(8,128)}), f32[8,4,128,128]{3,2,1,0:T(8,128)S(1)}, u32[]{:S(2)}, u32[]{:S(2)}) async-start(f32[8,4,128,128]{3,2,1,0:T(8,128)} %bitcast.12), calls=%async_computation.2 | async-start | bytes 4194304 | tf_op jit(solution)/shard_map/all_to_all | solution.py:465
  231.3 1.4 copy-start.1
where the time goes:
time: 239 us; the launch traced here: 238 us
  Pallas kernels  92.1 us (39%)
  waiting for transfers between devices  65.4 us (27%)
  blocking collectives  43.5 us (18%)
  starting transfers between devices  25.6 us (11%)
  local copies, waits for them, and re-layouts  9.02 us (4%)
    pallas_call x3, Pallas kernels, run(): pl.pallas_call(kernel, out_shape=outs, in_specs=specs, out_specs=[pl.Bloc...  56 us
    psum x1, blocking collectives, likelihood(): return lax.psum(out[:, 0], ('dom', 'tile'))  43.5 us
    ppermute x2, waiting for transfers between devices, shards(): from_below = lax.ppermute(to_up, 'tile', up)  30.2 us
    all_to_all x1, waiting for transfers between devices, shards(): owned = lax.all_to_all(sent, 'dom', split_axis=0, concat_axis=0, tiled=True)  27.1 us
    pallas_call x2, Pallas kernels, likelihood(): pl.pallas_call(functools.partial(score, members=members, per=per, chunk=c...  23.5 us
    ppermute x2, starting transfers between devices, shards(): from_below = lax.ppermute(to_up, 'tile', up)  9.1 us
    ppermute x2, waiting for transfers between devices, shards(): from_above = lax.ppermute(to_down, 'tile', down)  8.11 us
    pallas_call x1, Pallas kernels, shards(): pl.pallas_call(functools.partial(unpack_state, per=per), grid=(groups,),...  5.62 us
  transfers between devices with their start and end apart: 7, of which 5 were waited for; matrix products, arithmetic and copies ran while one was open for 2% of the time, Pallas kernels for 20%

commit v1 on v0

--- a/solution.py
+++ b/solution.py
@@ -192,16 +192,19 @@
         p = parent[k]
         for c in range(per):
             for v in range(8):
-                main_ref[c, pl.ds(v * 8 * members + k, SUB, stride=members), :] = x_ref[p, c * 8 + v]
+                main_ref[c, pl.ds(v * 8 * members + k, SUB, stride=members), :] = x_ref[
+                    p, (c * 8 + v) * SUB : (c * 8 + v + 1) * SUB, :
+                ]
             for v in range(4):
                 noise[c, pl.ds(v * 8 * members + k, SUB, stride=members), :] = n_ref[k, c * 4 + v]
             for g in range(2):
-                for r in range(SUB):
-                    j = g * SUB + r
-                    z_ref[c, pl.ds(j * members + k, 1), :] = x_ref[
-                        k, c * 8 + j // 2, (j % 2) * 4 + 2 : (j % 2) * 4 + 3, :
-                    ]
-        edge_ref[pl.ds(k, SUB, stride=members), :] = x_ref[p, size - 1] + n_ref[k, per * 4]
+                s = c * 64 + g * 32 + 2
+                z_ref[c, pl.ds(g * SUB * members + k, SUB, stride=members), :] = x_ref[
+                    k, pl.ds(s, SUB, stride=4), :
+                ]
+        edge_ref[pl.ds(k, SUB, stride=members), :] = (
+            x_ref[p, size * SUB - SUB :, :] + n_ref[k, per * 4]
+        )
         return 0
 
     lax.fori_loop(0, members, one, 0)
@@ -319,7 +322,10 @@
 
     @pl.when((a == pl.num_programs(0) - 1) & (c == pl.num_programs(1) - 1) & (j == pl.num_programs(2) - 1))
     def _():
-        out_ref[...] = jnp.broadcast_to(jnp.sum(total[...], axis=1, keepdims=True) * -0.5, (members, BW))
+        ones = jnp.full((SUB, total.shape[1]), -0.5, F32)
+        out_ref[...] = lax.dot_general(
+            ones, total[...], dims, precision=lax.Precision.HIGHEST, preferred_element_type=F32
+        )
 
 
 def shape(*dims):
@@ -384,6 +390,8 @@
         ],
         name="pack_state",
     )(vorticity, streamfunction, model_noise)
+
+    later_noise, to_up, to_down = lax.optimization_barrier((model_noise, to_up, to_down))
     from_below = lax.ppermute(to_up, "tile", up)
     from_above = lax.ppermute(to_down, "tile", down)
 
@@ -395,7 +403,8 @@
         out_shape=shape(groups, MEM, per * 4 + 1, SUB, BW),
         scratch_shapes=[pltpu.VMEM((blocks, ROWS * SUB, BW), F32), pltpu.VMEM((groups, 32, BW), F32)],
         name="pack_noise",
-    )(model_noise)
+    )(later_noise)
+    noise, main = lax.optimization_barrier((noise, main))
     noise = lax.all_to_all(noise, "dom", split_axis=0, concat_axis=0, tiled=True)
     noise = noise.reshape(members, per * 4 + 1, SUB, BW)
 
@@ -408,7 +417,7 @@
         name="advance_members",
     )(edge, main, from_below, from_above)
     owned = lax.all_to_all(sent, "dom", split_axis=0, concat_axis=0, tiled=True)
-    owned = owned.reshape(members, per * 8 + 1, SUB, BW)
+    owned = owned.reshape(members, (per * 8 + 1) * SUB, BW)
 
     row = 4 * members
     main, sides, to_up, to_down, surface = call(
@@ -440,8 +449,8 @@
                 pl.BlockSpec((1, 1, 1, chunk), lambda a, c, j: (a, c, 0, j)),
                 pl.BlockSpec((1, 1, 1, chunk), lambda a, c, j: (a, c, 0, j)),
             ],
-            out_specs=pl.BlockSpec((members, BW), lambda a, c, j: (0, 0)),
-            out_shape=shape(members, BW),
+            out_specs=pl.BlockSpec((SUB, members), lambda a, c, j: (0, 0)),
+            out_shape=shape(SUB, members),
             scratch_shapes=[
                 pltpu.VMEM((2 * members, cells), jnp.bfloat16),
                 pltpu.VMEM((members, chunk), F32),
@@ -449,9 +458,10 @@
             compiler_params=pltpu.CompilerParams(vmem_limit_bytes=VMEM_LIMIT),
             name="score",
         )(block_rows, surface, footprint, observed.reshape(obs), precision.reshape(obs))
-        return lax.psum(out[:, 0], ("dom", "tile"))
+        return out[:1]
 
     logs = [likelihood(surface)]
+    main, logs[0] = lax.optimization_barrier((main, logs[0]))
 
     work = (per + 1, (ROWS + 2 * STEPS) * row, BW)
     back, surface = call(
@@ -474,7 +484,13 @@
         name="unpack_state",
     )(mine)
 
-    loglik = jnp.stack(logs)
+    loglik = jnp.concatenate(logs, axis=0)
+    for axis, size in (("dom", groups), ("tile", tiles)):
+        hop = 1
+        while hop < size:
+            pairs = [(i, i ^ hop) for i in range(size)]
+            loglik = loglik + lax.ppermute(loglik, axis, pairs)
+            hop *= 2
     total_obs = observed.size * groups * tiles
     mean_loglik = loglik / total_obs
     highest = jnp.max(loglik, axis=1, keepdims=True)

time: 239 us -> 209 us (0.87)
  blocking collectives: 43.5 us -> 0 us
  starting transfers between devices: 25.6 us -> 35.8 us
  waiting for transfers between devices: 65.4 us -> 68.5 us
    psum x1 -> x0, blocking collectives: 43.5 us -> none  [likelihood(): return lax.psum(out[:, 0], ('dom', 'tile'))]
    ppermute x0 -> x5, waiting for transfers between devices: none -> 16.9 us  [shards(): loglik = loglik + lax.ppermute(loglik, axis, pairs)]
    ppermute x2, waiting for transfers between devices: 30.2 us -> 16.5 us  [shards(): from_below = lax.ppermute(to_up, 'tile', up)]
    ppermute x0 -> x5, starting transfers between devices: none -> 10.3 us  [shards(): loglik = loglik + lax.ppermute(loglik, axis, pairs)]
    unnamed x20 -> x22, local copies, waits for them, and re-layouts: 5.55 us -> 5.58 us
  transfers between devices with their start and end apart: 7 -> 12, of which waited for: 5 -> 10; matrix products, arithmetic and copies ran while one was open for 2% -> 2% of each run, Pallas kernels for 20% -> 21%
where the time goes in v1:
time: 209 us; the launch traced here: 208 us
  Pallas kernels  92.1 us (44%)
  waiting for transfers between devices  68.5 us (33%)
  starting transfers between devices  35.8 us (17%)
  local copies, waits for them, and re-layouts  8.77 us (4%)
    pallas_call x3, Pallas kernels, run(): pl.pallas_call(kernel, out_shape=outs, in_specs=specs, out_specs=[pl.Bloc...  55.9 us
    all_to_all x1, waiting for transfers between devices, shards(): owned = lax.all_to_all(sent, 'dom', split_axis=0, concat_axis=0, tiled=True)  27.1 us
    pallas_call x2, Pallas kernels, likelihood(): pl.pallas_call(functools.partial(score, members=members, per=per, chunk=c...  23.5 us
    ppermute x5, waiting for transfers between devices, shards(): loglik = loglik + lax.ppermute(loglik, axis, pairs)  16.9 us
    ppermute x2, waiting for transfers between devices, shards(): from_below = lax.ppermute(to_up, 'tile', up)  16.5 us
    ppermute x5, starting transfers between devices, shards(): loglik = loglik + lax.ppermute(loglik, axis, pairs)  10.3 us
    ppermute x2, starting transfers between devices, shards(): from_below = lax.ppermute(to_up, 'tile', up)  9.1 us
    ppermute x2, waiting for transfers between devices, shards(): from_above = lax.ppermute(to_down, 'tile', down)  7.91 us
  transfers between devices with their start and end apart: 12, of which 10 were waited for; matrix products, arithmetic and copies ran while one was open for 2% of the time, Pallas kernels for 21%

profile of v1, /device:TPU:0, one launch (start us, length us, event | category | flops | bytes accessed | tf_op | source)
XLA Modules:
  0.0 207.8 jit_solution(11282413638784977217)
XLA Ops:
  0.6 4.4 %pack_state.1 = (f32[16,256,128]{2,1,0:T(8,128)}, f32[16,96,128]{2,1,0:T(8,128)}, f32[16,96,128]{2,1,0:T(8,128)}) custom-call(f32[4,2,16,2048]{3,2,1,0:T(8,128)} %q_ref.1, f32[4,2,16,2048]{3,2,1,0:T(8,128)} %p_ref.1, f32[2,4,2,16,2048]{4,3,2,1,0:T(8,128)} %n_ref.2), custom_call_target="tpu_custom_call" | custom-call | tf_op jit(solution)/shard_map/pack_state/pallas_call | solution.py:373
  5.0 2.7 %pack_noise.1 = f32[8,4,9,8,128]{4,3,2,1,0:T(8,128)} custom-call(f32[2,4,2,16,2048]{4,3,2,1,0:T(8,128)} %n_ref.2), custom_call_target="tpu_custom_call" | custom-call | tf_op jit(solution)/shard_map/pack_noise/pallas_call | solution.py:398
  7.7 5.2 %all-to-all-start.1 = ((f32[8,4,9,8,128]{4,3,2,1,0:T(8,128)}), f32[8,4,9,8,128]{4,3,2,1,0:T(8,128)S(1)}, u32[]{:S(2)}, u32[]{:S(2)}) async-start(f32[8,4,9,8,128]{4,3,2,1,0:T(8,128)} %pack_noise.1), calls=%async_computation.1 | async-start | bytes 2359296 | tf_op jit(solution)/shard_map/all_to_all | solution.py:408
  12.9 3.5 %collective-permute-start = (f32[16,96,128]{2,1,0:T(8,128)}, f32[16,96,128]{2,1,0:T(8,128)S(1)}, u32[]{:S(2)}, u32[]{:S(2)}) collective-permute-start(f32[16,96,128]{2,1,0:T(8,128)} %get-tuple-element.28), channel_id=1, source_target_pairs={{0,1},{1,2},{2,3},{4,5},{5,6},{6,7},{8,9},{9,10},{10,11},{12,13},{... | collective-permute-start | bytes 2359304 | tf_op jit(solution)/shard_map/ppermute | solution.py:395
  18.3 15.8 %collective-permute-done.up_ref = f32[16,96,128]{2,1,0:T(8,128)S(1)} collective-permute-done((f32[16,96,128]{2,1,0:T(8,128)}, f32[16,96,128]{2,1,0:T(8,128)S(1)}, u32[]{:S(2)}, u32[]{:S(2)}) %collective-permute-start) | collective-permute-done | bytes 786464 | tf_op jit(solution)/shard_map/ppermute | solution.py:395
  34.2 3.9 %collective-permute-done.1.down_ref = f32[16,96,128]{2,1,0:T(8,128)S(1)} collective-permute-done((f32[16,96,128]{2,1,0:T(8,128)S(1)}, f32[16,96,128]{2,1,0:T(8,128)S(1)}, u32[]{:S(2)}, u32[]{:S(2)}) %collective-permute-start.1) | collective-permute-done | bytes 786464 | tf_op jit(solution)/shard_map/ppermute | solution.py:396
  38.9 20.0 %advance_members.1 = f32[8,4,17,8,128]{4,3,2,1,0:T(8,128)} custom-call(s32[2]{0:T(128)} %pad_add_fusion.edge, f32[16,256,128]{2,1,0:T(8,128)} %get-tuple-element.27.main_ref, f32[16,96,128]{2,1,0:T(8,128)} %copy-done.5, f32[16,96,128]{2,1,0:T(8,128)} %copy-done.6), custom_call_target="tpu_custom_call" | custom-call | tf_op jit(solution)/shard_map/advance_members/pallas_call | solution.py:339
  59.9 3.8 %all-to-all-start = ((f32[8,4,17,8,128]{4,3,2,1,0:T(8,128)}), f32[8,4,17,8,128]{4,3,2,1,0:T(8,128)S(1)}, u32[]{:S(2)}, u32[]{:S(2)}) async-start(f32[8,4,17,8,128]{4,3,2,1,0:T(8,128)} %advance_members.1), calls=%async_computation | async-start | bytes 4456448 | tf_op jit(solution)/shard_map/all_to_all | solution.py:419
  64.7 27.1 %all-to-all-done = f32[8,4,17,8,128]{4,3,2,1,0:T(8,128)S(1)} async-done(((f32[8,4,17,8,128]{4,3,2,1,0:T(8,128)}), f32[8,4,17,8,128]{4,3,2,1,0:T(8,128)S(1)}, u32[]{:S(2)}, u32[]{:S(2)}) %all-to-all-start) | async-done | bytes 2228256 | tf_op jit(solution)/shard_map/all_to_all | solution.py:419
  93.2 8.0 %resample.1 = (f32[2,2048,128]{2,1,0:T(8,128)}, f32[256,128]{1,0:T(8,128)}, f32[13,128,128]{2,1,0:T(8,128)}, f32[13,128,128]{2,1,0:T(8,128)}, f32[2,512,128]{2,1,0:T(8,128)}) custom-call(s32[32]{0:T(128)} %get-tuple-element.46.parent, f32[32,136,128]{2,1,0:T(8,128)} %bitcast.8, f32[32,9,8,128]{3,2,1,0:T(8,128)} %bitcast.9), custom_call_target="tpu_custom_call" | custom-call | tf_op jit(solution)/shard_map/resample/pallas_call | solution.py:339
  101.2 5.6 %collective-permute-start.2 = (f32[13,128,128]{2,1,0:T(8,128)}, f32[13,128,128]{2,1,0:T(8,128)S(1)}, u32[]{:S(2)}, u32[]{:S(2)}) collective-permute-start(f32[13,128,128]{2,1,0:T(8,128)} %get-tuple-element.35), channel_id=1, source_target_pairs={{0,1},{1,2},{2,3},{4,5},{5,6},{6,7},{8,9},{9,10},{10,11},{12,13},{... | collective-permute-start | bytes 2555912 | tf_op jit(solution)/shard_map/ppermute | solution.py:436
  109.4 11.7 %score.2 = f32[8,32]{1,0:T(8,128)} custom-call(s32[2,2]{1,0:T(2,128)} %rows_ref.3, f32[2,512,128]{2,1,0:T(8,128)} %get-tuple-element.32.z_ref, f32[2,2,1024,1024]{3,2,1,0:T(8,128)} %f_ref.3, f32[2,2,1,1024]{3,2,1,0:T(1,128)} %reshape.32.o_ref, f32[2,2,1,1024]{3,2,1,0:T(1,128)} %reshape.33.w_ref), custom_call_target="tpu_custom_call" | custom-call | tf_op jit(solution)/shard_map/score/pallas_call | solution.py:442
  122.5 4.1 %collective-permute-done.3.down_ref = f32[13,128,128]{2,1,0:T(8,128)S(1)} collective-permute-done((f32[13,128,128]{2,1,0:T(8,128)}, f32[13,128,128]{2,1,0:T(8,128)S(1)}, u32[]{:S(2)}, u32[]{:S(2)}) %collective-permute-start.3) | collective-permute-done | bytes 852000 | tf_op jit(solution)/shard_map/ppermute | solution.py:437
  127.5 27.9 %advance_columns.1 = (f32[32,16,8,128]{3,2,1,0:T(8,128)}, f32[2,512,128]{2,1,0:T(8,128)}) custom-call(s32[2]{0:T(128)} %pad_add_fusion.edge, s32[32]{0:T(128)} %get-tuple-element.47.parent, f32[2,2048,128]{2,1,0:T(8,128)} %get-tuple-element.33.main_ref, f32[256,128]{1,0:T(8,128)} %get-tuple-element.34.edge_ref, f32[13,128,128]{2,1,0:T(8,128)} %copy-done.3, ...), custom_call_target="tpu_custom_call" | custom-call | tf_op jit(solution)/shard_map/advance_columns/pallas_call | solution.py:339
  155.3 4.8 %all-to-all-start.2 = ((f32[8,4,128,128]{3,2,1,0:T(8,128)}), f32[8,4,128,128]{3,2,1,0:T(8,128)S(1)}, u32[]{:S(2)}, u32[]{:S(2)}) async-start(f32[8,4,128,128]{3,2,1,0:T(8,128)} %bitcast.10), calls=%async_computation.2 | async-start | bytes 4194304 | tf_op jit(solution)/shard_map/all_to_all | solution.py:475
  160.1 11.7 %score.3 = f32[8,32]{1,0:T(8,128)} custom-call(s32[2,2]{1,0:T(2,128)} %rows_ref.3, f32[2,512,128]{2,1,0:T(8,128)} %get-tuple-element.41.z_ref, f32[2,2,1024,1024]{3,2,1,0:T(8,128)} %f_ref.3, f32[2,2,1,1024]{3,2,1,0:T(1,128)} %reshape.32.o_ref, f32[2,2,1,1024]{3,2,1,0:T(1,128)} %reshape.33.w_ref), custom_call_target="tpu_custom_call" | custom-call | tf_op jit(solution)/shard_map/score/pallas_call | solution.py:442
  173.9 2.2 %collective-permute-start.5 = (f32[2,32]{1,0:T(2,128)S(1)}, f32[2,32]{1,0:T(2,128)S(1)}, u32[]{:S(2)}, u32[]{:S(2)}) collective-permute-start(f32[2,32]{1,0:T(2,128)S(1)} %fusion.2), channel_id=1, source_target_pairs={{0,8},{4,12},{8,0},{12,4},{16,24},{20,28},{24,16},{28,20},{1,9},{5... | collective-permute-start | bytes 776 | tf_op jit(solution)/shard_map/ppermute | solution.py:492
  176.1 9.7 %collective-permute-done.5 = f32[2,32]{1,0:T(2,128)S(1)} collective-permute-done((f32[2,32]{1,0:T(2,128)S(1)}, f32[2,32]{1,0:T(2,128)S(1)}, u32[]{:S(2)}, u32[]{:S(2)}) %collective-permute-start.5) | collective-permute-done | bytes 288 | tf_op jit(solution)/shard_map/ppermute | solution.py:492
  187.4 2.1 %collective-permute-done.6 = f32[2,32]{1,0:T(2,128)S(1)} collective-permute-done((f32[2,32]{1,0:T(2,128)S(1)}, f32[2,32]{1,0:T(2,128)S(1)}, u32[]{:S(2)}, u32[]{:S(2)}) %collective-permute-start.6) | collective-permute-done | bytes 288 | tf_op jit(solution)/shard_map/ppermute | solution.py:492
  189.5 4.3 %collective-permute-start.7 = (f32[2,32]{1,0:T(2,128)S(1)}, f32[2,32]{1,0:T(2,128)S(1)}, u32[]{:S(2)}, u32[]{:S(2)}) collective-permute-start(f32[2,32]{1,0:T(2,128)S(1)} %add.17), channel_id=1, source_target_pairs={{0,1},{1,0},{2,3},{3,2},{4,5},{5,4},{6,7},{7,6},{8,9},{9,8},{10,11... | collective-permute-start | bytes 776 | tf_op jit(solution)/shard_map/ppermute | solution.py:492
  193.8 1.5 collective-permute-done.7
  195.4 1.8 collective-permute-start.8
  197.2 2.7 %collective-permute-done.8 = f32[2,32]{1,0:T(2,128)S(1)} collective-permute-done((f32[2,32]{1,0:T(2,128)S(1)}, f32[2,32]{1,0:T(2,128)S(1)}, u32[]{:S(2)}, u32[]{:S(2)}) %collective-permute-start.8) | collective-permute-done | bytes 288 | tf_op jit(solution)/shard_map/ppermute | solution.py:492
  202.2 5.6 %unpack_state.1 = (f32[4,2,16,2048]{3,2,1,0:T(8,128)}, f32[4,2,16,2048]{3,2,1,0:T(8,128)}) custom-call(f32[8,4,128,128]{3,2,1,0:T(8,128)} %copy-done.1), custom_call_target="tpu_custom_call" | custom-call | tf_op jit(solution)/shard_map/unpack_state/pallas_call | solution.py:478
  (47 shorter events, 16.9 us)
Async XLA Ops:
  5.0 11.4 %copy-start.10 = (f32[16,96,128]{2,1,0:T(8,128)S(1)}, f32[16,96,128]{2,1,0:T(8,128)}, u32[]{:S(2)}) copy-start(f32[16,96,128]{2,1,0:T(8,128)} %get-tuple-element.29) | copy-start | bytes 2359300
  7.7 51.1 %all-to-all-start.1 = ((f32[8,4,9,8,128]{4,3,2,1,0:T(8,128)}), f32[8,4,9,8,128]{4,3,2,1,0:T(8,128)S(1)}, u32[]{:S(2)}, u32[]{:S(2)}) async-start(f32[8,4,9,8,128]{4,3,2,1,0:T(8,128)} %pack_noise.1), calls=%async_computation.1 | async-start | bytes 2359296 | tf_op jit(solution)/shard_map/all_to_all | solution.py:408
  12.9 21.2 %collective-permute-start = (f32[16,96,128]{2,1,0:T(8,128)}, f32[16,96,128]{2,1,0:T(8,128)S(1)}, u32[]{:S(2)}, u32[]{:S(2)}) collective-permute-start(f32[16,96,128]{2,1,0:T(8,128)} %get-tuple-element.28), channel_id=1, source_target_pairs={{0,1},{1,2},{2,3},{4,5},{5,6},{6,7},{8,9},{9,10},{10,11},{12,13},{... | collective-permute-start | bytes 2359304 | tf_op jit(solution)/shard_map/ppermute | solution.py:395
  16.4 21.6 %collective-permute-start.1 = (f32[16,96,128]{2,1,0:T(8,128)S(1)}, f32[16,96,128]{2,1,0:T(8,128)S(1)}, u32[]{:S(2)}, u32[]{:S(2)}) collective-permute-start(f32[16,96,128]{2,1,0:T(8,128)S(1)} %copy-done.10), channel_id=1, source_target_pairs={{1,0},{2,1},{3,2},{5,4},{6,5},{7,6},{9,8},{10,9},{11,10},{13,12},{... | collective-permute-start | bytes 2359304 | tf_op jit(solution)/shard_map/ppermute | solution.py:396
  34.2 3.9 %copy-start.5 = (f32[16,96,128]{2,1,0:T(8,128)}, f32[16,96,128]{2,1,0:T(8,128)S(1)}, u32[]{:S(2)}) copy-start(f32[16,96,128]{2,1,0:T(8,128)S(1)} %collective-permute-done.up_ref) | copy-start | bytes 2359300
  38.0 0.9 copy-start.6
  58.9 4.9 %copy-start.9 = (s32[2,32]{1,0:T(2,128)S(1)}, s32[2,32]{1,0:T(2,128)}, u32[]{:S(2)}) copy-start(s32[2,32]{1,0:T(2,128)} %param.11) | copy-start | bytes 772
  58.9 1.1 copy-start.2
  59.9 31.9 %all-to-all-start = ((f32[8,4,17,8,128]{4,3,2,1,0:T(8,128)}), f32[8,4,17,8,128]{4,3,2,1,0:T(8,128)S(1)}, u32[]{:S(2)}, u32[]{:S(2)}) async-start(f32[8,4,17,8,128]{4,3,2,1,0:T(8,128)} %advance_members.1), calls=%async_computation | async-start | bytes 4456448 | tf_op jit(solution)/shard_map/all_to_all | solution.py:419
  63.8 44.3 %copy-start.7 = (f32[2,2,1024]{2,1,0:T(2,128)S(1)}, f32[2,2,1024]{2,1,0:T(2,128)}, u32[]{:S(2)}) copy-start(f32[2,2,1024]{2,1,0:T(2,128)} %param.13) | copy-start | bytes 49156
  63.8 45.0 %copy-start.8 = (f32[2,2,1024]{2,1,0:T(2,128)S(1)}, f32[2,2,1024]{2,1,0:T(2,128)}, u32[]{:S(2)}) copy-start(f32[2,2,1024]{2,1,0:T(2,128)} %param.14) | copy-start | bytes 49156
  91.8 1.4 copy-start
  101.2 21.3 %collective-permute-start.2 = (f32[13,128,128]{2,1,0:T(8,128)}, f32[13,128,128]{2,1,0:T(8,128)S(1)}, u32[]{:S(2)}, u32[]{:S(2)}) collective-permute-start(f32[13,128,128]{2,1,0:T(8,128)} %get-tuple-element.35), channel_id=1, source_target_pairs={{0,1},{1,2},{2,3},{4,5},{5,6},{6,7},{8,9},{9,10},{10,11},{12,13},{... | collective-permute-start | bytes 2555912 | tf_op jit(solution)/shard_map/ppermute | solution.py:436
  106.8 19.7 %collective-permute-start.3 = (f32[13,128,128]{2,1,0:T(8,128)}, f32[13,128,128]{2,1,0:T(8,128)S(1)}, u32[]{:S(2)}, u32[]{:S(2)}) collective-permute-start(f32[13,128,128]{2,1,0:T(8,128)} %get-tuple-element.36), channel_id=1, source_target_pairs={{1,0},{2,1},{3,2},{5,4},{6,5},{7,6},{9,8},{10,9},{11,10},{13,12},{... | collective-permute-start | bytes 2555912 | tf_op jit(solution)/shard_map/ppermute | solution.py:437
  122.5 4.1 %copy-start.3 = (f32[13,128,128]{2,1,0:T(8,128)}, f32[13,128,128]{2,1,0:T(8,128)S(1)}, u32[]{:S(2)}) copy-start(f32[13,128,128]{2,1,0:T(8,128)S(1)} %collective-permute-done.2.up_ref) | copy-start | bytes 2555908
  126.6 0.9 copy-start.4
  155.3 45.5 %all-to-all-start.2 = ((f32[8,4,128,128]{3,2,1,0:T(8,128)}), f32[8,4,128,128]{3,2,1,0:T(8,128)S(1)}, u32[]{:S(2)}, u32[]{:S(2)}) async-start(f32[8,4,128,128]{3,2,1,0:T(8,128)} %bitcast.10), calls=%async_computation.2 | async-start | bytes 4194304 | tf_op jit(solution)/shard_map/all_to_all | solution.py:475
  172.6 1.4 collective-permute-start.4
  173.9 11.9 %collective-permute-start.5 = (f32[2,32]{1,0:T(2,128)S(1)}, f32[2,32]{1,0:T(2,128)S(1)}, u32[]{:S(2)}, u32[]{:S(2)}) collective-permute-start(f32[2,32]{1,0:T(2,128)S(1)} %fusion.2), channel_id=1, source_target_pairs={{0,8},{4,12},{8,0},{12,4},{16,24},{20,28},{24,16},{28,20},{1,9},{5... | collective-permute-start | bytes 776 | tf_op jit(solution)/shard_map/ppermute | solution.py:492
  185.9 3.6 %collective-permute-start.6 = (f32[2,32]{1,0:T(2,128)S(1)}, f32[2,32]{1,0:T(2,128)S(1)}, u32[]{:S(2)}, u32[]{:S(2)}) collective-permute-start(f32[2,32]{1,0:T(2,128)S(1)} %fusion.4), channel_id=1, source_target_pairs={{0,16},{4,20},{8,24},{12,28},{16,0},{20,4},{24,8},{28,12},{1,17},{... | collective-permute-start | bytes 776 | tf_op jit(solution)/shard_map/ppermute | solution.py:492
  189.5 5.9 %collective-permute-start.7 = (f32[2,32]{1,0:T(2,128)S(1)}, f32[2,32]{1,0:T(2,128)S(1)}, u32[]{:S(2)}, u32[]{:S(2)}) collective-permute-start(f32[2,32]{1,0:T(2,128)S(1)} %add.17), channel_id=1, source_target_pairs={{0,1},{1,0},{2,3},{3,2},{4,5},{5,4},{6,7},{7,6},{8,9},{9,8},{10,11... | collective-permute-start | bytes 776 | tf_op jit(solution)/shard_map/ppermute | solution.py:492
  195.4 4.5 %collective-permute-start.8 = (f32[2,32]{1,0:T(2,128)S(1)}, f32[2,32]{1,0:T(2,128)S(1)}, u32[]{:S(2)}, u32[]{:S(2)}) collective-permute-start(f32[2,32]{1,0:T(2,128)S(1)} %add.18), channel_id=1, source_target_pairs={{0,2},{1,3},{2,0},{3,1},{4,6},{5,7},{6,4},{7,5},{8,10},{9,11},{10,... | collective-permute-start | bytes 776 | tf_op jit(solution)/shard_map/ppermute | solution.py:492
  200.8 1.3 copy-start.1

commit v2 on v1

v2 whole, which is shorter than its diff:
```python
import functools

import jax
import jax.numpy as jnp
from jax import lax
from jax.experimental import pallas as pl
from jax.experimental.pallas import tpu as pltpu
from jax.sharding import PartitionSpec as P

STEPS = 6
CYCLES = 2
BW = 128
BR = 8
ROWS = 16
MEM = 4
LAYERS = 2
SUB = 8
SEG = 16
F32 = jnp.float32
VMEM_LIMIT = 56 * 1024 * 1024
DRAG_STEP = 0.1 * 0.2
HALF = 64
PARTS = 10
DEEP = ROWS + 2 * STEPS
FULL = 2 * HALF


def lanes():
    return lax.broadcasted_iota(jnp.int32, (SUB, BW), 1)


def lane_roll(x, shift):
    return pltpu.roll(x, shift % BW, axis=1)


def halo_pack(take):
    segment = ((lanes() + SEG // 2) // SEG) % SUB
    lower = lanes() < BW // 2
    packed = None
    for j in range(SUB):
        before, after = take(j)
        edge = lane_roll(jnp.where(lower, after, before), SEG * j)
        packed = edge if packed is None else jnp.where(segment == j, edge, packed)
    return packed


def wide_roll(x, shift):
    return pltpu.roll(x, shift % BW, axis=1)


def lower_half(rows):
    return lax.broadcasted_iota(jnp.int32, (rows, BW), 1) < HALF


def by_layer(turned):
    top, bottom = turned[:HALF], turned[HALF:]
    low = lower_half(HALF)
    return (
        jnp.where(low, top, wide_roll(bottom, HALF)),
        jnp.where(low, wide_roll(top, HALF), bottom),
    )


def to_layers(first, second):
    low = lower_half(HALF)
    top = jnp.where(low, first, wide_roll(second, HALF))
    bottom = jnp.where(low, wide_roll(first, HALF), second)
    return jnp.concatenate([top, bottom], axis=0)


def pack_field(*refs, blocks, noisy):
    x_ref, (main_ref, up_ref, down_ref, work) = refs[0], refs[-4:]
    g = pl.program_id(0)
    for b in range(blocks):
        cols = slice(b * BW, (b + 1) * BW)
        for m in range(MEM):
            for l in range(LAYERS):
                value = x_ref[m, l, :, cols]
                if noisy:
                    value = value + refs[1][0, m, l, :, cols]
                work[pl.ds(l * HALF + b * MEM + m, SUB, stride=FULL), :] = value
    for r in range(SUB):
        for l, part in enumerate(by_layer(work[r * FULL : (r + 1) * FULL, :].T)):
            main_ref[(r * 2 + l) * HALF : (r * 2 + l + 1) * HALF, :] = part

    @pl.when(g == 0)
    def _():
        down_ref[...] = main_ref[: STEPS * FULL, :]

    @pl.when(g == 1)
    def _():
        up_ref[...] = main_ref[(SUB - STEPS) * FULL :, :]


def pack_noise(n_ref, out_ref, work, wide, *, groups, per):
    blocks = groups * per
    for b in range(blocks):
        for m in range(MEM):
            for l in range(LAYERS):
                for g in range(ROWS // SUB):
                    value = n_ref[0, m, l, g * SUB : (g + 1) * SUB, b * BW : (b + 1) * BW]
                    s = l * HALF + b * MEM + m
                    work[pl.ds(g * SUB * FULL + s, SUB, stride=FULL), :] = value
                    wide[pl.ds(g * SUB * 2 * FULL + s, SUB, stride=2 * FULL), :] = value
    for r in range(ROWS):
        wide[(2 * r + 1) * FULL : (2 * r + 2) * FULL, :] = jnp.zeros((FULL, BW), F32)
    for d in range(groups):
        for m in range(MEM):
            def take(v):
                before = (d * per - 1) % blocks * MEM + m
                after = (d * per + per) % blocks * MEM + m
                return tuple(
                    wide[pl.ds(v * 4 * FULL + s, SUB, stride=HALF), :] for s in (before, after)
                )

            for c in range(per):
                for v in range(4):
                    s = v * 4 * FULL + (d * per + c) * MEM + m
                    out_ref[d, m, c * 4 + v] = work[pl.ds(s, SUB, stride=HALF), :]
            out_ref[d, m, per * 4] = halo_pack(take)


def place(natural, slot, dst, plane, body, left, right):
    natural[slot, :SUB, :] = left
    natural[slot, SUB : SUB + HALF, :] = body
    natural[slot, SUB + HALF :, :] = right
    for j in range(PARTS):
        dst[plane, j * SUB : (j + 1) * SUB, :] = natural[slot, pl.ds(j, SUB, stride=PARTS), :]


def margins(body, unit, left_end, right_end):
    lane = lanes()
    first, last = body[:SUB], body[HALF - SUB :]
    left = jnp.where(lane < HALF, wide_roll(last, HALF + unit), wide_roll(last, HALF))
    right = jnp.where(lane < HALF, wide_roll(first, HALF), wide_roll(first, HALF - unit))
    return jnp.where(lane < unit, left_end, left), jnp.where(lane >= BW - unit, right_end, right)


def run_steps(edge, first, second):
    zero = jnp.zeros((STEPS * 4, PARTS * SUB, BW), F32)

    @pl.when(edge[0] == 0)
    def _():
        second[: STEPS * 4] = zero

    @pl.when(edge[0] == edge[1] - 1)
    def _():
        second[(STEPS + ROWS) * 4 :] = zero

    src, dst = first, second
    for step in range(STEPS):
        low = jnp.where(edge[0] == 0, STEPS, step + 1)
        high = jnp.where(edge[0] == edge[1] - 1, STEPS + ROWS, DEEP - 1 - step)

        def body(i, _, src=src, dst=dst):
            for l in range(LAYERS):
                def load(f, j, di=0, layer=l):
                    return src[((i + di) * 2 + layer) * 2 + f, j * SUB : (j + 1) * SUB, :]

                west = tuple(pltpu.roll(load(f, PARTS - 1), 1, axis=0) for f in range(2))
                final = tuple(pltpu.roll(load(f, 0), SUB - 1, axis=0) for f in range(2))
                here = (load(0, 0), load(1, 0))
                for j in range(PARTS):
                    east = (load(0, j + 1), load(1, j + 1)) if j + 1 < PARTS else final
                    q, psi = here
                    psi_n, psi_s = load(1, j, 1), load(1, j, -1)
                    around = (psi_n + psi_s) + (east[1] + west[1])
                    along = east[1] - west[1]
                    psi_new = (around + load(1, j, 0, 1 - l) - q) * 0.2
                    change = along * ((load(0, j, 1) - load(0, j, -1)) + 1.0) - (
                        psi_n - psi_s
                    ) * (east[0] - west[0])
                    q_new = q - 0.025 * change
                    if l == 1:
                        q_new = q_new - DRAG_STEP * (around - 4.0 * psi)
                    dst[(i * 2 + l) * 2, j * SUB : (j + 1) * SUB, :] = q_new
                    dst[(i * 2 + l) * 2 + 1, j * SUB : (j + 1) * SUB, :] = psi_new
                    west, here = here, east
            return 0

        lax.fori_loop(low, high, body, 0)
        src, dst = dst, src
    return src


def turn_back(src, natural, turned):
    def body(r, _):
        for f in range(2):
            parts = []
            for l in range(LAYERS):
                slot = f * 2 + l
                plane = ((r + STEPS) * 2 + l) * 2 + f
                for j in range(PARTS):
                    natural[slot, pl.ds(j, SUB, stride=PARTS), :] = src[
                        plane, j * SUB : (j + 1) * SUB, :
                    ]
                parts.append(natural[slot, SUB : SUB + HALF, :])
            s = pl.multiple_of((r * 2 + f) * FULL, FULL)
            turned[pl.ds(s, FULL), :] = to_layers(*parts).T
        return 0

    lax.fori_loop(0, ROWS, body, 0)


def advance_members(
    edge, q_main, p_main, q_up, p_up, q_down, p_down, out_ref, first, second, natural, turned, *, groups, per
):
    def fill(refs, count, start):
        def body(r, _):
            for f in range(2):
                for l in range(LAYERS):
                    s = pl.multiple_of((r * 2 + l) * HALF, HALF)
                    value = refs[f][pl.ds(s, HALF), :]
                    ends = wide_roll(value[HALF - SUB :], MEM), wide_roll(value[:SUB], -MEM)
                    plane = ((r + start) * 2 + l) * 2 + f
                    place(natural, f * 2 + l, first, plane, value, *margins(value, MEM, *ends))
            return 0

        lax.fori_loop(0, count, body, 0)

    fill((q_main, p_main), ROWS, STEPS)
    fill((q_up, p_up), STEPS, 0)
    fill((q_down, p_down), STEPS, STEPS + ROWS)
    src = run_steps(edge, first, second)
    turn_back(src, natural, turned)
    for m in range(MEM):
        for d in range(groups):
            for c in range(per):
                for v in range(8):
                    s = v * 4 * FULL + (d * per + c) * MEM + m
                    out_ref[d, m, c * 8 + v] = turned[pl.ds(s, SUB, stride=HALF), :]
        for d in range(groups):
            def take(v):
                return out_ref[(d - 1) % groups, m, per * 8 - 8 + v], out_ref[(d + 1) % groups, m, v]

            out_ref[d, m, per * 8] = halo_pack(take)


def resample(
    parent, x_ref, n_ref, main_ref, edge_ref, up_ref, down_ref, z_ref, work, noise, *, members, per
):
    def one(k, _):
        p = parent[k]
        for c in range(per):
            for v in range(8):
                s = v * 4 * FULL + c * members + k
                work[pl.ds(s, SUB, stride=HALF), :] = x_ref[p, (c * 8 + v) * SUB : (c * 8 + v + 1) * SUB, :]
            for v in range(4):
                s = v * 4 * FULL + c * members + k
                noise[pl.ds(s, SUB, stride=HALF), :] = n_ref[k, c * 4 + v]
            for g in range(2):
                s = c * 64 + g * 32 + 2
                z_ref[c, pl.ds(g * SUB * members + k, SUB, stride=members), :] = x_ref[
                    k, pl.ds(s, SUB, stride=4), :
                ]
        edge_ref[pl.ds(k, SUB, stride=members), :] = x_ref[p, per * 64 :, :] + n_ref[k, per * 4]
        return 0

    lax.fori_loop(0, members, one, 0)
    for r in range(ROWS):
        for f in range(2):
            value = work[(r * 2 + f) * FULL : (r * 2 + f + 1) * FULL, :]
            if f == 0:
                value = value + noise[r * FULL : (r + 1) * FULL, :]
            for l, part in enumerate(by_layer(value.T)):
                s = ((r * 2 + l) * 2 + f) * HALF
                main_ref[s : s + HALF, :] = part
                if r < STEPS:
                    down_ref[s : s + HALF, :] = part
                if r >= ROWS - STEPS:
                    s -= (ROWS - STEPS) * 4 * HALF
                    up_ref[s : s + HALF, :] = part
    count = 4 * members
    segment = ((lax.broadcasted_iota(jnp.int32, (count, BW), 1) + SEG // 2) // SEG) % SUB
    even, odd = edge_ref[:count, :], wide_roll(edge_ref[count:, :], HALF)
    top = STEPS * 4 * HALF
    up_ref[top:, :] = jnp.where(segment >= 5, even, odd)
    down_ref[top:, :] = jnp.where(segment <= 2, even, odd)


def advance_columns(
    edge, parent, main_ref, edge_ref, up_ref, down_ref, out_ref, z_ref,
    first, second, natural, turned, sides, *, members, per
):
    top = STEPS * 4 * HALF
    count = 8 * members // BW
    for i in range(count):
        sides[i] = edge_ref[i * BW : (i + 1) * BW, :].T
    for i in range(count // 2):
        sides[count + i] = up_ref[top + i * BW : top + (i + 1) * BW, :].T
        sides[count + count // 2 + i] = down_ref[top + i * BW : top + (i + 1) * BW, :].T

    def put(source, at, plane, f, l, base, group):
        value = source[pl.ds(pl.multiple_of(at, HALF), HALF), :]
        index = base * BW + (f * 2 + l) * members
        matrix, offset = index // BW, index % BW
        before = pl.multiple_of((group * SEG + BW - SUB) % BW, SUB)
        after = pl.multiple_of(group * SEG, SUB)
        ends = (
            wide_roll(sides[matrix, pl.ds(before, SUB), :], -offset),
            wide_roll(sides[matrix, pl.ds(after, SUB), :], BW - members - offset),
        )
        place(natural, f * 2 + l, first, plane, value, *margins(value, members, *ends))

    def rows_own(v, _):
        for pair in range(2):
            for f in range(2):
                for l in range(LAYERS):
                    r = 2 * v + pair
                    at = ((r * 2 + l) * 2 + f) * HALF
                    put(main_ref, at, ((r + STEPS) * 2 + l) * 2 + f, f, l, pair * count // 2, v)
        return 0

    lax.fori_loop(0, SUB, rows_own, 0)

    def rows_beside(v, _):
        for pair in range(2):
            for f in range(2):
                for l in range(LAYERS):
                    r = 2 * v + pair
                    at = ((r * 2 + l) * 2 + f) * HALF
                    plane = (r * 2 + l) * 2 + f
                    put(up_ref, at, plane, f, l, count, v + 5 if pair == 0 else v + 1)
                    plane = ((r + STEPS + ROWS) * 2 + l) * 2 + f
                    put(down_ref, at, plane, f, l, count + count // 2, v if pair == 0 else v + 4)
        return 0

    lax.fori_loop(0, STEPS // 2, rows_beside, 0)
    src = run_steps(edge, first, second)
    turn_back(src, natural, turned)

    def one(k, _):
        p = parent[k]
        for c in range(per):
            for v in range(8):
                s = v * 4 * FULL + c * members + p
                out_ref[k, c * 8 + v] = turned[pl.ds(s, SUB, stride=HALF), :]
        return 0

    lax.fori_loop(0, members, one, 0)
    for c in range(per):
        for r in range(ROWS):
            s = (2 * r + 1) * FULL + c * members
            z_ref[c, r * members : (r + 1) * members, :] = turned[s : s + members, :]


def unpack_state(y_ref, q_ref, p_ref, *, groups, per):
    for d in range(groups):
        for c in range(per):
            b = d * per + c
            for l in range(LAYERS):
                for g in range(ROWS // SUB):
                    rows, cols = slice(g * SUB, (g + 1) * SUB), slice(b * BW, (b + 1) * BW)
                    s = c * 64 + g * 32 + l
                    q_ref[0, l, rows, cols] = y_ref[d, 0, pl.ds(s, SUB, stride=4), :]
                    p_ref[0, l, rows, cols] = y_ref[d, 0, pl.ds(s + 2, SUB, stride=4), :]


def score(rows_ref, z_ref, f_ref, o_ref, w_ref, out_ref, patch, total, *, members, per, chunk):
    a, c, j = pl.program_id(0), pl.program_id(1), pl.program_id(2)

    @pl.when((a == 0) & (c == 0) & (j == 0))
    def _():
        total[...] = jnp.zeros_like(total)

    @pl.when(j == 0)
    def _():
        start = rows_ref[a, c]
        for r in range(BR):
            s = pl.multiple_of((start + r) * members, SUB)
            part = z_ref[c, pl.ds(s, members), :]
            high = part.astype(jnp.bfloat16)
            patch[:members, r * BW : (r + 1) * BW] = high
            patch[members:, r * BW : (r + 1) * BW] = (part - high.astype(F32)).astype(jnp.bfloat16)

    weights = f_ref[0, 0]
    high = weights.astype(jnp.bfloat16)
    low = (weights - high.astype(F32)).astype(jnp.bfloat16)
    dims = (((1,), (1,)), ((), ()))
    main = lax.dot_general(patch[...], high, dims, preferred_element_type=F32)
    rest = lax.dot_general(patch[:members, :], low, dims, preferred_element_type=F32)
    predicted = main[:members] + (main[members:] + rest)
    miss = o_ref[0, 0] - predicted
    total[...] += w_ref[0, 0] * miss * miss

    @pl.when((a == pl.num_programs(0) - 1) & (c == pl.num_programs(1) - 1) & (j == pl.num_programs(2) - 1))
    def _():
        ones = jnp.full((SUB, total.shape[1]), -0.5, F32)
        out_ref[...] = lax.dot_general(
            ones, total[...], dims, precision=lax.Precision.HIGHEST, preferred_element_type=F32
        )


def shape(*dims):
    return jax.ShapeDtypeStruct(dims, F32)


def call(kernel, outs, scratch=(), scalars=0, name=None):
    def run(*args):
        specs = [pl.BlockSpec(memory_space=pltpu.SMEM)] * scalars
        specs += [pl.BlockSpec(memory_space=pltpu.VMEM)] * (len(args) - scalars)
        return pl.pallas_call(
            kernel,
            out_shape=outs,
            in_specs=specs,
            out_specs=[pl.BlockSpec(memory_space=pltpu.VMEM)] * len(outs),
            scratch_shapes=list(scratch),
            compiler_params=pltpu.CompilerParams(vmem_limit_bytes=VMEM_LIMIT),
            name=name,
        )(*args)

    return run


def shards(
    vorticity, streamfunction, model_noise, offspring, footprint, observed, precision, block_rows
):
    groups, tiles = lax.axis_size("dom"), lax.axis_size("tile")
    members = offspring.shape[1]
    width = vorticity.shape[3]
    blocks = width // BW
    per = blocks // groups
    bands, observations, cells = footprint.shape[0], footprint.shape[2], footprint.shape[3]

    running = jnp.cumsum(offspring, axis=1)
    slots = jnp.arange(members, dtype=jnp.int32)
    parent = jnp.sum((running[:, None, :] <= slots[None, :, None]).astype(jnp.int32), axis=2)
    parent = jnp.minimum(parent, members - 1)
    edge = jnp.stack([lax.axis_index("tile"), jnp.int32(tiles)]).astype(jnp.int32)

    up = [(i, i + 1) for i in range(tiles - 1)]
    down = [(i + 1, i) for i in range(tiles - 1)]
    params = pltpu.CompilerParams(vmem_limit_bytes=VMEM_LIMIT)

    def pack(field, *noise):
        half = (MEM, LAYERS, SUB, width)
        return pl.pallas_call(
            functools.partial(pack_field, blocks=blocks, noisy=bool(noise)),
            grid=(2,),
            in_specs=[pl.BlockSpec(half, lambda i: (0, 0, i, 0))]
            + [pl.BlockSpec((1,) + half, lambda i: (0, 0, 0, i, 0))] * len(noise),
            out_specs=[
                pl.BlockSpec((SUB * FULL, BW), lambda i: (i, 0)),
                pl.BlockSpec((STEPS * FULL, BW), lambda i: (0, 0)),
                pl.BlockSpec((STEPS * FULL, BW), lambda i: (0, 0)),
            ],
            out_shape=[shape(ROWS * FULL, BW), shape(STEPS * FULL, BW), shape(STEPS * FULL, BW)],
            scratch_shapes=[pltpu.VMEM((SUB * FULL, BW), F32)],
            compiler_params=params,
            name="pack_q" if noise else "pack_psi",
        )(field, *noise)

    p_main, p_up, p_down = pack(streamfunction)
    vorticity, p_up, p_down = lax.optimization_barrier((vorticity, p_up, p_down))
    p_below = lax.ppermute(p_up, "tile", up)
    p_above = lax.ppermute(p_down, "tile", down)
    q_main, q_up, q_down = pack(vorticity, model_noise)
    q_below = lax.ppermute(q_up, "tile", up)
    q_above = lax.ppermute(q_down, "tile", down)

    later_noise, p_below, p_above = lax.optimization_barrier((model_noise, p_below, p_above))
    noise = pl.pallas_call(
        functools.partial(pack_noise, groups=groups, per=per),
        grid=(1,),
        in_specs=[pl.BlockSpec((1, MEM, LAYERS, ROWS, width), lambda i: (1, 0, 0, 0, 0))],
        out_specs=pl.BlockSpec((groups, MEM, per * 4 + 1, SUB, BW), lambda i: (0, 0, 0, 0, 0)),
        out_shape=shape(groups, MEM, per * 4 + 1, SUB, BW),
        scratch_shapes=[pltpu.VMEM((ROWS * FULL, BW), F32), pltpu.VMEM((2 * ROWS * FULL, BW), F32)],
        compiler_params=params,
        name="pack_noise",
    )(later_noise)
    noise, q_below, q_above = lax.optimization_barrier((noise, q_below, q_above))
    noise = lax.all_to_all(noise, "dom", split_axis=0, concat_axis=0, tiled=True)
    noise = noise.reshape(members, per * 4 + 1, SUB, BW)

    work = [
        pltpu.VMEM((DEEP * 4, PARTS * SUB, BW), F32),
        pltpu.VMEM((DEEP * 4, PARTS * SUB, BW), F32),
        pltpu.VMEM((4, PARTS * SUB, BW), F32),
        pltpu.VMEM((2 * ROWS * FULL, BW), F32),
    ]
    (sent,) = call(
        functools.partial(advance_members, groups=groups, per=per),
        [shape(groups, MEM, per * 8 + 1, SUB, BW)],
        work,
        scalars=1,
        name="advance_members",
    )(edge, q_main, p_main, q_below, p_below, q_above, p_above)
    owned = lax.all_to_all(sent, "dom", split_axis=0, concat_axis=0, tiled=True)
    owned = owned.reshape(members, (per * 8 + 1) * SUB, BW)

    beside = STEPS * 4 * HALF + 4 * members
    main, sides, to_up, to_down, surface = call(
        functools.partial(resample, members=members, per=per),
        [
            shape(ROWS * 4 * HALF, BW),
            shape(8 * members, BW),
            shape(beside, BW),
            shape(beside, BW),
            shape(per, ROWS * members, BW),
        ],
        [pltpu.VMEM((2 * ROWS * FULL, BW), F32), pltpu.VMEM((ROWS * FULL, BW), F32)],
        scalars=1,
        name="resample",
    )(parent[0], owned, noise)
    from_below = lax.ppermute(to_up, "tile", up)
    from_above = lax.ppermute(to_down, "tile", down)

    def likelihood(surface):
        chunk = observations
        obs = (bands, per, 1, observations)
        out = pl.pallas_call(
            functools.partial(score, members=members, per=per, chunk=chunk),
            grid=(bands, per, observations // chunk),
            in_specs=[
                pl.BlockSpec(memory_space=pltpu.SMEM),
                pl.BlockSpec((per, ROWS * members, BW), lambda a, c, j: (0, 0, 0)),
                pl.BlockSpec((1, 1, chunk, cells), lambda a, c, j: (a, c, j, 0)),
                pl.BlockSpec((1, 1, 1, chunk), lambda a, c, j: (a, c, 0, j)),
                pl.BlockSpec((1, 1, 1, chunk), lambda a, c, j: (a, c, 0, j)),
            ],
            out_specs=pl.BlockSpec((SUB, members), lambda a, c, j: (0, 0)),
            out_shape=shape(SUB, members),
            scratch_shapes=[
                pltpu.VMEM((2 * members, cells), jnp.bfloat16),
                pltpu.VMEM((members, chunk), F32),
            ],
            compiler_params=params,
            name="score",
        )(block_rows, surface, footprint, observed.reshape(obs), precision.reshape(obs))
        return out[:1]

    logs = [likelihood(surface)]
    main, logs[0] = lax.optimization_barrier((main, logs[0]))

    back, surface = call(
        functools.partial(advance_columns, members=members, per=per),
        [shape(members, per * 8, SUB, BW), shape(per, ROWS * members, BW)],
        work + [pltpu.VMEM((members // SUB * 2, BW, BW), F32)],
        scalars=2,
        name="advance_columns",
    )(edge, parent[1], main, sides, from_below, from_above)
    back = back.reshape(groups, MEM, per * 64, BW)
    mine = lax.all_to_all(back, "dom", split_axis=0, concat_axis=0, tiled=True)
    logs.append(likelihood(surface))

    q_out, psi_out = pl.pallas_call(
        functools.partial(unpack_state, groups=groups, per=per),
        grid=(MEM,),
        in_specs=[pl.BlockSpec((groups, 1, per * 64, BW), lambda i: (0, i, 0, 0))],
        out_specs=[pl.BlockSpec((1, LAYERS, ROWS, width), lambda i: (i, 0, 0, 0))] * 2,
        out_shape=[shape(MEM, LAYERS, ROWS, width)] * 2,
        compiler_params=params,
        name="unpack_state",
    )(mine)

    loglik = jnp.concatenate(logs, axis=0)
    for axis, size in (("tile", tiles), ("dom", groups)):
        hop = 1
        while hop < size:
            pairs = [(i, i ^ hop) for i in range(size)]
            loglik = loglik + lax.ppermute(loglik, axis, pairs)
            hop *= 2
    total_obs = observed.size * groups * tiles
    mean_loglik = loglik / total_obs
    highest = jnp.max(loglik, axis=1, keepdims=True)
    scaled = jnp.exp(loglik - highest)
    weights = scaled / jnp.sum(scaled, axis=1, keepdims=True)
    return (q_out, psi_out, mean_loglik, weights)


def solution(mesh):
    return jax.shard_map(
        shards,
        mesh=mesh,
        in_specs=(
            P("dom", None, "tile", None),
            P("dom", None, "tile", None),
            P(None, "dom", None, "tile", None),
            P(),
            P("tile", "dom", None, None),
            P("tile", "dom", None),
            P("tile", "dom", None),
            P("tile", "dom"),
        ),
        out_specs=(P("dom", None, "tile", None), P("dom", None, "tile", None), P(), P()),
        check_vma=False,
    )
```

time: 209 us -> 179 us (0.86)
  waiting for transfers between devices: 68.5 us -> 49.5 us
  Pallas kernels: 92.1 us -> 79.6 us
  starting transfers between devices: 35.8 us -> 38.4 us
    ppermute x2 -> x1, waiting for transfers between devices: 16.5 us -> 2.69 us  [shards(): from_below = lax.ppermute(to_up, 'tile', up)]
    pallas_call x3, Pallas kernels: 55.9 us -> 43.1 us  [run(): pl.pallas_call(kernel, out_shape=outs, in_specs=specs, out_specs=[pl.Bloc...]
    ppermute x0 -> x4, starting transfers between devices: none -> 12.1 us  [the longest x1 4.94 us: shards(): p_below = lax.ppermute(p_up, 'tile', up)]
    ppermute x5, waiting for transfers between devices: 16.9 us -> 10.8 us  [shards(): loglik = loglik + lax.ppermute(loglik, axis, pairs)]
    ppermute x0 -> x4, waiting for transfers between devices: none -> 4.86 us  [the longest x1 3.07 us: shards(): q_above = lax.ppermute(q_down, 'tile', down)]
    ppermute x2 -> x1, starting transfers between devices: 9.1 us -> 4.26 us  [shards(): from_below = lax.ppermute(to_up, 'tile', up)]
    pallas_call x2, Pallas kernels: 23.5 us -> 19.6 us  [likelihood(): pl.pallas_call(functools.partial(score, members=members, per=per, chunk=c...]
    ppermute x2 -> x1, waiting for transfers between devices: 7.91 us -> 4.06 us  [shards(): from_above = lax.ppermute(to_down, 'tile', down)]
  transfers between devices with their start and end apart: 12 -> 14, of which waited for: 10 -> 10; matrix products, arithmetic and copies ran while one was open for 2% -> 3% of each run, Pallas kernels for 21% -> 26%
where the time goes in v2:
time: 179 us; the launch traced here: 178 us
  Pallas kernels  79.6 us (44%)
  waiting for transfers between devices  49.5 us (28%)
  starting transfers between devices  38.4 us (21%)
  local copies, waits for them, and re-layouts  7.84 us (4%)
  other arithmetic  1.9 us (1%)
    pallas_call x3, Pallas kernels, run(): pl.pallas_call(kernel, out_shape=outs, in_specs=specs, out_specs=[pl.Bloc...  43.1 us
    all_to_all x1, waiting for transfers between devices, shards(): owned = lax.all_to_all(sent, 'dom', split_axis=0, concat_axis=0, tiled=True)  27.2 us
    pallas_call x2, Pallas kernels, likelihood(): pl.pallas_call(functools.partial(score, members=members, per=per, chunk=c...  19.6 us
    ppermute x5, waiting for transfers between devices, shards(): loglik = loglik + lax.ppermute(loglik, axis, pairs)  10.8 us
    ppermute x5, starting transfers between devices, shards(): loglik = loglik + lax.ppermute(loglik, axis, pairs)  8.03 us
    pallas_call x2, Pallas kernels, pack(): pl.pallas_call(functools.partial(pack_field, blocks=blocks, noisy=bool(no...  7.25 us
    pallas_call x1, Pallas kernels, shards(): pl.pallas_call(functools.partial(pack_noise, groups=groups, per=per), gri...  5.94 us
    ppermute x1, starting transfers between devices, shards(): p_below = lax.ppermute(p_up, 'tile', up)  4.94 us
  transfers between devices with their start and end apart: 14, of which 10 were waited for; matrix products, arithmetic and copies ran while one was open for 3% of the time, Pallas kernels for 26%

profile of v2, /device:TPU:0, one launch (start us, length us, event | category | flops | bytes accessed | tf_op | source)
XLA Modules:
  0.0 178.1 jit_solution(12178395460750734077)
XLA Ops:
  0.6 3.5 %pack_psi.1 = (f32[2048,128]{1,0:T(8,128)}, f32[768,128]{1,0:T(8,128)}, f32[768,128]{1,0:T(8,128)}) custom-call(f32[4,2,16,2048]{3,2,1,0:T(8,128)} %refs_0_.1), custom_call_target="tpu_custom_call" | custom-call | tf_op jit(solution)/shard_map/pack_psi/pallas_call | solution.py:437
  4.2 4.9 %collective-permute-start = (f32[768,128]{1,0:T(8,128)}, f32[768,128]{1,0:T(8,128)S(1)}, u32[]{:S(2)}, u32[]{:S(2)}) collective-permute-start(f32[768,128]{1,0:T(8,128)} %get-tuple-element.35), channel_id=1, source_target_pairs={{0,1},{1,2},{2,3},{4,5},{5,6},{6,7},{8,9},{9,10},{10,11},{12,13},{... | collective-permute-start | bytes 1179656 | tf_op jit(solution)/shard_map/ppermute | solution.py:455
  10.4 3.7 %pack_q.1 = (f32[2048,128]{1,0:T(8,128)}, f32[768,128]{1,0:T(8,128)}, f32[768,128]{1,0:T(8,128)}) custom-call(f32[4,2,16,2048]{3,2,1,0:T(8,128)} %refs_0_.2, f32[2,4,2,16,2048]{4,3,2,1,0:T(8,128)} %n_ref), custom_call_target="tpu_custom_call" | custom-call | tf_op jit(solution)/shard_map/pack_q/pallas_call | solution.py:437
  14.1 4.6 %collective-permute-start.2 = (f32[768,128]{1,0:T(8,128)}, f32[768,128]{1,0:T(8,128)S(1)}, u32[]{:S(2)}, u32[]{:S(2)}) collective-permute-start(f32[768,128]{1,0:T(8,128)} %get-tuple-element.38), channel_id=1, source_target_pairs={{0,1},{1,2},{2,3},{4,5},{5,6},{6,7},{8,9},{9,10},{10,11},{12,13},{... | collective-permute-start | bytes 1179656 | tf_op jit(solution)/shard_map/ppermute | solution.py:458
  21.8 5.9 %pack_noise.1 = f32[8,4,9,8,128]{4,3,2,1,0:T(8,128)} custom-call(f32[2,4,2,16,2048]{4,3,2,1,0:T(8,128)} %n_ref), custom_call_target="tpu_custom_call" | custom-call | tf_op jit(solution)/shard_map/pack_noise/pallas_call | solution.py:462
  27.7 3.1 %collective-permute-done.3.q_down = f32[768,128]{1,0:T(8,128)S(1)} collective-permute-done((f32[768,128]{1,0:T(8,128)}, f32[768,128]{1,0:T(8,128)S(1)}, u32[]{:S(2)}, u32[]{:S(2)}) %collective-permute-start.3) | collective-permute-done | bytes 393248 | tf_op jit(solution)/shard_map/ppermute | solution.py:459
  30.8 3.7 %all-to-all-start.1 = ((f32[8,4,9,8,128]{4,3,2,1,0:T(8,128)}), f32[8,4,9,8,128]{4,3,2,1,0:T(8,128)S(1)}, u32[]{:S(2)}, u32[]{:S(2)}) async-start(f32[8,4,9,8,128]{4,3,2,1,0:T(8,128)} %pack_noise.1), calls=%async_computation.1 | async-start | bytes 2359296 | tf_op jit(solution)/shard_map/all_to_all | solution.py:473
  35.1 16.9 %advance_members.1 = f32[8,4,17,8,128]{4,3,2,1,0:T(8,128)} custom-call(s32[2]{0:T(128)} %pad_add_fusion.edge, f32[2048,128]{1,0:T(8,128)} %get-tuple-element.33.q_main, f32[2048,128]{1,0:T(8,128)} %get-tuple-element.34.p_main, f32[768,128]{1,0:T(8,128)} %copy-done.7, f32[768,128]{1,0:T(8,128)} %copy-done.5, f32[768,128]{1,0:T(8,128)} %copy-done.8, ...), custom_call_target="tpu_custom_call" | custom-call | tf_op jit(solution)/shard_map/advance_members/pallas_call | solution.py:402
  53.1 4.2 %all-to-all-start = ((f32[8,4,17,8,128]{4,3,2,1,0:T(8,128)}), f32[8,4,17,8,128]{4,3,2,1,0:T(8,128)S(1)}, u32[]{:S(2)}, u32[]{:S(2)}) async-start(f32[8,4,17,8,128]{4,3,2,1,0:T(8,128)} %advance_members.1), calls=%async_computation | async-start | bytes 4456448 | tf_op jit(solution)/shard_map/all_to_all | solution.py:489
  58.2 27.2 %all-to-all-done = f32[8,4,17,8,128]{4,3,2,1,0:T(8,128)S(1)} async-done(((f32[8,4,17,8,128]{4,3,2,1,0:T(8,128)}), f32[8,4,17,8,128]{4,3,2,1,0:T(8,128)S(1)}, u32[]{:S(2)}, u32[]{:S(2)}) %all-to-all-start) | async-done | bytes 2228256 | tf_op jit(solution)/shard_map/all_to_all | solution.py:489
  86.7 9.2 %resample.1 = (f32[4096,128]{1,0:T(8,128)}, f32[256,128]{1,0:T(8,128)}, f32[1664,128]{1,0:T(8,128)}, f32[1664,128]{1,0:T(8,128)}, f32[2,512,128]{2,1,0:T(8,128)}) custom-call(s32[32]{0:T(128)} %get-tuple-element.60.parent, f32[32,136,128]{2,1,0:T(8,128)} %bitcast.8, f32[32,9,8,128]{3,2,1,0:T(8,128)} %bitcast.9), custom_call_target="tpu_custom_call" | custom-call | tf_op jit(solution)/shard_map/resample/pallas_call | solution.py:402
  95.9 4.3 %collective-permute-start.4 = (f32[1664,128]{1,0:T(8,128)}, f32[1664,128]{1,0:T(8,128)S(1)}, u32[]{:S(2)}, u32[]{:S(2)}) collective-permute-start(f32[1664,128]{1,0:T(8,128)} %get-tuple-element.49), channel_id=1, source_target_pairs={{0,1},{1,2},{2,3},{4,5},{5,6},{6,7},{8,9},{9,10},{10,11},{12,13},{... | collective-permute-start | bytes 2555912 | tf_op jit(solution)/shard_map/ppermute | solution.py:506
  102.7 9.8 %score.2 = f32[8,32]{1,0:T(8,128)} custom-call(s32[2,2]{1,0:T(2,128)} %rows_ref.3, f32[2,512,128]{2,1,0:T(8,128)} %get-tuple-element.46.z_ref, f32[2,2,1024,1024]{3,2,1,0:T(8,128)} %f_ref.3, f32[2,2,1,1024]{3,2,1,0:T(1,128)} %reshape.32.o_ref, f32[2,2,1,1024]{3,2,1,0:T(1,128)} %reshape.33.w_ref), custom_call_target="tpu_custom_call" | custom-call | tf_op jit(solution)/shard_map/score/pallas_call | solution.py:512
  113.1 2.7 %collective-permute-done.4.up_ref = f32[1664,128]{1,0:T(8,128)S(1)} collective-permute-done((f32[1664,128]{1,0:T(8,128)}, f32[1664,128]{1,0:T(8,128)S(1)}, u32[]{:S(2)}, u32[]{:S(2)}) %collective-permute-start.4) | collective-permute-done | bytes 852000 | tf_op jit(solution)/shard_map/ppermute | solution.py:506
  115.8 4.1 %collective-permute-done.5.down_ref = f32[1664,128]{1,0:T(8,128)S(1)} collective-permute-done((f32[1664,128]{1,0:T(8,128)}, f32[1664,128]{1,0:T(8,128)S(1)}, u32[]{:S(2)}, u32[]{:S(2)}) %collective-permute-start.5) | collective-permute-done | bytes 852000 | tf_op jit(solution)/shard_map/ppermute | solution.py:507
  120.8 17.1 %advance_columns.1 = (f32[32,16,8,128]{3,2,1,0:T(8,128)}, f32[2,512,128]{2,1,0:T(8,128)}) custom-call(s32[2]{0:T(128)} %pad_add_fusion.edge, s32[32]{0:T(128)} %get-tuple-element.61.parent, f32[4096,128]{1,0:T(8,128)} %get-tuple-element.47.main_ref, f32[256,128]{1,0:T(8,128)} %get-tuple-element.48.edge_ref, f32[1664,128]{1,0:T(8,128)} %copy-done.3, ...), custom_call_target="tpu_custom_call" | custom-call | tf_op jit(solution)/shard_map/advance_columns/pallas_call | solution.py:402
  137.9 4.8 %all-to-all-start.2 = ((f32[8,4,128,128]{3,2,1,0:T(8,128)}), f32[8,4,128,128]{3,2,1,0:T(8,128)S(1)}, u32[]{:S(2)}, u32[]{:S(2)}) async-start(f32[8,4,128,128]{3,2,1,0:T(8,128)} %bitcast.10), calls=%async_computation.2 | async-start | bytes 4194304 | tf_op jit(solution)/shard_map/all_to_all | solution.py:544
  142.7 9.8 %score.3 = f32[8,32]{1,0:T(8,128)} custom-call(s32[2,2]{1,0:T(2,128)} %rows_ref.3, f32[2,512,128]{2,1,0:T(8,128)} %get-tuple-element.55.z_ref, f32[2,2,1024,1024]{3,2,1,0:T(8,128)} %f_ref.3, f32[2,2,1,1024]{3,2,1,0:T(1,128)} %reshape.32.o_ref, f32[2,2,1,1024]{3,2,1,0:T(1,128)} %reshape.33.w_ref), custom_call_target="tpu_custom_call" | custom-call | tf_op jit(solution)/shard_map/score/pallas_call | solution.py:512
  153.2 2.4 %collective-permute-start.6 = (f32[2,32]{1,0:T(2,128)S(1)}, f32[2,32]{1,0:T(2,128)S(1)}, u32[]{:S(2)}, u32[]{:S(2)}) collective-permute-start(f32[2,32]{1,0:T(2,128)S(1)} %pad_maximum_fusion), channel_id=1, source_target_pairs={{0,1},{1,0},{2,3},{3,2},{4,5},{5,4},{6,7},{7,6},{8,9},{9,8},{10,11... | collective-permute-start | bytes 776 | tf_op jit(solution)/shard_map/ppermute | solution.py:562
  158.9 2.7 %collective-permute-done.7 = f32[2,32]{1,0:T(2,128)S(1)} collective-permute-done((f32[2,32]{1,0:T(2,128)S(1)}, f32[2,32]{1,0:T(2,128)S(1)}, u32[]{:S(2)}, u32[]{:S(2)}) %collective-permute-start.7) | collective-permute-done | bytes 288 | tf_op jit(solution)/shard_map/ppermute | solution.py:562
  162.9 2.3 %collective-permute-start.9 = (f32[2,32]{1,0:T(2,128)S(1)}, f32[2,32]{1,0:T(2,128)S(1)}, u32[]{:S(2)}, u32[]{:S(2)}) collective-permute-start(f32[2,32]{1,0:T(2,128)S(1)} %add.17), channel_id=1, source_target_pairs={{0,8},{4,12},{8,0},{12,4},{16,24},{20,28},{24,16},{28,20},{1,9},{5... | collective-permute-start | bytes 776 | tf_op jit(solution)/shard_map/ppermute | solution.py:562
  165.2 3.3 %collective-permute-done.9 = f32[2,32]{1,0:T(2,128)S(1)} collective-permute-done((f32[2,32]{1,0:T(2,128)S(1)}, f32[2,32]{1,0:T(2,128)S(1)}, u32[]{:S(2)}, u32[]{:S(2)}) %collective-permute-start.9) | collective-permute-done | bytes 288 | tf_op jit(solution)/shard_map/ppermute | solution.py:562
  169.9 2.1 %collective-permute-done.10 = f32[2,32]{1,0:T(2,128)S(1)} collective-permute-done((f32[2,32]{1,0:T(2,128)S(1)}, f32[2,32]{1,0:T(2,128)S(1)}, u32[]{:S(2)}, u32[]{:S(2)}) %collective-permute-start.10) | collective-permute-done | bytes 288 | tf_op jit(solution)/shard_map/ppermute | solution.py:562
  174.3 3.8 %unpack_state.1 = (f32[4,2,16,2048]{3,2,1,0:T(8,128)}, f32[4,2,16,2048]{3,2,1,0:T(8,128)}) custom-call(f32[8,4,128,128]{3,2,1,0:T(8,128)} %copy-done.1), custom_call_target="tpu_custom_call" | custom-call | tf_op jit(solution)/shard_map/unpack_state/pallas_call | solution.py:547
  (54 shorter events, 21.4 us)
Async XLA Ops:
  4.2 15.8 %collective-permute-start = (f32[768,128]{1,0:T(8,128)}, f32[768,128]{1,0:T(8,128)S(1)}, u32[]{:S(2)}, u32[]{:S(2)}) collective-permute-start(f32[768,128]{1,0:T(8,128)} %get-tuple-element.35), channel_id=1, source_target_pairs={{0,1},{1,2},{2,3},{4,5},{5,6},{6,7},{8,9},{9,10},{10,11},{12,13},{... | collective-permute-start | bytes 1179656 | tf_op jit(solution)/shard_map/ppermute | solution.py:455
  9.1 12.7 %collective-permute-start.1 = (f32[768,128]{1,0:T(8,128)}, f32[768,128]{1,0:T(8,128)S(1)}, u32[]{:S(2)}, u32[]{:S(2)}) collective-permute-start(f32[768,128]{1,0:T(8,128)} %get-tuple-element.36), channel_id=1, source_target_pairs={{1,0},{2,1},{3,2},{5,4},{6,5},{7,6},{9,8},{10,9},{11,10},{13,12},{... | collective-permute-start | bytes 1179656 | tf_op jit(solution)/shard_map/ppermute | solution.py:456
  14.1 13.6 %collective-permute-start.2 = (f32[768,128]{1,0:T(8,128)}, f32[768,128]{1,0:T(8,128)S(1)}, u32[]{:S(2)}, u32[]{:S(2)}) collective-permute-start(f32[768,128]{1,0:T(8,128)} %get-tuple-element.38), channel_id=1, source_target_pairs={{0,1},{1,2},{2,3},{4,5},{5,6},{6,7},{8,9},{9,10},{10,11},{12,13},{... | collective-permute-start | bytes 1179656 | tf_op jit(solution)/shard_map/ppermute | solution.py:458
  18.7 12.1 %collective-permute-start.3 = (f32[768,128]{1,0:T(8,128)}, f32[768,128]{1,0:T(8,128)S(1)}, u32[]{:S(2)}, u32[]{:S(2)}) collective-permute-start(f32[768,128]{1,0:T(8,128)} %get-tuple-element.39), channel_id=1, source_target_pairs={{1,0},{2,1},{3,2},{5,4},{6,5},{7,6},{9,8},{10,9},{11,10},{13,12},{... | collective-permute-start | bytes 1179656 | tf_op jit(solution)/shard_map/ppermute | solution.py:459
  20.0 10.8 %copy-start.5 = (f32[768,128]{1,0:T(8,128)}, f32[768,128]{1,0:T(8,128)S(1)}, u32[]{:S(2)}) copy-start(f32[768,128]{1,0:T(8,128)S(1)} %collective-permute-done.p_up) | copy-start | bytes 1179652
  21.8 9.0 %copy-start.6 = (f32[768,128]{1,0:T(8,128)}, f32[768,128]{1,0:T(8,128)S(1)}, u32[]{:S(2)}) copy-start(f32[768,128]{1,0:T(8,128)S(1)} %collective-permute-done.1.p_down) | copy-start | bytes 1179652
  27.7 7.4 %copy-start.7 = (f32[768,128]{1,0:T(8,128)}, f32[768,128]{1,0:T(8,128)S(1)}, u32[]{:S(2)}) copy-start(f32[768,128]{1,0:T(8,128)S(1)} %collective-permute-done.2.q_up) | copy-start | bytes 1179652
  30.8 4.3 %copy-start.8 = (f32[768,128]{1,0:T(8,128)}, f32[768,128]{1,0:T(8,128)S(1)}, u32[]{:S(2)}) copy-start(f32[768,128]{1,0:T(8,128)S(1)} %collective-permute-done.3.q_down) | copy-start | bytes 1179652
  30.8 21.2 %all-to-all-start.1 = ((f32[8,4,9,8,128]{4,3,2,1,0:T(8,128)}), f32[8,4,9,8,128]{4,3,2,1,0:T(8,128)S(1)}, u32[]{:S(2)}, u32[]{:S(2)}) async-start(f32[8,4,9,8,128]{4,3,2,1,0:T(8,128)} %pack_noise.1), calls=%async_computation.1 | async-start | bytes 2359296 | tf_op jit(solution)/shard_map/all_to_all | solution.py:473
  52.0 5.3 %copy-start.11 = (s32[2,32]{1,0:T(2,128)S(1)}, s32[2,32]{1,0:T(2,128)}, u32[]{:S(2)}) copy-start(s32[2,32]{1,0:T(2,128)} %param.11) | copy-start | bytes 772
  53.1 32.2 %all-to-all-start = ((f32[8,4,17,8,128]{4,3,2,1,0:T(8,128)}), f32[8,4,17,8,128]{4,3,2,1,0:T(8,128)S(1)}, u32[]{:S(2)}, u32[]{:S(2)}) async-start(f32[8,4,17,8,128]{4,3,2,1,0:T(8,128)} %advance_members.1), calls=%async_computation | async-start | bytes 4456448 | tf_op jit(solution)/shard_map/all_to_all | solution.py:489
  57.3 44.2 %copy-start.9 = (f32[2,2,1024]{2,1,0:T(2,128)S(1)}, f32[2,2,1024]{2,1,0:T(2,128)}, u32[]{:S(2)}) copy-start(f32[2,2,1024]{2,1,0:T(2,128)} %param.13) | copy-start | bytes 49156
  57.3 44.8 %copy-start.10 = (f32[2,2,1024]{2,1,0:T(2,128)S(1)}, f32[2,2,1024]{2,1,0:T(2,128)}, u32[]{:S(2)}) copy-start(f32[2,2,1024]{2,1,0:T(2,128)} %param.14) | copy-start | bytes 49156
  85.3 1.4 copy-start
  95.9 19.9 %collective-permute-start.4 = (f32[1664,128]{1,0:T(8,128)}, f32[1664,128]{1,0:T(8,128)S(1)}, u32[]{:S(2)}, u32[]{:S(2)}) collective-permute-start(f32[1664,128]{1,0:T(8,128)} %get-tuple-element.49), channel_id=1, source_target_pairs={{0,1},{1,2},{2,3},{4,5},{5,6},{6,7},{8,9},{9,10},{10,11},{12,13},{... | collective-permute-start | bytes 2555912 | tf_op jit(solution)/shard_map/ppermute | solution.py:506
  100.1 19.7 %collective-permute-start.5 = (f32[1664,128]{1,0:T(8,128)}, f32[1664,128]{1,0:T(8,128)S(1)}, u32[]{:S(2)}, u32[]{:S(2)}) collective-permute-start(f32[1664,128]{1,0:T(8,128)} %get-tuple-element.50), channel_id=1, source_target_pairs={{1,0},{2,1},{3,2},{5,4},{6,5},{7,6},{9,8},{10,9},{11,10},{13,12},{... | collective-permute-start | bytes 2555912 | tf_op jit(solution)/shard_map/ppermute | solution.py:507
  115.8 4.1 %copy-start.3 = (f32[1664,128]{1,0:T(8,128)}, f32[1664,128]{1,0:T(8,128)S(1)}, u32[]{:S(2)}) copy-start(f32[1664,128]{1,0:T(8,128)S(1)} %collective-permute-done.4.up_ref) | copy-start | bytes 2555908
  137.9 35.1 %all-to-all-start.2 = ((f32[8,4,128,128]{3,2,1,0:T(8,128)}), f32[8,4,128,128]{3,2,1,0:T(8,128)S(1)}, u32[]{:S(2)}, u32[]{:S(2)}) async-start(f32[8,4,128,128]{3,2,1,0:T(8,128)} %bitcast.10), calls=%async_computation.2 | async-start | bytes 4194304 | tf_op jit(solution)/shard_map/all_to_all | solution.py:544
  153.2 3.9 %collective-permute-start.6 = (f32[2,32]{1,0:T(2,128)S(1)}, f32[2,32]{1,0:T(2,128)S(1)}, u32[]{:S(2)}, u32[]{:S(2)}) collective-permute-start(f32[2,32]{1,0:T(2,128)S(1)} %pad_maximum_fusion), channel_id=1, source_target_pairs={{0,1},{1,0},{2,3},{3,2},{4,5},{5,4},{6,7},{7,6},{8,9},{9,8},{10,11... | collective-permute-start | bytes 776 | tf_op jit(solution)/shard_map/ppermute | solution.py:562
  157.1 4.5 %collective-permute-start.7 = (f32[2,32]{1,0:T(2,128)S(1)}, f32[2,32]{1,0:T(2,128)S(1)}, u32[]{:S(2)}, u32[]{:S(2)}) collective-permute-start(f32[2,32]{1,0:T(2,128)S(1)} %fusion.2), channel_id=1, source_target_pairs={{0,2},{1,3},{2,0},{3,1},{4,6},{5,7},{6,4},{7,5},{8,10},{9,11},{10,... | collective-permute-start | bytes 776 | tf_op jit(solution)/shard_map/ppermute | solution.py:562
  161.7 1.2 collective-permute-start.8
  162.9 5.6 %collective-permute-start.9 = (f32[2,32]{1,0:T(2,128)S(1)}, f32[2,32]{1,0:T(2,128)S(1)}, u32[]{:S(2)}, u32[]{:S(2)}) collective-permute-start(f32[2,32]{1,0:T(2,128)S(1)} %add.17), channel_id=1, source_target_pairs={{0,8},{4,12},{8,0},{12,4},{16,24},{20,28},{24,16},{28,20},{1,9},{5... | collective-permute-start | bytes 776 | tf_op jit(solution)/shard_map/ppermute | solution.py:562
  168.4 3.6 %collective-permute-start.10 = (f32[2,32]{1,0:T(2,128)S(1)}, f32[2,32]{1,0:T(2,128)S(1)}, u32[]{:S(2)}, u32[]{:S(2)}) collective-permute-start(f32[2,32]{1,0:T(2,128)S(1)} %add.18), channel_id=1, source_target_pairs={{0,16},{4,20},{8,24},{12,28},{16,0},{20,4},{24,8},{28,12},{1,17},{... | collective-permute-start | bytes 776 | tf_op jit(solution)/shard_map/ppermute | solution.py:562
  173.0 1.3 copy-start.1
  (2 other events, 2.0 us)

commit v3 on v2

--- a/solution.py
+++ b/solution.py
@@ -21,6 +21,7 @@
 DRAG_STEP = 0.1 * 0.2
 HALF = 64
 PARTS = 10
+QUAD = ROWS // 4
 DEEP = ROWS + 2 * STEPS
 FULL = 2 * HALF
 
@@ -37,7 +38,7 @@
     segment = ((lanes() + SEG // 2) // SEG) % SUB
     lower = lanes() < BW // 2
     packed = None
-    for j in range(SUB):
+    for j in range(QUAD):
         before, after = take(j)
         edge = lane_roll(jnp.where(lower, after, before), SEG * j)
         packed = edge if packed is None else jnp.where(segment == j, edge, packed)
@@ -92,32 +93,32 @@
         up_ref[...] = main_ref[(SUB - STEPS) * FULL :, :]
 
 
-def pack_noise(n_ref, out_ref, work, wide, *, groups, per):
+def send_rows(work, base, out_ref, groups, per):
     blocks = groups * per
-    for b in range(blocks):
+    for m in range(MEM):
+        for d in range(groups):
+            def rows(block, v):
+                s = base + v * 4 * FULL + block % blocks * MEM + m
+                return work[pl.ds(s, SUB, stride=HALF), :]
+
+            for c in range(per):
+                for v in range(QUAD):
+                    out_ref[d, m, c * QUAD + v] = rows(d * per + c, v)
+            out_ref[d, m, per * QUAD] = halo_pack(
+                lambda v: (rows(d * per - 1, v), rows(d * per + per, v))
+            )
+
+
+def pack_noise(n_ref, out_ref, work, *, groups, per):
+    for b in range(groups * per):
         for m in range(MEM):
             for l in range(LAYERS):
                 for g in range(ROWS // SUB):
-                    value = n_ref[0, m, l, g * SUB : (g + 1) * SUB, b * BW : (b + 1) * BW]
-                    s = l * HALF + b * MEM + m
-                    work[pl.ds(g * SUB * FULL + s, SUB, stride=FULL), :] = value
-                    wide[pl.ds(g * SUB * 2 * FULL + s, SUB, stride=2 * FULL), :] = value
-    for r in range(ROWS):
-        wide[(2 * r + 1) * FULL : (2 * r + 2) * FULL, :] = jnp.zeros((FULL, BW), F32)
-    for d in range(groups):
-        for m in range(MEM):
-            def take(v):
-                before = (d * per - 1) % blocks * MEM + m
-                after = (d * per + per) % blocks * MEM + m
-                return tuple(
-                    wide[pl.ds(v * 4 * FULL + s, SUB, stride=HALF), :] for s in (before, after)
-                )
-
-            for c in range(per):
-                for v in range(4):
-                    s = v * 4 * FULL + (d * per + c) * MEM + m
-                    out_ref[d, m, c * 4 + v] = work[pl.ds(s, SUB, stride=HALF), :]
-            out_ref[d, m, per * 4] = halo_pack(take)
+                    s = g * SUB * FULL + l * HALF + b * MEM + m
+                    work[pl.ds(s, SUB, stride=FULL), :] = n_ref[
+                        0, m, l, g * SUB : (g + 1) * SUB, b * BW : (b + 1) * BW
+                    ]
+    send_rows(work, 0, out_ref, groups, per)
 
 
 def place(natural, slot, dst, plane, body, left, right):
@@ -195,7 +196,7 @@
                         plane, j * SUB : (j + 1) * SUB, :
                     ]
                 parts.append(natural[slot, SUB : SUB + HALF, :])
-            s = pl.multiple_of((r * 2 + f) * FULL, FULL)
+            s = pl.multiple_of((f * ROWS + r) * FULL, FULL)
             turned[pl.ds(s, FULL), :] = to_layers(*parts).T
         return 0
 
@@ -203,7 +204,8 @@
 
 
 def advance_members(
-    edge, q_main, p_main, q_up, p_up, q_down, p_down, out_ref, first, second, natural, turned, *, groups, per
+    edge, q_main, p_main, q_up, p_up, q_down, p_down, q_out, p_out,
+    first, second, natural, turned, *, groups, per
 ):
     def fill(refs, count, start):
         def body(r, _):
@@ -223,124 +225,115 @@
     fill((q_down, p_down), STEPS, STEPS + ROWS)
     src = run_steps(edge, first, second)
     turn_back(src, natural, turned)
-    for m in range(MEM):
-        for d in range(groups):
-            for c in range(per):
-                for v in range(8):
-                    s = v * 4 * FULL + (d * per + c) * MEM + m
-                    out_ref[d, m, c * 8 + v] = turned[pl.ds(s, SUB, stride=HALF), :]
-        for d in range(groups):
-            def take(v):
-                return out_ref[(d - 1) % groups, m, per * 8 - 8 + v], out_ref[(d + 1) % groups, m, v]
-
-            out_ref[d, m, per * 8] = halo_pack(take)
-
-
-def resample(
-    parent, x_ref, n_ref, main_ref, edge_ref, up_ref, down_ref, z_ref, work, noise, *, members, per
-):
+    send_rows(turned, 0, q_out, groups, per)
+    send_rows(turned, ROWS * FULL, p_out, groups, per)
+
+
+def resample(parent, x_ref, *refs, members, per, noisy):
+    main_ref, edge_ref, up_ref, down_ref = refs[noisy : noisy + 4]
+    work = refs[-1]
+
     def one(k, _):
         p = parent[k]
+        beside = x_ref[p, per * 32 :, :]
         for c in range(per):
-            for v in range(8):
-                s = v * 4 * FULL + c * members + k
-                work[pl.ds(s, SUB, stride=HALF), :] = x_ref[p, (c * 8 + v) * SUB : (c * 8 + v + 1) * SUB, :]
-            for v in range(4):
-                s = v * 4 * FULL + c * members + k
-                noise[pl.ds(s, SUB, stride=HALF), :] = n_ref[k, c * 4 + v]
-            for g in range(2):
-                s = c * 64 + g * 32 + 2
-                z_ref[c, pl.ds(g * SUB * members + k, SUB, stride=members), :] = x_ref[
-                    k, pl.ds(s, SUB, stride=4), :
-                ]
-        edge_ref[pl.ds(k, SUB, stride=members), :] = x_ref[p, per * 64 :, :] + n_ref[k, per * 4]
+            for v in range(QUAD):
+                value = x_ref[p, (c * QUAD + v) * SUB : (c * QUAD + v + 1) * SUB, :]
+                if noisy:
+                    value = value + refs[0][k, (c * QUAD + v) * SUB : (c * QUAD + v + 1) * SUB, :]
+                work[pl.ds(v * 4 * FULL + c * members + k, SUB, stride=HALF), :] = value
+            if not noisy:
+                for g in range(2):
+                    refs[-2][c, pl.ds(g * SUB * members + k, SUB, stride=members), :] = x_ref[
+                        k, pl.ds(c * 32 + g * 16, SUB, stride=2), :
+                    ]
+        if noisy:
+            beside = beside + refs[0][k, per * 32 :, :]
+        edge_ref[pl.ds(k, SUB, stride=members), :] = beside
         return 0
 
     lax.fori_loop(0, members, one, 0)
     for r in range(ROWS):
-        for f in range(2):
-            value = work[(r * 2 + f) * FULL : (r * 2 + f + 1) * FULL, :]
-            if f == 0:
-                value = value + noise[r * FULL : (r + 1) * FULL, :]
-            for l, part in enumerate(by_layer(value.T)):
-                s = ((r * 2 + l) * 2 + f) * HALF
-                main_ref[s : s + HALF, :] = part
-                if r < STEPS:
-                    down_ref[s : s + HALF, :] = part
-                if r >= ROWS - STEPS:
-                    s -= (ROWS - STEPS) * 4 * HALF
-                    up_ref[s : s + HALF, :] = part
-    count = 4 * members
+        for l, part in enumerate(by_layer(work[r * FULL : (r + 1) * FULL, :].T)):
+            s = (r * 2 + l) * HALF
+            main_ref[s : s + HALF, :] = part
+            if r < STEPS:
+                down_ref[s : s + HALF, :] = part
+            if r >= ROWS - STEPS:
+                s -= (ROWS - STEPS) * 2 * HALF
+                up_ref[s : s + HALF, :] = part
+    count = 2 * members
     segment = ((lax.broadcasted_iota(jnp.int32, (count, BW), 1) + SEG // 2) // SEG) % SUB
-    even, odd = edge_ref[:count, :], wide_roll(edge_ref[count:, :], HALF)
-    top = STEPS * 4 * HALF
-    up_ref[top:, :] = jnp.where(segment >= 5, even, odd)
-    down_ref[top:, :] = jnp.where(segment <= 2, even, odd)
+    for ref, start in ((up_ref, ROWS - STEPS), (down_ref, 0)):
+        sides = None
+        for i in range(STEPS):
+            v, q = divmod(start + i, 4)
+            rows = wide_roll(edge_ref[q * count : (q + 1) * count, :], SEG * (i - v))
+            sides = rows if sides is None else jnp.where(segment == i, rows, sides)
+        ref[STEPS * 2 * HALF :, :] = sides
 
 
 def advance_columns(
-    edge, parent, main_ref, edge_ref, up_ref, down_ref, out_ref, z_ref,
+    edge, parent, q_main, p_main, q_edge, p_edge, q_up, p_up, q_down, p_down, out_ref, z_ref,
     first, second, natural, turned, sides, *, members, per
 ):
-    top = STEPS * 4 * HALF
-    count = 8 * members // BW
-    for i in range(count):
-        sides[i] = edge_ref[i * BW : (i + 1) * BW, :].T
-    for i in range(count // 2):
-        sides[count + i] = up_ref[top + i * BW : top + (i + 1) * BW, :].T
-        sides[count + count // 2 + i] = down_ref[top + i * BW : top + (i + 1) * BW, :].T
-
-    def put(source, at, plane, f, l, base, group):
-        value = source[pl.ds(pl.multiple_of(at, HALF), HALF), :]
-        index = base * BW + (f * 2 + l) * members
-        matrix, offset = index // BW, index % BW
+    top = STEPS * 2 * HALF
+    own = 8 * members // BW
+    beside = own // 2
+    for f, ref in enumerate((q_edge, p_edge)):
+        for i in range(own):
+            sides[f * own + i] = ref[i * BW : (i + 1) * BW, :].T
+    for n, refs in enumerate(((q_up, p_up), (q_down, p_down))):
+        both = jnp.concatenate([refs[0][top:, :], refs[1][top:, :]], axis=0)
+        for i in range(beside):
+            sides[2 * own + n * beside + i] = both[i * BW : (i + 1) * BW, :].T
+
+    def put(source, r, row, f, l, base, index, group):
+        value = source[pl.ds(pl.multiple_of((r * 2 + l) * HALF, HALF), HALF), :]
+        matrix, offset = base + index * members // BW, index * members % BW
         before = pl.multiple_of((group * SEG + BW - SUB) % BW, SUB)
         after = pl.multiple_of(group * SEG, SUB)
         ends = (
             wide_roll(sides[matrix, pl.ds(before, SUB), :], -offset),
             wide_roll(sides[matrix, pl.ds(after, SUB), :], BW - members - offset),
         )
+        plane = (row * 2 + l) * 2 + f
         place(natural, f * 2 + l, first, plane, value, *margins(value, members, *ends))
 
     def rows_own(v, _):
-        for pair in range(2):
+        for q in range(4):
+            for f, source in enumerate((q_main, p_main)):
+                for l in range(LAYERS):
+                    put(source, 4 * v + q, 4 * v + q + STEPS, f, l, f * own, q * 2 + l, v)
+        return 0
+
+    lax.fori_loop(0, QUAD, rows_own, 0)
+
+    def rows_beside(i, _):
+        for n, refs in enumerate(((q_up, p_up), (q_down, p_down))):
             for f in range(2):
                 for l in range(LAYERS):
-                    r = 2 * v + pair
-                    at = ((r * 2 + l) * 2 + f) * HALF
-                    put(main_ref, at, ((r + STEPS) * 2 + l) * 2 + f, f, l, pair * count // 2, v)
+                    row = i + n * (STEPS + ROWS)
+                    put(refs[f], i, row, f, l, 2 * own + n * beside, f * 2 + l, i)
         return 0
 
-    lax.fori_loop(0, SUB, rows_own, 0)
-
-    def rows_beside(v, _):
-        for pair in range(2):
-            for f in range(2):
-                for l in range(LAYERS):
-                    r = 2 * v + pair
-                    at = ((r * 2 + l) * 2 + f) * HALF
-                    plane = (r * 2 + l) * 2 + f
-                    put(up_ref, at, plane, f, l, count, v + 5 if pair == 0 else v + 1)
-                    plane = ((r + STEPS + ROWS) * 2 + l) * 2 + f
-                    put(down_ref, at, plane, f, l, count + count // 2, v if pair == 0 else v + 4)
-        return 0
-
-    lax.fori_loop(0, STEPS // 2, rows_beside, 0)
+    lax.fori_loop(0, STEPS, rows_beside, 0)
     src = run_steps(edge, first, second)
     turn_back(src, natural, turned)
 
     def one(k, _):
         p = parent[k]
         for c in range(per):
-            for v in range(8):
-                s = v * 4 * FULL + c * members + p
-                out_ref[k, c * 8 + v] = turned[pl.ds(s, SUB, stride=HALF), :]
+            for f in range(2):
+                for v in range(QUAD):
+                    s = f * ROWS * FULL + v * 4 * FULL + c * members + p
+                    out_ref[k, (c * 2 + f) * QUAD + v] = turned[pl.ds(s, SUB, stride=HALF), :]
         return 0
 
     lax.fori_loop(0, members, one, 0)
     for c in range(per):
         for r in range(ROWS):
-            s = (2 * r + 1) * FULL + c * members
+            s = (ROWS + r) * FULL + c * members
             z_ref[c, r * members : (r + 1) * members, :] = turned[s : s + members, :]
 
 
@@ -351,9 +344,9 @@
             for l in range(LAYERS):
                 for g in range(ROWS // SUB):
                     rows, cols = slice(g * SUB, (g + 1) * SUB), slice(b * BW, (b + 1) * BW)
-                    s = c * 64 + g * 32 + l
-                    q_ref[0, l, rows, cols] = y_ref[d, 0, pl.ds(s, SUB, stride=4), :]
-                    p_ref[0, l, rows, cols] = y_ref[d, 0, pl.ds(s + 2, SUB, stride=4), :]
+                    s = c * 64 + g * 16 + l
+                    q_ref[0, l, rows, cols] = y_ref[d, 0, pl.ds(s, SUB, stride=2), :]
+                    p_ref[0, l, rows, cols] = y_ref[d, 0, pl.ds(s + 32, SUB, stride=2), :]
 
 
 def score(rows_ref, z_ref, f_ref, o_ref, w_ref, out_ref, patch, total, *, members, per, chunk):
@@ -391,12 +384,19 @@
         )
 
 
+CHEAP = pl.CostEstimate(flops=1000, transcendentals=0, bytes_accessed=1000)
+
+
 def shape(*dims):
     return jax.ShapeDtypeStruct(dims, F32)
 
 
-def call(kernel, outs, scratch=(), scalars=0, name=None):
+def call(kernel, outs, scratch=(), scalars=0, resident=9, name=None):
     def run(*args):
+        args = args[:scalars] + tuple(
+            pltpu.with_memory_space_constraint(x, pltpu.VMEM) if i < resident else x
+            for i, x in enumerate(args[scalars:])
+        )
         specs = [pl.BlockSpec(memory_space=pltpu.SMEM)] * scalars
         specs += [pl.BlockSpec(memory_space=pltpu.VMEM)] * (len(args) - scalars)
         return pl.pallas_call(
@@ -406,6 +406,7 @@
             out_specs=[pl.BlockSpec(memory_space=pltpu.VMEM)] * len(outs),
             scratch_shapes=list(scratch),
             compiler_params=pltpu.CompilerParams(vmem_limit_bytes=VMEM_LIMIT),
+            cost_estimate=CHEAP,
             name=name,
         )(*args)
 
@@ -447,6 +448,7 @@
             out_shape=[shape(ROWS * FULL, BW), shape(STEPS * FULL, BW), shape(STEPS * FULL, BW)],
             scratch_shapes=[pltpu.VMEM((SUB * FULL, BW), F32)],
             compiler_params=params,
+            cost_estimate=CHEAP,
             name="pack_q" if noise else "pack_psi",
         )(field, *noise)
 
@@ -465,13 +467,14 @@
         in_specs=[pl.BlockSpec((1, MEM, LAYERS, ROWS, width), lambda i: (1, 0, 0, 0, 0))],
         out_specs=pl.BlockSpec((groups, MEM, per * 4 + 1, SUB, BW), lambda i: (0, 0, 0, 0, 0)),
         out_shape=shape(groups, MEM, per * 4 + 1, SUB, BW),
-        scratch_shapes=[pltpu.VMEM((ROWS * FULL, BW), F32), pltpu.VMEM((2 * ROWS * FULL, BW), F32)],
+        scratch_shapes=[pltpu.VMEM((ROWS * FULL, BW), F32)],
         compiler_params=params,
+        cost_estimate=CHEAP,
         name="pack_noise",
     )(later_noise)
     noise, q_below, q_above = lax.optimization_barrier((noise, q_below, q_above))
     noise = lax.all_to_all(noise, "dom", split_axis=0, concat_axis=0, tiled=True)
-    noise = noise.reshape(members, per * 4 + 1, SUB, BW)
+    noise = noise.reshape(members, (per * 4 + 1) * SUB, BW)
 
     work = [
         pltpu.VMEM((DEEP * 4, PARTS * SUB, BW), F32),
@@ -479,32 +482,40 @@
         pltpu.VMEM((4, PARTS * SUB, BW), F32),
         pltpu.VMEM((2 * ROWS * FULL, BW), F32),
     ]
-    (sent,) = call(
+    q_sent, p_sent = call(
         functools.partial(advance_members, groups=groups, per=per),
-        [shape(groups, MEM, per * 8 + 1, SUB, BW)],
+        [shape(groups, MEM, per * 4 + 1, SUB, BW)] * 2,
         work,
         scalars=1,
+        resident=2,
         name="advance_members",
     )(edge, q_main, p_main, q_below, p_below, q_above, p_above)
-    owned = lax.all_to_all(sent, "dom", split_axis=0, concat_axis=0, tiled=True)
-    owned = owned.reshape(members, (per * 8 + 1) * SUB, BW)
-
-    beside = STEPS * 4 * HALF + 4 * members
-    main, sides, to_up, to_down, surface = call(
-        functools.partial(resample, members=members, per=per),
-        [
-            shape(ROWS * 4 * HALF, BW),
-            shape(8 * members, BW),
-            shape(beside, BW),
-            shape(beside, BW),
-            shape(per, ROWS * members, BW),
-        ],
-        [pltpu.VMEM((2 * ROWS * FULL, BW), F32), pltpu.VMEM((ROWS * FULL, BW), F32)],
-        scalars=1,
-        name="resample",
-    )(parent[0], owned, noise)
-    from_below = lax.ppermute(to_up, "tile", up)
-    from_above = lax.ppermute(to_down, "tile", down)
+    beside = STEPS * 2 * HALF + 2 * members
+    pieces = [shape(ROWS * 2 * HALF, BW), shape(8 * members, BW), shape(beside, BW), shape(beside, BW)]
+
+    def spread(sent):
+        owned = lax.all_to_all(sent, "dom", split_axis=0, concat_axis=0, tiled=True)
+        return owned.reshape(members, (per * 4 + 1) * SUB, BW)
+
+    def exchange(owned, noise=()):
+        extra = [] if noise else [shape(per, ROWS * members, BW)]
+        main, edges, to_up, to_down, *surface = call(
+            functools.partial(resample, members=members, per=per, noisy=len(noise)),
+            pieces + extra,
+            [pltpu.VMEM((ROWS * FULL, BW), F32)],
+            scalars=1,
+            name="resample_q" if noise else "resample_psi",
+        )(parent[0], owned, *noise)
+        below = lax.ppermute(to_up, "tile", up)
+        above = lax.ppermute(to_down, "tile", down)
+        return main, edges, below, above, *surface
+
+    p_sent, noise = lax.optimization_barrier((p_sent, noise))
+    p_owned = spread(p_sent)
+    q_sent, p_owned = lax.optimization_barrier((q_sent, p_owned))
+    q_owned = spread(q_sent)
+    p_main, p_edge, p_below, p_above, surface = exchange(p_owned)
+    q_main, q_edge, q_below, q_above = exchange(q_owned, (noise,))
 
     def likelihood(surface):
         chunk = observations
@@ -526,12 +537,13 @@
                 pltpu.VMEM((members, chunk), F32),
             ],
             compiler_params=params,
+            cost_estimate=CHEAP,
             name="score",
         )(block_rows, surface, footprint, observed.reshape(obs), precision.reshape(obs))
         return out[:1]
 
     logs = [likelihood(surface)]
-    main, logs[0] = lax.optimization_barrier((main, logs[0]))
+    p_main, logs[0] = lax.optimization_barrier((p_main, logs[0]))
 
     back, surface = call(
         functools.partial(advance_columns, members=members, per=per),
@@ -539,7 +551,7 @@
         work + [pltpu.VMEM((members // SUB * 2, BW, BW), F32)],
         scalars=2,
         name="advance_columns",
-    )(edge, parent[1], main, sides, from_below, from_above)
+    )(edge, parent[1], q_main, p_main, q_edge, p_edge, q_below, p_below, q_above, p_above)
     back = back.reshape(groups, MEM, per * 64, BW)
     mine = lax.all_to_all(back, "dom", split_axis=0, concat_axis=0, tiled=True)
     logs.append(likelihood(surface))
@@ -551,6 +563,7 @@
         out_specs=[pl.BlockSpec((1, LAYERS, ROWS, width), lambda i: (i, 0, 0, 0))] * 2,
         out_shape=[shape(MEM, LAYERS, ROWS, width)] * 2,
         compiler_params=params,
+        cost_estimate=CHEAP,
         name="unpack_state",
     )(mine)
 

time: 179 us -> 171 us (0.955)
  waiting for transfers between devices: 49.5 us -> 20.7 us
  blocking collectives: 0 us -> 21 us
  starting transfers between devices: 38.4 us -> 44.2 us
  Pallas kernels: 79.6 us -> 75.7 us
  local copies, waits for them, and re-layouts: 7.84 us -> 5.31 us
    all_to_all x1, waiting for transfers between devices: 27.2 us -> 5.73 us  [spread(): owned = lax.all_to_all(sent, 'dom', split_axis=0, concat_axis=0, tiled=True)]
    all_to_all x0 -> x1, blocking collectives: none -> 21 us  [spread(): owned = lax.all_to_all(sent, 'dom', split_axis=0, concat_axis=0, tiled=True)]
    ppermute x2 -> x4, waiting for transfers between devices: 6.75 us -> 0.01 us  [the longest x2 0.01 us: exchange(): above = lax.ppermute(to_down, 'tile', down)]
    ppermute x2 -> x4, starting transfers between devices: 5.55 us -> 11.1 us  [the longest x2 8.47 us: exchange(): below = lax.ppermute(to_up, 'tile', up)]
    unnamed x24 -> x26, local copies, waits for them, and re-layouts: 4.72 us -> 2.14 us
    pallas_call x1, Pallas kernels: 5.94 us -> 3.8 us  [shards(): pl.pallas_call(functools.partial(pack_noise, groups=groups, per=per), gri...]
    ppermute x5, waiting for transfers between devices: 10.8 us -> 8.64 us  [shards(): loglik = loglik + lax.ppermute(loglik, axis, pairs)]
    pallas_call x3 -> x4, Pallas kernels: 43.1 us -> 41.1 us  [run(): pl.pallas_call(kernel, out_shape=outs, in_specs=specs, out_specs=[pl.Bloc...]
  transfers between devices with their start and end apart: 14 -> 16, of which waited for: 10 -> 9; matrix products, arithmetic and copies ran while one was open for 3% -> 3% of each run, Pallas kernels for 26% -> 31%
where the time goes in v3:
time: 171 us; the launch traced here: 170 us
  Pallas kernels  75.7 us (44%)
  starting transfers between devices  44.2 us (26%)
  blocking collectives  21 us (12%)
  waiting for transfers between devices  20.7 us (12%)
  local copies, waits for them, and re-layouts  5.31 us (3%)
  other arithmetic  1.9 us (1%)
    pallas_call x4, Pallas kernels, run(): pl.pallas_call(kernel, out_shape=outs, in_specs=specs, out_specs=[pl.Bloc...  41.1 us
    all_to_all x1, blocking collectives, spread(): owned = lax.all_to_all(sent, 'dom', split_axis=0, concat_axis=0, tiled=True)  21 us
    pallas_call x2, Pallas kernels, likelihood(): pl.pallas_call(functools.partial(score, members=members, per=per, chunk=c...  19.7 us
    ppermute x5, starting transfers between devices, shards(): loglik = loglik + lax.ppermute(loglik, axis, pairs)  10.1 us
    ppermute x5, waiting for transfers between devices, shards(): loglik = loglik + lax.ppermute(loglik, axis, pairs)  8.64 us
    ppermute x2, starting transfers between devices, exchange(): below = lax.ppermute(to_up, 'tile', up)  8.47 us
    pallas_call x2, Pallas kernels, pack(): pl.pallas_call(functools.partial(pack_field, blocks=blocks, noisy=bool(no...  7.26 us
    all_to_all x1, waiting for transfers between devices, spread(): owned = lax.all_to_all(sent, 'dom', split_axis=0, concat_axis=0, tiled=True)  5.73 us
  transfers between devices with their start and end apart: 16, of which 9 were waited for; matrix products, arithmetic and copies ran while one was open for 3% of the time, Pallas kernels for 31%

profile of v3, /device:TPU:0, one launch (start us, length us, event | category | flops | bytes accessed | tf_op | source)
XLA Modules:
  0.0 169.6 jit_solution(5736016907476832017)
XLA Ops:
  0.6 3.5 %pack_psi.1 = (f32[2048,128]{1,0:T(8,128)}, f32[768,128]{1,0:T(8,128)}, f32[768,128]{1,0:T(8,128)}) custom-call(f32[4,2,16,2048]{3,2,1,0:T(8,128)} %refs_0_.1), custom_call_target="tpu_custom_call" | custom-call | flops 1000 | bytes 1000 | tf_op jit(solution)/shard_map/pack_psi/pallas_call | solution.py:438
  4.2 4.9 %collective-permute-start = (f32[768,128]{1,0:T(8,128)}, f32[768,128]{1,0:T(8,128)S(1)}, u32[]{:S(2)}, u32[]{:S(2)}) collective-permute-start(f32[768,128]{1,0:T(8,128)} %get-tuple-element.45), channel_id=1, source_target_pairs={{0,1},{1,2},{2,3},{4,5},{5,6},{6,7},{8,9},{9,10},{10,11},{12,13},{... | collective-permute-start | bytes 1179656 | tf_op jit(solution)/shard_map/ppermute | solution.py:457
  10.4 3.7 %pack_q.1 = (f32[2048,128]{1,0:T(8,128)}, f32[768,128]{1,0:T(8,128)}, f32[768,128]{1,0:T(8,128)}) custom-call(f32[4,2,16,2048]{3,2,1,0:T(8,128)} %refs_0_.2, f32[2,4,2,16,2048]{4,3,2,1,0:T(8,128)} %n_ref), custom_call_target="tpu_custom_call" | custom-call | flops 1000 | bytes 1000 | tf_op jit(solution)/shard_map/pack_q/pallas_call | solution.py:438
  14.1 4.6 %collective-permute-start.2 = (f32[768,128]{1,0:T(8,128)}, f32[768,128]{1,0:T(8,128)S(1)}, u32[]{:S(2)}, u32[]{:S(2)}) collective-permute-start(f32[768,128]{1,0:T(8,128)} %get-tuple-element.48), channel_id=1, source_target_pairs={{0,1},{1,2},{2,3},{4,5},{5,6},{6,7},{8,9},{9,10},{10,11},{12,13},{... | collective-permute-start | bytes 1179656 | tf_op jit(solution)/shard_map/ppermute | solution.py:460
  21.8 3.8 %pack_noise.1 = f32[8,4,9,8,128]{4,3,2,1,0:T(8,128)} custom-call(f32[2,4,2,16,2048]{4,3,2,1,0:T(8,128)} %n_ref), custom_call_target="tpu_custom_call" | custom-call | flops 1000 | bytes 1000 | tf_op jit(solution)/shard_map/pack_noise/pallas_call | solution.py:464
  27.5 3.4 %collective-permute-done.3.q_down = f32[768,128]{1,0:T(8,128)} collective-permute-done((f32[768,128]{1,0:T(8,128)}, f32[768,128]{1,0:T(8,128)}, u32[]{:S(2)}, u32[]{:S(2)}) %collective-permute-start.3) | collective-permute-done | bytes 393248 | tf_op jit(solution)/shard_map/ppermute | solution.py:461
  30.9 3.7 %all-to-all-start = ((f32[8,4,9,8,128]{4,3,2,1,0:T(8,128)}), f32[8,4,9,8,128]{4,3,2,1,0:T(8,128)S(1)}, u32[]{:S(2)}, u32[]{:S(2)}) async-start(f32[8,4,9,8,128]{4,3,2,1,0:T(8,128)} %pack_noise.1), calls=%async_computation | async-start | bytes 2359296 | tf_op jit(solution)/shard_map/all_to_all | solution.py:476
  35.2 16.9 %advance_members.1 = (f32[8,4,9,8,128]{4,3,2,1,0:T(8,128)}, f32[8,4,9,8,128]{4,3,2,1,0:T(8,128)}) custom-call(s32[2]{0:T(128)} %pad_add_fusion.edge, f32[2048,128]{1,0:T(8,128)S(1)} %copy-done.3, f32[2048,128]{1,0:T(8,128)S(1)} %copy-done.2, f32[768,128]{1,0:T(8,128)} %copy-done.9, f32[768,128]{1,0:T(8,128)} %copy-done.7, ...), custom_call_target="tpu_custom_call" | custom-call | flops 1000 | bytes 1000 | tf_op jit(solution)/shard_map/advance_members/pallas_call | solution.py:402
  52.2 21.0 %all_to_all.20 = f32[8,4,9,8,128]{4,3,2,1,0:T(8,128)S(1)} all-to-all(f32[8,4,9,8,128]{4,3,2,1,0:T(8,128)} %get-tuple-element.57), channel_id=1, replica_groups=mesh['dom'=8,'tile'=4] {'dom'}, dimensions={0} | all-to-all | bytes 2359296 | tf_op jit(solution)/shard_map/all_to_all | solution.py:497
  73.1 3.7 %all-to-all-start.2 = ((f32[8,4,9,8,128]{4,3,2,1,0:T(8,128)}), f32[8,4,9,8,128]{4,3,2,1,0:T(8,128)S(1)}, u32[]{:S(2)}, u32[]{:S(2)}) async-start(f32[8,4,9,8,128]{4,3,2,1,0:T(8,128)} %get-tuple-element.58), calls=%async_computation.2 | async-start | bytes 2359296 | tf_op jit(solution)/shard_map/all_to_all | solution.py:497
  77.7 4.5 %resample_psi.1 = (f32[2048,128]{1,0:T(8,128)}, f32[256,128]{1,0:T(8,128)}, f32[832,128]{1,0:T(8,128)}, f32[832,128]{1,0:T(8,128)}, f32[2,512,128]{2,1,0:T(8,128)}) custom-call(s32[32]{0:T(128)} %get-tuple-element.80.parent, f32[32,72,128]{2,1,0:T(8,128)S(1)} %bitcast.11), custom_call_target="tpu_custom_call" | custom-call | flops 1000 | bytes 1000 | tf_op jit(solution)/shard_map/resample_psi/pallas_call | solution.py:402
  82.3 4.2 %collective-permute-start.5 = (f32[832,128]{1,0:T(8,128)}, f32[832,128]{1,0:T(8,128)S(1)}, u32[]{:S(2)}, u32[]{:S(2)}) collective-permute-start(f32[832,128]{1,0:T(8,128)} %get-tuple-element.68), channel_id=1, source_target_pairs={{0,1},{1,2},{2,3},{4,5},{5,6},{6,7},{8,9},{9,10},{10,11},{12,13},{... | collective-permute-start | bytes 1277960 | tf_op jit(solution)/shard_map/ppermute | solution.py:509
  87.8 5.7 %all-to-all-done.2 = f32[8,4,9,8,128]{4,3,2,1,0:T(8,128)S(1)} async-done(((f32[8,4,9,8,128]{4,3,2,1,0:T(8,128)}), f32[8,4,9,8,128]{4,3,2,1,0:T(8,128)S(1)}, u32[]{:S(2)}, u32[]{:S(2)}) %all-to-all-start.2) | async-done | bytes 1179680 | tf_op jit(solution)/shard_map/all_to_all | solution.py:497
  93.6 4.0 %resample_q.1 = (f32[2048,128]{1,0:T(8,128)}, f32[256,128]{1,0:T(8,128)}, f32[832,128]{1,0:T(8,128)}, f32[832,128]{1,0:T(8,128)}) custom-call(s32[32]{0:T(128)} %get-tuple-element.80.parent, f32[32,72,128]{2,1,0:T(8,128)S(1)} %bitcast.10, f32[32,72,128]{2,1,0:T(8,128)S(1)} %bitcast.9), custom_call_target="tpu_custom_call" | custom-call | flops 1000 | bytes 1000 | tf_op jit(solution)/shard_map/resample_q/pallas_call | solution.py:402
  97.6 4.2 %collective-permute-start.4 = (f32[832,128]{1,0:T(8,128)}, f32[832,128]{1,0:T(8,128)S(1)}, u32[]{:S(2)}, u32[]{:S(2)}) collective-permute-start(f32[832,128]{1,0:T(8,128)} %get-tuple-element.67), channel_id=1, source_target_pairs={{0,1},{1,2},{2,3},{4,5},{5,6},{6,7},{8,9},{9,10},{10,11},{12,13},{... | collective-permute-start | bytes 1277960 | tf_op jit(solution)/shard_map/ppermute | solution.py:509
  104.4 9.9 %score.2 = f32[8,32]{1,0:T(8,128)} custom-call(s32[2,2]{1,0:T(2,128)} %rows_ref.3, f32[2,512,128]{2,1,0:T(8,128)} %get-tuple-element.63.z_ref, f32[2,2,1024,1024]{3,2,1,0:T(8,128)} %f_ref.3, f32[2,2,1,1024]{3,2,1,0:T(1,128)} %reshape.36.o_ref, f32[2,2,1,1024]{3,2,1,0:T(1,128)} %reshape.37.w_ref), custom_call_target="tpu_custom_call" | custom-call | flops 1000 | bytes 1000 | tf_op jit(solution)/shard_map/score/pallas_call | solution.py:523
  115.1 15.6 %advance_columns.1 = (f32[32,16,8,128]{3,2,1,0:T(8,128)}, f32[2,512,128]{2,1,0:T(8,128)}) custom-call(s32[2]{0:T(128)} %pad_add_fusion.edge, s32[32]{0:T(128)} %get-tuple-element.81.parent, f32[2048,128]{1,0:T(8,128)S(1)} %copy-done.1, f32[2048,128]{1,0:T(8,128)S(1)} %copy-done, f32[256,128]{1,0:T(8,128)S(1)} %copy-done.5, f32[256,128]{1,0:T(8,128)S(1)} %copy-done.4, ...), custom_call_target="tpu_custom_call" | custom-call | flops 1000 | bytes 1000 | tf_op jit(solution)/shard_map/advance_columns/pallas_call | solution.py:402
  130.7 3.6 %all-to-all-start.3 = ((f32[8,4,128,128]{3,2,1,0:T(8,128)}), f32[8,4,128,128]{3,2,1,0:T(8,128)S(1)}, u32[]{:S(2)}, u32[]{:S(2)}) async-start(f32[8,4,128,128]{3,2,1,0:T(8,128)} %bitcast.12), calls=%async_computation.3 | async-start | bytes 4194304 | tf_op jit(solution)/shard_map/all_to_all | solution.py:556
  134.3 9.8 %score.3 = f32[8,32]{1,0:T(8,128)} custom-call(s32[2,2]{1,0:T(2,128)} %rows_ref.3, f32[2,512,128]{2,1,0:T(8,128)} %get-tuple-element.75.z_ref, f32[2,2,1024,1024]{3,2,1,0:T(8,128)} %f_ref.3, f32[2,2,1,1024]{3,2,1,0:T(1,128)} %reshape.36.o_ref, f32[2,2,1,1024]{3,2,1,0:T(1,128)} %reshape.37.w_ref), custom_call_target="tpu_custom_call" | custom-call | flops 1000 | bytes 1000 | tf_op jit(solution)/shard_map/score/pallas_call | solution.py:523
  144.8 3.5 %collective-permute-start.8 = (f32[2,32]{1,0:T(2,128)S(1)}, f32[2,32]{1,0:T(2,128)S(1)}, u32[]{:S(2)}, u32[]{:S(2)}) collective-permute-start(f32[2,32]{1,0:T(2,128)S(1)} %pad_maximum_fusion), channel_id=1, source_target_pairs={{0,1},{1,0},{2,3},{3,2},{4,5},{5,4},{6,7},{7,6},{8,9},{9,8},{10,11... | collective-permute-start | bytes 776 | tf_op jit(solution)/shard_map/ppermute | solution.py:575
  149.8 3.1 %collective-permute-start.9 = (f32[2,32]{1,0:T(2,128)S(1)}, f32[2,32]{1,0:T(2,128)S(1)}, u32[]{:S(2)}, u32[]{:S(2)}) collective-permute-start(f32[2,32]{1,0:T(2,128)S(1)} %fusion.2), channel_id=1, source_target_pairs={{0,2},{1,3},{2,0},{3,1},{4,6},{5,7},{6,4},{7,5},{8,10},{9,11},{10,... | collective-permute-start | bytes 776 | tf_op jit(solution)/shard_map/ppermute | solution.py:575
  157.6 2.4 %collective-permute-done.11 = f32[2,32]{1,0:T(2,128)S(1)} collective-permute-done((f32[2,32]{1,0:T(2,128)S(1)}, f32[2,32]{1,0:T(2,128)S(1)}, u32[]{:S(2)}, u32[]{:S(2)}) %collective-permute-start.11) | collective-permute-done | bytes 288 | tf_op jit(solution)/shard_map/ppermute | solution.py:575
  161.4 2.1 %collective-permute-done.12 = f32[2,32]{1,0:T(2,128)S(1)} collective-permute-done((f32[2,32]{1,0:T(2,128)S(1)}, f32[2,32]{1,0:T(2,128)S(1)}, u32[]{:S(2)}, u32[]{:S(2)}) %collective-permute-start.12) | collective-permute-done | bytes 288 | tf_op jit(solution)/shard_map/ppermute | solution.py:575
  165.8 3.8 %unpack_state.1 = (f32[4,2,16,2048]{3,2,1,0:T(8,128)}, f32[4,2,16,2048]{3,2,1,0:T(8,128)}) custom-call(f32[8,4,128,128]{3,2,1,0:T(8,128)} %copy-done.6), custom_call_target="tpu_custom_call" | custom-call | flops 1000 | bytes 1000 | tf_op jit(solution)/shard_map/unpack_state/pallas_call | solution.py:559
  (62 shorter events, 23.0 us)
Async XLA Ops:
  4.2 15.8 %collective-permute-start = (f32[768,128]{1,0:T(8,128)}, f32[768,128]{1,0:T(8,128)S(1)}, u32[]{:S(2)}, u32[]{:S(2)}) collective-permute-start(f32[768,128]{1,0:T(8,128)} %get-tuple-element.45), channel_id=1, source_target_pairs={{0,1},{1,2},{2,3},{4,5},{5,6},{6,7},{8,9},{9,10},{10,11},{12,13},{... | collective-permute-start | bytes 1179656 | tf_op jit(solution)/shard_map/ppermute | solution.py:457
  9.1 12.7 %collective-permute-start.1 = (f32[768,128]{1,0:T(8,128)}, f32[768,128]{1,0:T(8,128)S(1)}, u32[]{:S(2)}, u32[]{:S(2)}) collective-permute-start(f32[768,128]{1,0:T(8,128)} %get-tuple-element.46), channel_id=1, source_target_pairs={{1,0},{2,1},{3,2},{5,4},{6,5},{7,6},{9,8},{10,9},{11,10},{13,12},{... | collective-permute-start | bytes 1179656 | tf_op jit(solution)/shard_map/ppermute | solution.py:458
  14.1 12.7 %collective-permute-start.2 = (f32[768,128]{1,0:T(8,128)}, f32[768,128]{1,0:T(8,128)S(1)}, u32[]{:S(2)}, u32[]{:S(2)}) collective-permute-start(f32[768,128]{1,0:T(8,128)} %get-tuple-element.48), channel_id=1, source_target_pairs={{0,1},{1,2},{2,3},{4,5},{5,6},{6,7},{8,9},{9,10},{10,11},{12,13},{... | collective-permute-start | bytes 1179656 | tf_op jit(solution)/shard_map/ppermute | solution.py:460
  18.7 12.2 %collective-permute-start.3 = (f32[768,128]{1,0:T(8,128)}, f32[768,128]{1,0:T(8,128)}, u32[]{:S(2)}, u32[]{:S(2)}) collective-permute-start(f32[768,128]{1,0:T(8,128)} %get-tuple-element.49), channel_id=1, source_target_pairs={{1,0},{2,1},{3,2},{5,4},{6,5},{7,6},{9,8},{10,9},{11,10},{13,12},{... | collective-permute-start | bytes 1179656 | tf_op jit(solution)/shard_map/ppermute | solution.py:461
  25.6 9.6 %copy-start.2 = (f32[2048,128]{1,0:T(8,128)S(1)}, f32[2048,128]{1,0:T(8,128)}, u32[]{:S(2)}) copy-start(f32[2048,128]{1,0:T(8,128)} %get-tuple-element.44.p_main) | copy-start | bytes 3145732
  25.6 9.6 %copy-start.3 = (f32[2048,128]{1,0:T(8,128)S(1)}, f32[2048,128]{1,0:T(8,128)}, u32[]{:S(2)}) copy-start(f32[2048,128]{1,0:T(8,128)} %get-tuple-element.43.q_main) | copy-start | bytes 3145732
  30.9 21.2 %all-to-all-start = ((f32[8,4,9,8,128]{4,3,2,1,0:T(8,128)}), f32[8,4,9,8,128]{4,3,2,1,0:T(8,128)S(1)}, u32[]{:S(2)}, u32[]{:S(2)}) async-start(f32[8,4,9,8,128]{4,3,2,1,0:T(8,128)} %pack_noise.1), calls=%async_computation | async-start | bytes 2359296 | tf_op jit(solution)/shard_map/all_to_all | solution.py:476
  73.1 20.4 %all-to-all-start.2 = ((f32[8,4,9,8,128]{4,3,2,1,0:T(8,128)}), f32[8,4,9,8,128]{4,3,2,1,0:T(8,128)S(1)}, u32[]{:S(2)}, u32[]{:S(2)}) async-start(f32[8,4,9,8,128]{4,3,2,1,0:T(8,128)} %get-tuple-element.58), calls=%async_computation.2 | async-start | bytes 2359296 | tf_op jit(solution)/shard_map/all_to_all | solution.py:497
  82.3 32.7 %collective-permute-start.5 = (f32[832,128]{1,0:T(8,128)}, f32[832,128]{1,0:T(8,128)S(1)}, u32[]{:S(2)}, u32[]{:S(2)}) collective-permute-start(f32[832,128]{1,0:T(8,128)} %get-tuple-element.68), channel_id=1, source_target_pairs={{0,1},{1,2},{2,3},{4,5},{5,6},{6,7},{8,9},{9,10},{10,11},{12,13},{... | collective-permute-start | bytes 1277960 | tf_op jit(solution)/shard_map/ppermute | solution.py:509
  86.5 28.5 %collective-permute-start.7 = (f32[832,128]{1,0:T(8,128)}, f32[832,128]{1,0:T(8,128)S(1)}, u32[]{:S(2)}, u32[]{:S(2)}) collective-permute-start(f32[832,128]{1,0:T(8,128)} %get-tuple-element.70), channel_id=1, source_target_pairs={{1,0},{2,1},{3,2},{5,4},{6,5},{7,6},{9,8},{10,9},{11,10},{13,12},{... | collective-permute-start | bytes 1277960 | tf_op jit(solution)/shard_map/ppermute | solution.py:510
  93.6 9.6 %copy-start.10 = (f32[2,2,1024]{2,1,0:T(2,128)S(1)}, f32[2,2,1024]{2,1,0:T(2,128)}, u32[]{:S(2)}) copy-start(f32[2,2,1024]{2,1,0:T(2,128)} %param.13) | copy-start | bytes 49156
  93.6 10.2 %copy-start.11 = (f32[2,2,1024]{2,1,0:T(2,128)S(1)}, f32[2,2,1024]{2,1,0:T(2,128)}, u32[]{:S(2)}) copy-start(f32[2,2,1024]{2,1,0:T(2,128)} %param.14) | copy-start | bytes 49156
  97.6 17.4 %collective-permute-start.4 = (f32[832,128]{1,0:T(8,128)}, f32[832,128]{1,0:T(8,128)S(1)}, u32[]{:S(2)}, u32[]{:S(2)}) collective-permute-start(f32[832,128]{1,0:T(8,128)} %get-tuple-element.67), channel_id=1, source_target_pairs={{0,1},{1,2},{2,3},{4,5},{5,6},{6,7},{8,9},{9,10},{10,11},{12,13},{... | collective-permute-start | bytes 1277960 | tf_op jit(solution)/shard_map/ppermute | solution.py:509
  101.9 13.2 %collective-permute-start.6 = (f32[832,128]{1,0:T(8,128)}, f32[832,128]{1,0:T(8,128)S(1)}, u32[]{:S(2)}, u32[]{:S(2)}) collective-permute-start(f32[832,128]{1,0:T(8,128)} %get-tuple-element.69), channel_id=1, source_target_pairs={{1,0},{2,1},{3,2},{5,4},{6,5},{7,6},{9,8},{10,9},{11,10},{13,12},{... | collective-permute-start | bytes 1277960 | tf_op jit(solution)/shard_map/ppermute | solution.py:510
  104.4 10.7 %copy-start = (f32[2048,128]{1,0:T(8,128)S(1)}, f32[2048,128]{1,0:T(8,128)}, u32[]{:S(2)}) copy-start(f32[2048,128]{1,0:T(8,128)} %get-tuple-element.64.p_main) | copy-start | bytes 3145732
  104.4 10.7 %copy-start.1 = (f32[2048,128]{1,0:T(8,128)S(1)}, f32[2048,128]{1,0:T(8,128)}, u32[]{:S(2)}) copy-start(f32[2048,128]{1,0:T(8,128)} %get-tuple-element.60.q_main) | copy-start | bytes 3145732
  104.4 10.7 %copy-start.4 = (f32[256,128]{1,0:T(8,128)S(1)}, f32[256,128]{1,0:T(8,128)}, u32[]{:S(2)}) copy-start(f32[256,128]{1,0:T(8,128)} %get-tuple-element.66.p_edge) | copy-start | bytes 393220
  104.4 10.7 %copy-start.5 = (f32[256,128]{1,0:T(8,128)S(1)}, f32[256,128]{1,0:T(8,128)}, u32[]{:S(2)}) copy-start(f32[256,128]{1,0:T(8,128)} %get-tuple-element.65.q_edge) | copy-start | bytes 393220
  130.7 33.8 %all-to-all-start.3 = ((f32[8,4,128,128]{3,2,1,0:T(8,128)}), f32[8,4,128,128]{3,2,1,0:T(8,128)S(1)}, u32[]{:S(2)}, u32[]{:S(2)}) async-start(f32[8,4,128,128]{3,2,1,0:T(8,128)} %bitcast.12), calls=%async_computation.3 | async-start | bytes 4194304 | tf_op jit(solution)/shard_map/all_to_all | solution.py:556
  144.8 5.0 %collective-permute-start.8 = (f32[2,32]{1,0:T(2,128)S(1)}, f32[2,32]{1,0:T(2,128)S(1)}, u32[]{:S(2)}, u32[]{:S(2)}) collective-permute-start(f32[2,32]{1,0:T(2,128)S(1)} %pad_maximum_fusion), channel_id=1, source_target_pairs={{0,1},{1,0},{2,3},{3,2},{4,5},{5,4},{6,7},{7,6},{8,9},{9,8},{10,11... | collective-permute-start | bytes 776 | tf_op jit(solution)/shard_map/ppermute | solution.py:575
  149.8 4.7 %collective-permute-start.9 = (f32[2,32]{1,0:T(2,128)S(1)}, f32[2,32]{1,0:T(2,128)S(1)}, u32[]{:S(2)}, u32[]{:S(2)}) collective-permute-start(f32[2,32]{1,0:T(2,128)S(1)} %fusion.2), channel_id=1, source_target_pairs={{0,2},{1,3},{2,0},{3,1},{4,6},{5,7},{6,4},{7,5},{8,10},{9,11},{10,... | collective-permute-start | bytes 776 | tf_op jit(solution)/shard_map/ppermute | solution.py:575
  154.5 1.2 collective-permute-start.10
  155.7 4.2 %collective-permute-start.11 = (f32[2,32]{1,0:T(2,128)S(1)}, f32[2,32]{1,0:T(2,128)S(1)}, u32[]{:S(2)}, u32[]{:S(2)}) collective-permute-start(f32[2,32]{1,0:T(2,128)S(1)} %add.17), channel_id=1, source_target_pairs={{0,8},{4,12},{8,0},{12,4},{16,24},{20,28},{24,16},{28,20},{1,9},{5... | collective-permute-start | bytes 776 | tf_op jit(solution)/shard_map/ppermute | solution.py:575
  160.0 3.6 %collective-permute-start.12 = (f32[2,32]{1,0:T(2,128)S(1)}, f32[2,32]{1,0:T(2,128)S(1)}, u32[]{:S(2)}, u32[]{:S(2)}) collective-permute-start(f32[2,32]{1,0:T(2,128)S(1)} %add.18), channel_id=1, source_target_pairs={{0,16},{4,20},{8,24},{12,28},{16,0},{20,4},{24,8},{28,12},{1,17},{... | collective-permute-start | bytes 776 | tf_op jit(solution)/shard_map/ppermute | solution.py:575
  (5 other events, 15.2 us)

commit v4 on v3

--- a/solution.py
+++ b/solution.py
@@ -17,7 +17,7 @@
 SUB = 8
 SEG = 16
 F32 = jnp.float32
-VMEM_LIMIT = 56 * 1024 * 1024
+VMEM_LIMIT = 20 * 1024 * 1024
 DRAG_STEP = 0.1 * 0.2
 HALF = 64
 PARTS = 10
@@ -185,11 +185,12 @@
 
 
 def turn_back(src, natural, turned):
-    def body(r, _):
-        for f in range(2):
+    def body(pair, _):
+        for turn in range(4):
+            r, f = 2 * pair + turn // 2, turn % 2
             parts = []
             for l in range(LAYERS):
-                slot = f * 2 + l
+                slot = turn * 2 + l
                 plane = ((r + STEPS) * 2 + l) * 2 + f
                 for j in range(PARTS):
                     natural[slot, pl.ds(j, SUB, stride=PARTS), :] = src[
@@ -200,7 +201,7 @@
             turned[pl.ds(s, FULL), :] = to_layers(*parts).T
         return 0
 
-    lax.fori_loop(0, ROWS, body, 0)
+    lax.fori_loop(0, ROWS // 2, body, 0)
 
 
 def advance_members(
@@ -208,17 +209,18 @@
     first, second, natural, turned, *, groups, per
 ):
     def fill(refs, count, start):
-        def body(r, _):
-            for f in range(2):
+        def body(pair, _):
+            for turn in range(4):
+                r, f = 2 * pair + turn // 2, turn % 2
                 for l in range(LAYERS):
                     s = pl.multiple_of((r * 2 + l) * HALF, HALF)
                     value = refs[f][pl.ds(s, HALF), :]
                     ends = wide_roll(value[HALF - SUB :], MEM), wide_roll(value[:SUB], -MEM)
                     plane = ((r + start) * 2 + l) * 2 + f
-                    place(natural, f * 2 + l, first, plane, value, *margins(value, MEM, *ends))
+                    place(natural, turn * 2 + l, first, plane, value, *margins(value, MEM, *ends))
             return 0
 
-        lax.fori_loop(0, count, body, 0)
+        lax.fori_loop(0, count // 2, body, 0)
 
     fill((q_main, p_main), ROWS, STEPS)
     fill((q_up, p_up), STEPS, 0)
@@ -288,7 +290,7 @@
         for i in range(beside):
             sides[2 * own + n * beside + i] = both[i * BW : (i + 1) * BW, :].T
 
-    def put(source, r, row, f, l, base, index, group):
+    def put(source, r, row, f, l, base, index, group, turn):
         value = source[pl.ds(pl.multiple_of((r * 2 + l) * HALF, HALF), HALF), :]
         matrix, offset = base + index * members // BW, index * members % BW
         before = pl.multiple_of((group * SEG + BW - SUB) % BW, SUB)
@@ -298,13 +300,13 @@
             wide_roll(sides[matrix, pl.ds(after, SUB), :], BW - members - offset),
         )
         plane = (row * 2 + l) * 2 + f
-        place(natural, f * 2 + l, first, plane, value, *margins(value, members, *ends))
+        place(natural, turn * 4 + f * 2 + l, first, plane, value, *margins(value, members, *ends))
 
     def rows_own(v, _):
         for q in range(4):
             for f, source in enumerate((q_main, p_main)):
                 for l in range(LAYERS):
-                    put(source, 4 * v + q, 4 * v + q + STEPS, f, l, f * own, q * 2 + l, v)
+                    put(source, 4 * v + q, 4 * v + q + STEPS, f, l, f * own, q * 2 + l, v, q % 2)
         return 0
 
     lax.fori_loop(0, QUAD, rows_own, 0)
@@ -314,7 +316,7 @@
             for f in range(2):
                 for l in range(LAYERS):
                     row = i + n * (STEPS + ROWS)
-                    put(refs[f], i, row, f, l, 2 * own + n * beside, f * 2 + l, i)
+                    put(refs[f], i, row, f, l, 2 * own + n * beside, f * 2 + l, i, n)
         return 0
 
     lax.fori_loop(0, STEPS, rows_beside, 0)
@@ -341,30 +343,28 @@
     for d in range(groups):
         for c in range(per):
             b = d * per + c
-            for l in range(LAYERS):
+            for m, l in [(m, l) for m in range(MEM) for l in range(LAYERS)]:
                 for g in range(ROWS // SUB):
                     rows, cols = slice(g * SUB, (g + 1) * SUB), slice(b * BW, (b + 1) * BW)
                     s = c * 64 + g * 16 + l
-                    q_ref[0, l, rows, cols] = y_ref[d, 0, pl.ds(s, SUB, stride=2), :]
-                    p_ref[0, l, rows, cols] = y_ref[d, 0, pl.ds(s + 32, SUB, stride=2), :]
-
-
-def score(rows_ref, z_ref, f_ref, o_ref, w_ref, out_ref, patch, total, *, members, per, chunk):
-    a, c, j = pl.program_id(0), pl.program_id(1), pl.program_id(2)
-
-    @pl.when((a == 0) & (c == 0) & (j == 0))
+                    q_ref[m, l, rows, cols] = y_ref[d, m, pl.ds(s, SUB, stride=2), :]
+                    p_ref[m, l, rows, cols] = y_ref[d, m, pl.ds(s + 32, SUB, stride=2), :]
+
+
+def score(rows_ref, z_ref, f_ref, o_ref, w_ref, first_ref, out_ref, patch, total, *, members, cycle):
+    a, c = pl.program_id(0), pl.program_id(1)
+
+    @pl.when((a == 0) & (c == 0))
     def _():
         total[...] = jnp.zeros_like(total)
 
-    @pl.when(j == 0)
-    def _():
-        start = rows_ref[a, c]
-        for r in range(BR):
-            s = pl.multiple_of((start + r) * members, SUB)
-            part = z_ref[c, pl.ds(s, members), :]
-            high = part.astype(jnp.bfloat16)
-            patch[:members, r * BW : (r + 1) * BW] = high
-            patch[members:, r * BW : (r + 1) * BW] = (part - high.astype(F32)).astype(jnp.bfloat16)
+    start = rows_ref[a, c]
+    for r in range(BR):
+        s = pl.multiple_of((start + r) * members, SUB)
+        part = z_ref[c, pl.ds(s, members), :]
+        high = part.astype(jnp.bfloat16)
+        patch[:members, r * BW : (r + 1) * BW] = high
+        patch[members:, r * BW : (r + 1) * BW] = (part - high.astype(F32)).astype(jnp.bfloat16)
 
     weights = f_ref[0, 0]
     high = weights.astype(jnp.bfloat16)
@@ -373,15 +373,17 @@
     main = lax.dot_general(patch[...], high, dims, preferred_element_type=F32)
     rest = lax.dot_general(patch[:members, :], low, dims, preferred_element_type=F32)
     predicted = main[:members] + (main[members:] + rest)
-    miss = o_ref[0, 0] - predicted
-    total[...] += w_ref[0, 0] * miss * miss
-
-    @pl.when((a == pl.num_programs(0) - 1) & (c == pl.num_programs(1) - 1) & (j == pl.num_programs(2) - 1))
+    miss = o_ref[0, pl.ds(c, 1), :] - predicted
+    total[...] += w_ref[0, pl.ds(c, 1), :] * miss * miss
+
+    @pl.when((a == pl.num_programs(0) - 1) & (c == pl.num_programs(1) - 1))
     def _():
         ones = jnp.full((SUB, total.shape[1]), -0.5, F32)
-        out_ref[...] = lax.dot_general(
+        here = lax.dot_general(
             ones, total[...], dims, precision=lax.Precision.HIGHEST, preferred_element_type=F32
         )
+        mine = lax.broadcasted_iota(jnp.int32, (SUB, members), 0) == cycle
+        out_ref[...] = jnp.where(mine, here, first_ref[...])
 
 
 CHEAP = pl.CostEstimate(flops=1000, transcendentals=0, bytes_accessed=1000)
@@ -391,7 +393,7 @@
     return jax.ShapeDtypeStruct(dims, F32)
 
 
-def call(kernel, outs, scratch=(), scalars=0, resident=9, name=None):
+def call(kernel, outs, scratch=(), scalars=0, resident=10, limit=16, far=(), name=None):
     def run(*args):
         args = args[:scalars] + tuple(
             pltpu.with_memory_space_constraint(x, pltpu.VMEM) if i < resident else x
@@ -401,11 +403,11 @@
         specs += [pl.BlockSpec(memory_space=pltpu.VMEM)] * (len(args) - scalars)
         return pl.pallas_call(
             kernel,
-            out_shape=outs,
+            out_shape=[pltpu.HBM(o.shape, F32) if i in far else o for i, o in enumerate(outs)],
             in_specs=specs,
             out_specs=[pl.BlockSpec(memory_space=pltpu.VMEM)] * len(outs),
             scratch_shapes=list(scratch),
-            compiler_params=pltpu.CompilerParams(vmem_limit_bytes=VMEM_LIMIT),
+            compiler_params=pltpu.CompilerParams(vmem_limit_bytes=limit * 1024 * 1024),
             cost_estimate=CHEAP,
             name=name,
         )(*args)
@@ -479,7 +481,7 @@
     work = [
         pltpu.VMEM((DEEP * 4, PARTS * SUB, BW), F32),
         pltpu.VMEM((DEEP * 4, PARTS * SUB, BW), F32),
-        pltpu.VMEM((4, PARTS * SUB, BW), F32),
+        pltpu.VMEM((8, PARTS * SUB, BW), F32),
         pltpu.VMEM((2 * ROWS * FULL, BW), F32),
     ]
     q_sent, p_sent = call(
@@ -488,6 +490,8 @@
         work,
         scalars=1,
         resident=2,
+        limit=32,
+        far=(0, 1),
         name="advance_members",
     )(edge, q_main, p_main, q_below, p_below, q_above, p_above)
     beside = STEPS * 2 * HALF + 2 * members
@@ -504,6 +508,7 @@
             pieces + extra,
             [pltpu.VMEM((ROWS * FULL, BW), F32)],
             scalars=1,
+            far=() if noise else (0, 1, 4),
             name="resample_q" if noise else "resample_psi",
         )(parent[0], owned, *noise)
         below = lax.ppermute(to_up, "tile", up)
@@ -517,63 +522,61 @@
     p_main, p_edge, p_below, p_above, surface = exchange(p_owned)
     q_main, q_edge, q_below, q_above = exchange(q_owned, (noise,))
 
-    def likelihood(surface):
-        chunk = observations
-        obs = (bands, per, 1, observations)
-        out = pl.pallas_call(
-            functools.partial(score, members=members, per=per, chunk=chunk),
-            grid=(bands, per, observations // chunk),
+    def likelihood(cycle, surface, logs):
+        small = pl.BlockSpec((1, per, observations), lambda a, c: (a, 0, 0))
+        table = pl.BlockSpec((SUB, members), lambda a, c: (0, 0))
+        return pl.pallas_call(
+            functools.partial(score, members=members, cycle=cycle),
+            grid=(bands, per),
             in_specs=[
                 pl.BlockSpec(memory_space=pltpu.SMEM),
-                pl.BlockSpec((per, ROWS * members, BW), lambda a, c, j: (0, 0, 0)),
-                pl.BlockSpec((1, 1, chunk, cells), lambda a, c, j: (a, c, j, 0)),
-                pl.BlockSpec((1, 1, 1, chunk), lambda a, c, j: (a, c, 0, j)),
-                pl.BlockSpec((1, 1, 1, chunk), lambda a, c, j: (a, c, 0, j)),
+                pl.BlockSpec((per, ROWS * members, BW), lambda a, c: (0, 0, 0)),
+                pl.BlockSpec((1, 1, observations, cells), lambda a, c: (a, c, 0, 0)),
+                small,
+                small,
+                table,
             ],
-            out_specs=pl.BlockSpec((SUB, members), lambda a, c, j: (0, 0)),
+            out_specs=table,
             out_shape=shape(SUB, members),
             scratch_shapes=[
                 pltpu.VMEM((2 * members, cells), jnp.bfloat16),
-                pltpu.VMEM((members, chunk), F32),
+                pltpu.VMEM((members, observations), F32),
             ],
             compiler_params=params,
             cost_estimate=CHEAP,
             name="score",
-        )(block_rows, surface, footprint, observed.reshape(obs), precision.reshape(obs))
-        return out[:1]
-
-    logs = [likelihood(surface)]
-    p_main, logs[0] = lax.optimization_barrier((p_main, logs[0]))
+        )(block_rows, surface, footprint, observed, precision, logs)
+
+    logs = likelihood(0, surface, jnp.zeros((SUB, members), F32))
+    p_main, logs = lax.optimization_barrier((p_main, logs))
 
     back, surface = call(
         functools.partial(advance_columns, members=members, per=per),
         [shape(members, per * 8, SUB, BW), shape(per, ROWS * members, BW)],
         work + [pltpu.VMEM((members // SUB * 2, BW, BW), F32)],
         scalars=2,
+        limit=32,
+        far=(0,),
         name="advance_columns",
     )(edge, parent[1], q_main, p_main, q_edge, p_edge, q_below, p_below, q_above, p_above)
     back = back.reshape(groups, MEM, per * 64, BW)
     mine = lax.all_to_all(back, "dom", split_axis=0, concat_axis=0, tiled=True)
-    logs.append(likelihood(surface))
-
-    q_out, psi_out = pl.pallas_call(
+    loglik = likelihood(1, surface, logs)
+
+    q_out, psi_out = call(
         functools.partial(unpack_state, groups=groups, per=per),
-        grid=(MEM,),
-        in_specs=[pl.BlockSpec((groups, 1, per * 64, BW), lambda i: (0, i, 0, 0))],
-        out_specs=[pl.BlockSpec((1, LAYERS, ROWS, width), lambda i: (i, 0, 0, 0))] * 2,
-        out_shape=[shape(MEM, LAYERS, ROWS, width)] * 2,
-        compiler_params=params,
-        cost_estimate=CHEAP,
+        [shape(MEM, LAYERS, ROWS, width)] * 2,
+        limit=12,
         name="unpack_state",
     )(mine)
 
-    loglik = jnp.concatenate(logs, axis=0)
     for axis, size in (("tile", tiles), ("dom", groups)):
         hop = 1
         while hop < size:
             pairs = [(i, i ^ hop) for i in range(size)]
             loglik = loglik + lax.ppermute(loglik, axis, pairs)
             hop *= 2
+    loglik = loglik[:CYCLES]
     total_obs = observed.size * groups * tiles
     mean_loglik = loglik / total_obs
     highest = jnp.max(loglik, axis=1, keepdims=True)

time: 171 us -> 166 us (0.971)
  Pallas kernels: 75.7 us -> 55.6 us
  local copies, waits for them, and re-layouts: 5.31 us -> 19.9 us
    unnamed x26 -> x42, local copies, waits for them, and re-layouts: 2.14 us -> 19.9 us
    pallas_call x7, Pallas kernels: 64.6 us -> 50 us  [the longest x5 36.7 us: run(): pl.pallas_call(kernel, out_shape=[pltpu.HBM(o.shape, F32) if i in far els...]
    pallas_call x2, Pallas kernels: 7.26 us -> 3.12 us  [pack(): pl.pallas_call(functools.partial(pack_field, blocks=blocks, noisy=bool(no...]
  transfers between devices with their start and end apart: 16 -> 16, of which waited for: 9 -> 9; matrix products, arithmetic and copies ran while one was open for 3% -> 1% of each run, Pallas kernels for 31% -> 23%
where the time goes in v4:
time: 166 us; the launch traced here: 165 us
  Pallas kernels  55.6 us (33%)
  starting transfers between devices  44.5 us (27%)
  waiting for transfers between devices  21.5 us (13%)
  blocking collectives  21 us (13%)
  local copies, waits for them, and re-layouts  19.9 us (12%)
    pallas_call x5, Pallas kernels, run(): pl.pallas_call(kernel, out_shape=[pltpu.HBM(o.shape, F32) if i in far els...  36.7 us
    all_to_all x1, blocking collectives, spread(): owned = lax.all_to_all(sent, 'dom', split_axis=0, concat_axis=0, tiled=True)  21 us
    unnamed x42, local copies, waits for them, and re-layouts  19.9 us
    pallas_call x2, Pallas kernels, likelihood(): pl.pallas_call(functools.partial(score, members=members, cycle=cycle), gr...  13.3 us
    ppermute x5, starting transfers between devices, shards(): loglik = loglik + lax.ppermute(loglik, axis, pairs)  10.3 us
    ppermute x2, starting transfers between devices, exchange(): below = lax.ppermute(to_up, 'tile', up)  8.48 us
    ppermute x5, waiting for transfers between devices, shards(): loglik = loglik + lax.ppermute(loglik, axis, pairs)  7.69 us
    all_to_all x1, waiting for transfers between devices, spread(): owned = lax.all_to_all(sent, 'dom', split_axis=0, concat_axis=0, tiled=True)  6.43 us
  transfers between devices with their start and end apart: 16, of which 9 were waited for; matrix products, arithmetic and copies ran while one was open for 1% of the time, Pallas kernels for 23%

profile of v4, /device:TPU:0, one launch (start us, length us, event | category | flops | bytes accessed | tf_op | source)
XLA Modules:
  0.0 164.9 jit_solution(18141919186637599491)
XLA Ops:
  3.5 5.0 %collective-permute-start = (f32[768,128]{1,0:T(8,128)S(1)}, f32[768,128]{1,0:T(8,128)S(1)}, u32[]{:S(2)}, u32[]{:S(2)}) collective-permute-start(f32[768,128]{1,0:T(8,128)S(1)} %get-tuple-element.45), channel_id=1, source_target_pairs={{0,1},{1,2},{2,3},{4,5},{5,6},{6,7},{8,9},{9,10},{10,11},{12,13},{... | collective-permute-start | bytes 1179656 | tf_op jit(solution)/shard_map/ppermute | solution.py:459
  13.0 4.6 %collective-permute-start.2 = (f32[768,128]{1,0:T(8,128)S(1)}, f32[768,128]{1,0:T(8,128)S(1)}, u32[]{:S(2)}, u32[]{:S(2)}) collective-permute-start(f32[768,128]{1,0:T(8,128)S(1)} %get-tuple-element.48), channel_id=1, source_target_pairs={{0,1},{1,2},{2,3},{4,5},{5,6},{6,7},{8,9},{9,10},{10,11},{12,13},{... | collective-permute-start | bytes 1179656 | tf_op jit(solution)/shard_map/ppermute | solution.py:462
  18.9 2.0 %collective-permute-done.1.p_down = f32[768,128]{1,0:T(8,128)S(1)} collective-permute-done((f32[768,128]{1,0:T(8,128)S(1)}, f32[768,128]{1,0:T(8,128)S(1)}, u32[]{:S(2)}, u32[]{:S(2)}) %collective-permute-start.1) | collective-permute-done | bytes 393248 | tf_op jit(solution)/shard_map/ppermute | solution.py:460
  20.9 2.4 %pack_noise.1 = f32[8,4,9,8,128]{4,3,2,1,0:T(8,128)} custom-call(f32[2,4,2,16,2048]{4,3,2,1,0:T(8,128)S(1)} %copy-done.3), custom_call_target="tpu_custom_call" | custom-call | flops 1000 | bytes 1000 | tf_op jit(solution)/shard_map/pack_noise/pallas_call | solution.py:466
  23.3 2.0 %collective-permute-done.2.q_up = f32[768,128]{1,0:T(8,128)S(1)} collective-permute-done((f32[768,128]{1,0:T(8,128)S(1)}, f32[768,128]{1,0:T(8,128)S(1)}, u32[]{:S(2)}, u32[]{:S(2)}) %collective-permute-start.2) | collective-permute-done | bytes 393248 | tf_op jit(solution)/shard_map/ppermute | solution.py:462
  26.1 3.4 %collective-permute-done.3.q_down = f32[768,128]{1,0:T(8,128)S(1)} collective-permute-done((f32[768,128]{1,0:T(8,128)S(1)}, f32[768,128]{1,0:T(8,128)S(1)}, u32[]{:S(2)}, u32[]{:S(2)}) %collective-permute-start.3) | collective-permute-done | bytes 393248 | tf_op jit(solution)/shard_map/ppermute | solution.py:463
  30.2 3.7 %all-to-all-start = ((f32[8,4,9,8,128]{4,3,2,1,0:T(8,128)}), f32[8,4,9,8,128]{4,3,2,1,0:T(8,128)S(1)}, u32[]{:S(2)}, u32[]{:S(2)}) async-start(f32[8,4,9,8,128]{4,3,2,1,0:T(8,128)} %pack_noise.1), calls=%async_computation | async-start | bytes 2359296 | tf_op jit(solution)/shard_map/all_to_all | solution.py:478
  38.0 14.0 %advance_members.1 = (f32[8,4,9,8,128]{4,3,2,1,0:T(8,128)}, f32[8,4,9,8,128]{4,3,2,1,0:T(8,128)}) custom-call(s32[2]{0:T(128)S(1)} %pad_add_fusion.edge, f32[2048,128]{1,0:T(8,128)S(1)} %get-tuple-element.43.q_main, f32[2048,128]{1,0:T(8,128)S(1)} %get-tuple-element.44.p_main, f32[768,128]{1,0:T(8,128)S(1)} %copy-done.13, f32[768,128]{1,0:T(8,128)S(1)} %copy-done.9, ...), custom_call_target="tpu_custom_call" | custom-call | flops 1000 | bytes 1000 | tf_op jit(solution)/shard_map/advance_members/pallas_call | solution.py:404
  52.0 21.0 %all_to_all.20 = f32[8,4,9,8,128]{4,3,2,1,0:T(8,128)S(1)} all-to-all(f32[8,4,9,8,128]{4,3,2,1,0:T(8,128)} %get-tuple-element.57), channel_id=1, replica_groups=mesh['dom'=8,'tile'=4] {'dom'}, dimensions={0} | all-to-all | bytes 2359296 | tf_op jit(solution)/shard_map/all_to_all | solution.py:501
  72.9 3.7 %all-to-all-start.2 = ((f32[8,4,9,8,128]{4,3,2,1,0:T(8,128)}), f32[8,4,9,8,128]{4,3,2,1,0:T(8,128)S(1)}, u32[]{:S(2)}, u32[]{:S(2)}) async-start(f32[8,4,9,8,128]{4,3,2,1,0:T(8,128)} %get-tuple-element.58), calls=%async_computation.2 | async-start | bytes 2359296 | tf_op jit(solution)/shard_map/all_to_all | solution.py:501
  77.0 4.4 %resample_psi.1 = (f32[2048,128]{1,0:T(8,128)}, f32[256,128]{1,0:T(8,128)}, f32[832,128]{1,0:T(8,128)}, f32[832,128]{1,0:T(8,128)}, f32[2,512,128]{2,1,0:T(8,128)}) custom-call(s32[32]{0:T(128)S(1)} %get-tuple-element.78.parent, f32[32,72,128]{2,1,0:T(8,128)S(1)} %bitcast.11), custom_call_target="tpu_custom_call" | custom-call | flops 1000 | bytes 1000 | tf_op jit(solution)/shard_map/resample_psi/pallas_call | solution.py:404
  81.4 4.2 %collective-permute-start.5 = (f32[832,128]{1,0:T(8,128)}, f32[832,128]{1,0:T(8,128)S(1)}, u32[]{:S(2)}, u32[]{:S(2)}) collective-permute-start(f32[832,128]{1,0:T(8,128)} %get-tuple-element.68), channel_id=1, source_target_pairs={{0,1},{1,2},{2,3},{4,5},{5,6},{6,7},{8,9},{9,10},{10,11},{12,13},{... | collective-permute-start | bytes 1277960 | tf_op jit(solution)/shard_map/ppermute | solution.py:514
  86.9 6.4 %all-to-all-done.2 = f32[8,4,9,8,128]{4,3,2,1,0:T(8,128)S(1)} async-done(((f32[8,4,9,8,128]{4,3,2,1,0:T(8,128)}), f32[8,4,9,8,128]{4,3,2,1,0:T(8,128)S(1)}, u32[]{:S(2)}, u32[]{:S(2)}) %all-to-all-start.2) | async-done | bytes 1179680 | tf_op jit(solution)/shard_map/all_to_all | solution.py:501
  93.4 2.6 %resample_q.1 = (f32[2048,128]{1,0:T(8,128)S(1)}, f32[256,128]{1,0:T(8,128)S(1)}, f32[832,128]{1,0:T(8,128)S(1)}, f32[832,128]{1,0:T(8,128)S(1)}) custom-call(s32[32]{0:T(128)S(1)} %get-tuple-element.78.parent, f32[32,72,128]{2,1,0:T(8,128)S(1)} %bitcast.10, f32[32,72,128]{2,1,0:T(8,128)S(1)} %bitcast.9), custom_call_target="tpu_custom_call" | custom-call | flops 1000 | bytes 1000 | tf_op jit(solution)/shard_map/resample_q/pallas_call | solution.py:404
  95.9 4.2 %collective-permute-start.4 = (f32[832,128]{1,0:T(8,128)S(1)}, f32[832,128]{1,0:T(8,128)S(1)}, u32[]{:S(2)}, u32[]{:S(2)}) collective-permute-start(f32[832,128]{1,0:T(8,128)S(1)} %get-tuple-element.67), channel_id=1, source_target_pairs={{0,1},{1,2},{2,3},{4,5},{5,6},{6,7},{8,9},{9,10},{10,11},{12,13},{... | collective-permute-start | bytes 1277960 | tf_op jit(solution)/shard_map/ppermute | solution.py:514
  101.5 5.8 %copy-done = f32[2,2,1024,1024]{3,2,1,0:T(8,128)S(1)} copy-done((f32[2,2,1024,1024]{3,2,1,0:T(8,128)S(1)}, f32[2,2,1024,1024]{3,2,1,0:T(8,128)}, u32[]{:S(2)}) %copy-start) | copy-done | bytes 16777240
  107.3 6.6 %score.2.first_ref = f32[8,32]{1,0:T(8,128)S(1)} custom-call(s32[2,2]{1,0:T(2,128)S(1)} %copy-done.19, f32[2,512,128]{2,1,0:T(8,128)S(1)} %copy-done.7, f32[2,2,1024,1024]{3,2,1,0:T(8,128)S(1)} %copy-done, f32[2,2,1024]{2,1,0:T(2,128)S(1)} %copy-done.17, f32[2,2,1024]{2,1,0:T(2,128)S(1)} %copy-done.18, f32[8,32]{1,0:T(8,128)S(1)} %broadcast_in_dim.2.first_ref), custom_call_target="tpu_custom_call" | custom-call | flops 1000 | bytes 1000 | tf_op jit(solution)/shard_map/score/pallas_call | solution.py:528
  114.0 14.2 %advance_columns.1 = (f32[32,16,8,128]{3,2,1,0:T(8,128)}, f32[2,512,128]{2,1,0:T(8,128)S(1)}) custom-call(s32[2]{0:T(128)S(1)} %pad_add_fusion.edge, s32[32]{0:T(128)S(1)} %get-tuple-element.79.parent, f32[2048,128]{1,0:T(8,128)S(1)} %get-tuple-element.60.q_main, f32[2048,128]{1,0:T(8,128)S(1)} %copy-done.5, f32[256,128]{1,0:T(8,128)S(1)} %get-tuple-element.65.q_edge, ...), custom_call_target="tpu_custom_call" | custom-call | flops 1000 | bytes 1000 | tf_op jit(solution)/shard_map/advance_columns/pallas_call | solution.py:404
  128.3 3.6 %all-to-all-start.3 = ((f32[8,4,128,128]{3,2,1,0:T(8,128)}), f32[8,4,128,128]{3,2,1,0:T(8,128)S(1)}, u32[]{:S(2)}, u32[]{:S(2)}) async-start(f32[8,4,128,128]{3,2,1,0:T(8,128)} %bitcast.12), calls=%async_computation.3 | async-start | bytes 4194304 | tf_op jit(solution)/shard_map/all_to_all | solution.py:563
  131.9 5.8 %copy-done.1 = f32[2,2,1024,1024]{3,2,1,0:T(8,128)S(1)} copy-done((f32[2,2,1024,1024]{3,2,1,0:T(8,128)S(1)}, f32[2,2,1024,1024]{3,2,1,0:T(8,128)}, u32[]{:S(2)}) %copy-start.1) | copy-done | bytes 16777240
  137.6 6.6 %score.3 = f32[8,32]{1,0:T(8,128)S(1)} custom-call(s32[2,2]{1,0:T(2,128)S(1)} %copy-done.19, f32[2,512,128]{2,1,0:T(8,128)S(1)} %get-tuple-element.74.z_ref, f32[2,2,1024,1024]{3,2,1,0:T(8,128)S(1)} %copy-done.1, f32[2,2,1024]{2,1,0:T(2,128)S(1)} %copy-done.17, f32[2,2,1024]{2,1,0:T(2,128)S(1)} %copy-done.18, f32[8,32]{1,0:T(8,128)S(1)} %score.2.first_ref), custom_call_target="tpu_custom_call" | custom-call | flops 1000 | bytes 1000 | tf_op jit(solution)/shard_map/score/pallas_call | solution.py:528
  144.3 3.4 %collective-permute-start.8 = (f32[8,32]{1,0:T(8,128)S(1)}, f32[8,32]{1,0:T(8,128)S(1)}, u32[]{:S(2)}, u32[]{:S(2)}) collective-permute-start(f32[8,32]{1,0:T(8,128)S(1)} %score.3), channel_id=1, source_target_pairs={{0,1},{1,0},{2,3},{3,2},{4,5},{5,4},{6,7},{7,6},{8,9},{9,8},{10,11... | collective-permute-start | bytes 3080 | tf_op jit(solution)/shard_map/ppermute | solution.py:577
  149.3 3.0 %collective-permute-start.9 = (f32[8,32]{1,0:T(8,128)S(1)}, f32[8,32]{1,0:T(8,128)S(1)}, u32[]{:S(2)}, u32[]{:S(2)}) collective-permute-start(f32[8,32]{1,0:T(8,128)S(1)} %add.15), channel_id=1, source_target_pairs={{0,2},{1,3},{2,0},{3,1},{4,6},{5,7},{6,4},{7,5},{8,10},{9,11},{10,... | collective-permute-start | bytes 3080 | tf_op jit(solution)/shard_map/ppermute | solution.py:577
  158.7 1.9 %collective-permute-start.12 = (f32[8,32]{1,0:T(8,128)S(1)}, f32[8,32]{1,0:T(8,128)S(1)}, u32[]{:S(2)}, u32[]{:S(2)}) collective-permute-start(f32[8,32]{1,0:T(8,128)S(1)} %add.18), channel_id=1, source_target_pairs={{0,16},{4,20},{8,24},{12,28},{16,0},{20,4},{24,8},{28,12},{1,17},{... | collective-permute-start | bytes 3080 | tf_op jit(solution)/shard_map/ppermute | solution.py:577
  (75 shorter events, 29.3 us)
Async XLA Ops:
  0.6 9.1 %copy-start.4 = (f32[4,2,16,2048]{3,2,1,0:T(8,128)S(1)}, f32[4,2,16,2048]{3,2,1,0:T(8,128)}, u32[]{:S(2)}) copy-start(f32[4,2,16,2048]{3,2,1,0:T(8,128)} %refs_0_.2) | copy-start | bytes 3145732
  3.5 15.4 %collective-permute-start = (f32[768,128]{1,0:T(8,128)S(1)}, f32[768,128]{1,0:T(8,128)S(1)}, u32[]{:S(2)}, u32[]{:S(2)}) collective-permute-start(f32[768,128]{1,0:T(8,128)S(1)} %get-tuple-element.45), channel_id=1, source_target_pairs={{0,1},{1,2},{2,3},{4,5},{5,6},{6,7},{8,9},{9,10},{10,11},{12,13},{... | collective-permute-start | bytes 1179656 | tf_op jit(solution)/shard_map/ppermute | solution.py:459
  8.4 12.5 %collective-permute-start.1 = (f32[768,128]{1,0:T(8,128)S(1)}, f32[768,128]{1,0:T(8,128)S(1)}, u32[]{:S(2)}, u32[]{:S(2)}) collective-permute-start(f32[768,128]{1,0:T(8,128)S(1)} %get-tuple-element.46), channel_id=1, source_target_pairs={{1,0},{2,1},{3,2},{5,4},{6,5},{7,6},{9,8},{10,9},{11,10},{13,12},{... | collective-permute-start | bytes 1179656 | tf_op jit(solution)/shard_map/ppermute | solution.py:460
  11.3 9.6 %copy-start.3 = (f32[2,4,2,16,2048]{4,3,2,1,0:T(8,128)S(1)}, f32[2,4,2,16,2048]{4,3,2,1,0:T(8,128)}, u32[]{:S(2)}) copy-start(f32[2,4,2,16,2048]{4,3,2,1,0:T(8,128)} %n_ref) | copy-start | bytes 6291460
  13.0 12.3 %collective-permute-start.2 = (f32[768,128]{1,0:T(8,128)S(1)}, f32[768,128]{1,0:T(8,128)S(1)}, u32[]{:S(2)}, u32[]{:S(2)}) collective-permute-start(f32[768,128]{1,0:T(8,128)S(1)} %get-tuple-element.48), channel_id=1, source_target_pairs={{0,1},{1,2},{2,3},{4,5},{5,6},{6,7},{8,9},{9,10},{10,11},{12,13},{... | collective-permute-start | bytes 1179656 | tf_op jit(solution)/shard_map/ppermute | solution.py:462
  17.5 11.9 %collective-permute-start.3 = (f32[768,128]{1,0:T(8,128)S(1)}, f32[768,128]{1,0:T(8,128)S(1)}, u32[]{:S(2)}, u32[]{:S(2)}) collective-permute-start(f32[768,128]{1,0:T(8,128)S(1)} %get-tuple-element.49), channel_id=1, source_target_pairs={{1,0},{2,1},{3,2},{5,4},{6,5},{7,6},{9,8},{10,9},{11,10},{13,12},{... | collective-permute-start | bytes 1179656 | tf_op jit(solution)/shard_map/ppermute | solution.py:463
  30.2 21.8 %all-to-all-start = ((f32[8,4,9,8,128]{4,3,2,1,0:T(8,128)}), f32[8,4,9,8,128]{4,3,2,1,0:T(8,128)S(1)}, u32[]{:S(2)}, u32[]{:S(2)}) async-start(f32[8,4,9,8,128]{4,3,2,1,0:T(8,128)} %pack_noise.1), calls=%async_computation | async-start | bytes 2359296 | tf_op jit(solution)/shard_map/all_to_all | solution.py:478
  72.9 20.4 %all-to-all-start.2 = ((f32[8,4,9,8,128]{4,3,2,1,0:T(8,128)}), f32[8,4,9,8,128]{4,3,2,1,0:T(8,128)S(1)}, u32[]{:S(2)}, u32[]{:S(2)}) async-start(f32[8,4,9,8,128]{4,3,2,1,0:T(8,128)} %get-tuple-element.58), calls=%async_computation.2 | async-start | bytes 2359296 | tf_op jit(solution)/shard_map/all_to_all | solution.py:501
  81.4 32.6 %collective-permute-start.5 = (f32[832,128]{1,0:T(8,128)}, f32[832,128]{1,0:T(8,128)S(1)}, u32[]{:S(2)}, u32[]{:S(2)}) collective-permute-start(f32[832,128]{1,0:T(8,128)} %get-tuple-element.68), channel_id=1, source_target_pairs={{0,1},{1,2},{2,3},{4,5},{5,6},{6,7},{8,9},{9,10},{10,11},{12,13},{... | collective-permute-start | bytes 1277960 | tf_op jit(solution)/shard_map/ppermute | solution.py:514
  85.6 28.3 %collective-permute-start.7 = (f32[832,128]{1,0:T(8,128)}, f32[832,128]{1,0:T(8,128)S(1)}, u32[]{:S(2)}, u32[]{:S(2)}) collective-permute-start(f32[832,128]{1,0:T(8,128)} %get-tuple-element.70), channel_id=1, source_target_pairs={{1,0},{2,1},{3,2},{5,4},{6,5},{7,6},{9,8},{10,9},{11,10},{13,12},{... | collective-permute-start | bytes 1277960 | tf_op jit(solution)/shard_map/ppermute | solution.py:515
  93.4 8.1 %copy-start.7 = (f32[2,512,128]{2,1,0:T(8,128)S(1)}, f32[2,512,128]{2,1,0:T(8,128)}, u32[]{:S(2)}) copy-start(f32[2,512,128]{2,1,0:T(8,128)} %get-tuple-element.63.z_ref) | copy-start | bytes 1572868
  93.4 8.1 %copy-start.17 = (f32[2,2,1024]{2,1,0:T(2,128)S(1)}, f32[2,2,1024]{2,1,0:T(2,128)}, u32[]{:S(2)}) copy-start(f32[2,2,1024]{2,1,0:T(2,128)} %o_ref.3) | copy-start | bytes 49156
  93.4 8.2 %copy-start.18 = (f32[2,2,1024]{2,1,0:T(2,128)S(1)}, f32[2,2,1024]{2,1,0:T(2,128)}, u32[]{:S(2)}) copy-start(f32[2,2,1024]{2,1,0:T(2,128)} %w_ref.3) | copy-start | bytes 49156
  93.4 8.2 %copy-start.19 = (s32[2,2]{1,0:T(2,128)S(1)}, s32[2,2]{1,0:T(2,128)}, u32[]{:S(2)}) copy-start(s32[2,2]{1,0:T(2,128)} %rows_ref.3) | copy-start | bytes 52
  95.9 18.1 %collective-permute-start.4 = (f32[832,128]{1,0:T(8,128)S(1)}, f32[832,128]{1,0:T(8,128)S(1)}, u32[]{:S(2)}, u32[]{:S(2)}) collective-permute-start(f32[832,128]{1,0:T(8,128)S(1)} %get-tuple-element.67), channel_id=1, source_target_pairs={{0,1},{1,2},{2,3},{4,5},{5,6},{6,7},{8,9},{9,10},{10,11},{12,13},{... | collective-permute-start | bytes 1277960 | tf_op jit(solution)/shard_map/ppermute | solution.py:514
  100.2 13.8 %collective-permute-start.6 = (f32[832,128]{1,0:T(8,128)S(1)}, f32[832,128]{1,0:T(8,128)S(1)}, u32[]{:S(2)}, u32[]{:S(2)}) collective-permute-start(f32[832,128]{1,0:T(8,128)S(1)} %get-tuple-element.69), channel_id=1, source_target_pairs={{1,0},{2,1},{3,2},{5,4},{6,5},{7,6},{9,8},{10,9},{11,10},{13,12},{... | collective-permute-start | bytes 1277960 | tf_op jit(solution)/shard_map/ppermute | solution.py:515
  107.3 6.7 %copy-start.5 = (f32[2048,128]{1,0:T(8,128)S(1)}, f32[2048,128]{1,0:T(8,128)}, u32[]{:S(2)}) copy-start(f32[2048,128]{1,0:T(8,128)} %get-tuple-element.64.p_main) | copy-start | bytes 3145732
  107.3 6.7 %copy-start.16 = (f32[256,128]{1,0:T(8,128)S(1)}, f32[256,128]{1,0:T(8,128)}, u32[]{:S(2)}) copy-start(f32[256,128]{1,0:T(8,128)} %get-tuple-element.66.p_edge) | copy-start | bytes 393220
  128.3 35.0 %all-to-all-start.3 = ((f32[8,4,128,128]{3,2,1,0:T(8,128)}), f32[8,4,128,128]{3,2,1,0:T(8,128)S(1)}, u32[]{:S(2)}, u32[]{:S(2)}) async-start(f32[8,4,128,128]{3,2,1,0:T(8,128)} %bitcast.12), calls=%async_computation.3 | async-start | bytes 4194304 | tf_op jit(solution)/shard_map/all_to_all | solution.py:563
  144.3 5.0 %collective-permute-start.8 = (f32[8,32]{1,0:T(8,128)S(1)}, f32[8,32]{1,0:T(8,128)S(1)}, u32[]{:S(2)}, u32[]{:S(2)}) collective-permute-start(f32[8,32]{1,0:T(8,128)S(1)} %score.3), channel_id=1, source_target_pairs={{0,1},{1,0},{2,3},{3,2},{4,5},{5,4},{6,7},{7,6},{8,9},{9,8},{10,11... | collective-permute-start | bytes 3080 | tf_op jit(solution)/shard_map/ppermute | solution.py:577
  149.3 4.6 %collective-permute-start.9 = (f32[8,32]{1,0:T(8,128)S(1)}, f32[8,32]{1,0:T(8,128)S(1)}, u32[]{:S(2)}, u32[]{:S(2)}) collective-permute-start(f32[8,32]{1,0:T(8,128)S(1)} %add.15), channel_id=1, source_target_pairs={{0,2},{1,3},{2,0},{3,1},{4,6},{5,7},{6,4},{7,5},{8,10},{9,11},{10,... | collective-permute-start | bytes 3080 | tf_op jit(solution)/shard_map/ppermute | solution.py:577
  153.9 1.2 collective-permute-start.10
  155.1 3.6 %collective-permute-start.11 = (f32[8,32]{1,0:T(8,128)S(1)}, f32[8,32]{1,0:T(8,128)S(1)}, u32[]{:S(2)}, u32[]{:S(2)}) collective-permute-start(f32[8,32]{1,0:T(8,128)S(1)} %add.17), channel_id=1, source_target_pairs={{0,8},{4,12},{8,0},{12,4},{16,24},{20,28},{24,16},{28,20},{1,9},{5... | collective-permute-start | bytes 3080 | tf_op jit(solution)/shard_map/ppermute | solution.py:577
  158.7 3.6 %collective-permute-start.12 = (f32[8,32]{1,0:T(8,128)S(1)}, f32[8,32]{1,0:T(8,128)S(1)}, u32[]{:S(2)}, u32[]{:S(2)}) collective-permute-start(f32[8,32]{1,0:T(8,128)S(1)} %add.18), channel_id=1, source_target_pairs={{0,16},{4,20},{8,24},{12,28},{16,0},{20,4},{24,8},{28,12},{1,17},{... | collective-permute-start | bytes 3080 | tf_op jit(solution)/shard_map/ppermute | solution.py:577
  (13 other events, 30.6 us)

commit v5 on v4

--- a/solution.py
+++ b/solution.py
@@ -396,7 +396,7 @@
 def call(kernel, outs, scratch=(), scalars=0, resident=10, limit=16, far=(), name=None):
     def run(*args):
         args = args[:scalars] + tuple(
-            pltpu.with_memory_space_constraint(x, pltpu.VMEM) if i < resident else x
+            pltpu.with_memory_space_constraint(x, pltpu.VMEM if i < resident else pltpu.HBM)
             for i, x in enumerate(args[scalars:])
         )
         specs = [pl.BlockSpec(memory_space=pltpu.SMEM)] * scalars
@@ -521,6 +521,8 @@
     q_owned = spread(q_sent)
     p_main, p_edge, p_below, p_above, surface = exchange(p_owned)
     q_main, q_edge, q_below, q_above = exchange(q_owned, (noise,))
+
+    stored = pltpu.with_memory_space_constraint(footprint, pltpu.HBM)
 
     def likelihood(cycle, surface, logs):
         small = pl.BlockSpec((1, per, observations), lambda a, c: (a, 0, 0))
@@ -545,7 +547,7 @@
             compiler_params=params,
             cost_estimate=CHEAP,
             name="score",
-        )(block_rows, surface, footprint, observed, precision, logs)
+        )(block_rows, surface, stored, observed, precision, logs)
 
     logs = likelihood(0, surface, jnp.zeros((SUB, members), F32))
     p_main, logs = lax.optimization_barrier((p_main, logs))

time: 166 us -> 159 us (0.958)
  local copies, waits for them, and re-layouts: 19.9 us -> 3.69 us
  waiting for transfers between devices: 21.5 us -> 28.1 us
  Pallas kernels: 55.6 us -> 61.2 us
  starting transfers between devices: 44.5 us -> 42.7 us
    unnamed x42 -> x28, local copies, waits for them, and re-layouts: 19.9 us -> 3.68 us
    pallas_call x2, Pallas kernels: 13.3 us -> 18.2 us  [likelihood(): pl.pallas_call(functools.partial(score, members=members, cycle=cycle), gr...]
    ppermute x5, waiting for transfers between devices: 7.69 us -> 11.3 us  [shards(): loglik = loglik + lax.ppermute(loglik, axis, pairs)]
    all_to_all x1, waiting for transfers between devices: 0.01 us -> 1.96 us  [shards(): lax.all_to_all(noise, 'dom', split_axis=0, concat_axis=0, tiled=True)]
  transfers between devices with their start and end apart: 16 -> 16, of which waited for: 9 -> 10; matrix products, arithmetic and copies ran while one was open for 1% -> 1% of each run, Pallas kernels for 23% -> 28%
where the time goes in v5:
time: 159 us; the launch traced here: 158 us
  Pallas kernels  61.2 us (38%)
  starting transfers between devices  42.7 us (27%)
  waiting for transfers between devices  28.1 us (18%)
  blocking collectives  20.2 us (13%)
  local copies, waits for them, and re-layouts  3.69 us (2%)
    pallas_call x5, Pallas kernels, run(): pl.pallas_call(kernel, out_shape=[pltpu.HBM(o.shape, F32) if i in far els...  37.5 us
    all_to_all x1, blocking collectives, spread(): owned = lax.all_to_all(sent, 'dom', split_axis=0, concat_axis=0, tiled=True)  20.2 us
    pallas_call x2, Pallas kernels, likelihood(): pl.pallas_call(functools.partial(score, members=members, cycle=cycle), gr...  18.2 us
    ppermute x5, waiting for transfers between devices, shards(): loglik = loglik + lax.ppermute(loglik, axis, pairs)  11.3 us
    ppermute x5, starting transfers between devices, shards(): loglik = loglik + lax.ppermute(loglik, axis, pairs)  9.06 us
    all_to_all x1, waiting for transfers between devices, spread(): owned = lax.all_to_all(sent, 'dom', split_axis=0, concat_axis=0, tiled=True)  7.21 us
    ppermute x2, starting transfers between devices, exchange(): below = lax.ppermute(to_up, 'tile', up)  6.92 us
    ppermute x1, starting transfers between devices, shards(): p_below = lax.ppermute(p_up, 'tile', up)  4.95 us
  transfers between devices with their start and end apart: 16, of which 10 were waited for; matrix products, arithmetic and copies ran while one was open for 1% of the time, Pallas kernels for 28%

profile of v5, /device:TPU:0, one launch (start us, length us, event | category | flops | bytes accessed | tf_op | source)
XLA Modules:
  0.0 158.2 jit_solution(13708604312099334539)
XLA Ops:
  3.5 5.0 %collective-permute-start = (f32[768,128]{1,0:T(8,128)S(1)}, f32[768,128]{1,0:T(8,128)S(1)}, u32[]{:S(2)}, u32[]{:S(2)}) collective-permute-start(f32[768,128]{1,0:T(8,128)S(1)} %get-tuple-element.45), channel_id=1, source_target_pairs={{0,1},{1,2},{2,3},{4,5},{5,6},{6,7},{8,9},{9,10},{10,11},{12,13},{... | collective-permute-start | bytes 1179656 | tf_op jit(solution)/shard_map/ppermute | solution.py:459
  13.0 4.6 %collective-permute-start.2 = (f32[768,128]{1,0:T(8,128)S(1)}, f32[768,128]{1,0:T(8,128)S(1)}, u32[]{:S(2)}, u32[]{:S(2)}) collective-permute-start(f32[768,128]{1,0:T(8,128)S(1)} %get-tuple-element.48), channel_id=1, source_target_pairs={{0,1},{1,2},{2,3},{4,5},{5,6},{6,7},{8,9},{9,10},{10,11},{12,13},{... | collective-permute-start | bytes 1179656 | tf_op jit(solution)/shard_map/ppermute | solution.py:462
  18.9 2.0 %collective-permute-done.1.p_down = f32[768,128]{1,0:T(8,128)S(1)} collective-permute-done((f32[768,128]{1,0:T(8,128)S(1)}, f32[768,128]{1,0:T(8,128)S(1)}, u32[]{:S(2)}, u32[]{:S(2)}) %collective-permute-start.1) | collective-permute-done | bytes 393248 | tf_op jit(solution)/shard_map/ppermute | solution.py:460
  20.9 2.4 %pack_noise.1 = f32[8,4,9,8,128]{4,3,2,1,0:T(8,128)} custom-call(f32[2,4,2,16,2048]{4,3,2,1,0:T(8,128)S(1)} %copy-done.1), custom_call_target="tpu_custom_call" | custom-call | flops 1000 | bytes 1000 | tf_op jit(solution)/shard_map/pack_noise/pallas_call | solution.py:466
  23.3 2.0 %collective-permute-done.2.q_up = f32[768,128]{1,0:T(8,128)S(1)} collective-permute-done((f32[768,128]{1,0:T(8,128)S(1)}, f32[768,128]{1,0:T(8,128)S(1)}, u32[]{:S(2)}, u32[]{:S(2)}) %collective-permute-start.2) | collective-permute-done | bytes 393248 | tf_op jit(solution)/shard_map/ppermute | solution.py:462
  26.1 3.5 %collective-permute-done.3.q_down = f32[768,128]{1,0:T(8,128)} collective-permute-done((f32[768,128]{1,0:T(8,128)S(1)}, f32[768,128]{1,0:T(8,128)}, u32[]{:S(2)}, u32[]{:S(2)}) %collective-permute-start.3) | collective-permute-done | bytes 393248 | tf_op jit(solution)/shard_map/ppermute | solution.py:463
  29.6 3.7 %all-to-all-start = ((f32[8,4,9,8,128]{4,3,2,1,0:T(8,128)}), f32[8,4,9,8,128]{4,3,2,1,0:T(8,128)S(1)}, u32[]{:S(2)}, u32[]{:S(2)}) async-start(f32[8,4,9,8,128]{4,3,2,1,0:T(8,128)} %pack_noise.1), calls=%async_computation | async-start | bytes 2359296 | tf_op jit(solution)/shard_map/all_to_all | solution.py:478
  33.4 14.8 %advance_members.1 = (f32[8,4,9,8,128]{4,3,2,1,0:T(8,128)}, f32[8,4,9,8,128]{4,3,2,1,0:T(8,128)}) custom-call(s32[2]{0:T(128)S(1)} %pad_add_fusion.edge, f32[2048,128]{1,0:T(8,128)S(1)} %get-tuple-element.43.q_main, f32[2048,128]{1,0:T(8,128)S(1)} %get-tuple-element.44.p_main, f32[768,128]{1,0:T(8,128)} %copy-done.12, f32[768,128]{1,0:T(8,128)} %copy-done.10, ...), custom_call_target="tpu_custom_call" | custom-call | flops 1000 | bytes 1000 | tf_op jit(solution)/shard_map/advance_members/pallas_call | solution.py:404
  50.1 20.2 %all_to_all.20 = f32[8,4,9,8,128]{4,3,2,1,0:T(8,128)S(1)} all-to-all(f32[8,4,9,8,128]{4,3,2,1,0:T(8,128)} %get-tuple-element.57), channel_id=1, replica_groups=mesh['dom'=8,'tile'=4] {'dom'}, dimensions={0} | all-to-all | bytes 2359296 | tf_op jit(solution)/shard_map/all_to_all | solution.py:501
  70.3 3.7 %all-to-all-start.2 = ((f32[8,4,9,8,128]{4,3,2,1,0:T(8,128)}), f32[8,4,9,8,128]{4,3,2,1,0:T(8,128)S(1)}, u32[]{:S(2)}, u32[]{:S(2)}) async-start(f32[8,4,9,8,128]{4,3,2,1,0:T(8,128)} %get-tuple-element.58), calls=%async_computation.2 | async-start | bytes 2359296 | tf_op jit(solution)/shard_map/all_to_all | solution.py:501
  74.4 4.4 %resample_psi.1 = (f32[2048,128]{1,0:T(8,128)}, f32[256,128]{1,0:T(8,128)}, f32[832,128]{1,0:T(8,128)}, f32[832,128]{1,0:T(8,128)}, f32[2,512,128]{2,1,0:T(8,128)}) custom-call(s32[32]{0:T(128)S(1)} %get-tuple-element.78.parent, f32[32,72,128]{2,1,0:T(8,128)S(1)} %bitcast.11), custom_call_target="tpu_custom_call" | custom-call | flops 1000 | bytes 1000 | tf_op jit(solution)/shard_map/resample_psi/pallas_call | solution.py:404
  78.8 3.5 %collective-permute-start.5 = (f32[832,128]{1,0:T(8,128)}, f32[832,128]{1,0:T(8,128)S(1)}, u32[]{:S(2)}, u32[]{:S(2)}) collective-permute-start(f32[832,128]{1,0:T(8,128)} %get-tuple-element.68), channel_id=1, source_target_pairs={{0,1},{1,2},{2,3},{4,5},{5,6},{6,7},{8,9},{9,10},{10,11},{12,13},{... | collective-permute-start | bytes 1277960 | tf_op jit(solution)/shard_map/ppermute | solution.py:514
  83.6 7.2 %all-to-all-done.2 = f32[8,4,9,8,128]{4,3,2,1,0:T(8,128)S(1)} async-done(((f32[8,4,9,8,128]{4,3,2,1,0:T(8,128)}), f32[8,4,9,8,128]{4,3,2,1,0:T(8,128)S(1)}, u32[]{:S(2)}, u32[]{:S(2)}) %all-to-all-start.2) | async-done | bytes 1179680 | tf_op jit(solution)/shard_map/all_to_all | solution.py:501
  90.8 2.6 %resample_q.1 = (f32[2048,128]{1,0:T(8,128)S(1)}, f32[256,128]{1,0:T(8,128)S(1)}, f32[832,128]{1,0:T(8,128)S(1)}, f32[832,128]{1,0:T(8,128)S(1)}) custom-call(s32[32]{0:T(128)S(1)} %get-tuple-element.78.parent, f32[32,72,128]{2,1,0:T(8,128)S(1)} %bitcast.10, f32[32,72,128]{2,1,0:T(8,128)S(1)} %bitcast.9), custom_call_target="tpu_custom_call" | custom-call | flops 1000 | bytes 1000 | tf_op jit(solution)/shard_map/resample_q/pallas_call | solution.py:404
  93.3 3.5 %collective-permute-start.4 = (f32[832,128]{1,0:T(8,128)S(1)}, f32[832,128]{1,0:T(8,128)S(1)}, u32[]{:S(2)}, u32[]{:S(2)}) collective-permute-start(f32[832,128]{1,0:T(8,128)S(1)} %get-tuple-element.67), channel_id=1, source_target_pairs={{0,1},{1,2},{2,3},{4,5},{5,6},{6,7},{8,9},{9,10},{10,11},{12,13},{... | collective-permute-start | bytes 1277960 | tf_op jit(solution)/shard_map/ppermute | solution.py:514
  98.2 9.1 %score.2.first_ref = f32[8,32]{1,0:T(8,128)S(1)} custom-call(s32[2,2]{1,0:T(2,128)S(1)} %copy-done.9, f32[2,512,128]{2,1,0:T(8,128)S(1)} %copy-done.5, f32[2,2,1024,1024]{3,2,1,0:T(8,128)} %f_ref.3, f32[2,2,1024]{2,1,0:T(2,128)S(1)} %copy-done.7, f32[2,2,1024]{2,1,0:T(2,128)S(1)} %copy-done.8, f32[8,32]{1,0:T(8,128)S(1)} %broadcast_in_dim.2.first_ref), custom_call_target="tpu_custom_call" | custom-call | flops 1000 | bytes 1000 | tf_op jit(solution)/shard_map/score/pallas_call | solution.py:530
  107.4 14.2 %advance_columns.1 = (f32[32,16,8,128]{3,2,1,0:T(8,128)}, f32[2,512,128]{2,1,0:T(8,128)S(1)}) custom-call(s32[2]{0:T(128)S(1)} %pad_add_fusion.edge, s32[32]{0:T(128)S(1)} %get-tuple-element.79.parent, f32[2048,128]{1,0:T(8,128)S(1)} %get-tuple-element.60.q_main, f32[2048,128]{1,0:T(8,128)S(1)} %copy-done.3, f32[256,128]{1,0:T(8,128)S(1)} %get-tuple-element.65.q_edge, ...), custom_call_target="tpu_custom_call" | custom-call | flops 1000 | bytes 1000 | tf_op jit(solution)/shard_map/advance_columns/pallas_call | solution.py:404
  121.6 4.6 %all-to-all-start.3 = ((f32[8,4,128,128]{3,2,1,0:T(8,128)}), f32[8,4,128,128]{3,2,1,0:T(8,128)S(1)}, u32[]{:S(2)}, u32[]{:S(2)}) async-start(f32[8,4,128,128]{3,2,1,0:T(8,128)} %bitcast.12), calls=%async_computation.3 | async-start | bytes 4194304 | tf_op jit(solution)/shard_map/all_to_all | solution.py:565
  126.2 9.0 %score.3 = f32[8,32]{1,0:T(8,128)S(1)} custom-call(s32[2,2]{1,0:T(2,128)S(1)} %copy-done.9, f32[2,512,128]{2,1,0:T(8,128)S(1)} %get-tuple-element.74.z_ref, f32[2,2,1024,1024]{3,2,1,0:T(8,128)} %f_ref.3, f32[2,2,1024]{2,1,0:T(2,128)S(1)} %copy-done.7, f32[2,2,1024]{2,1,0:T(2,128)S(1)} %copy-done.8, f32[8,32]{1,0:T(8,128)S(1)} %score.2.first_ref), custom_call_target="tpu_custom_call" | custom-call | flops 1000 | bytes 1000 | tf_op jit(solution)/shard_map/score/pallas_call | solution.py:530
  135.3 2.4 %collective-permute-start.8 = (f32[8,32]{1,0:T(8,128)S(1)}, f32[8,32]{1,0:T(8,128)S(1)}, u32[]{:S(2)}, u32[]{:S(2)}) collective-permute-start(f32[8,32]{1,0:T(8,128)S(1)} %score.3), channel_id=1, source_target_pairs={{0,1},{1,0},{2,3},{3,2},{4,5},{5,4},{6,7},{7,6},{8,9},{9,8},{10,11... | collective-permute-start | bytes 3080 | tf_op jit(solution)/shard_map/ppermute | solution.py:579
  139.3 3.1 %collective-permute-start.9 = (f32[8,32]{1,0:T(8,128)S(1)}, f32[8,32]{1,0:T(8,128)S(1)}, u32[]{:S(2)}, u32[]{:S(2)}) collective-permute-start(f32[8,32]{1,0:T(8,128)S(1)} %add.15), channel_id=1, source_target_pairs={{0,2},{1,3},{2,0},{3,1},{4,6},{5,7},{6,4},{7,5},{8,10},{9,11},{10,... | collective-permute-start | bytes 3080 | tf_op jit(solution)/shard_map/ppermute | solution.py:579
  145.1 2.1 %collective-permute-start.11 = (f32[8,32]{1,0:T(8,128)S(1)}, f32[8,32]{1,0:T(8,128)S(1)}, u32[]{:S(2)}, u32[]{:S(2)}) collective-permute-start(f32[8,32]{1,0:T(8,128)S(1)} %add.17), channel_id=1, source_target_pairs={{0,8},{4,12},{8,0},{12,4},{16,24},{20,28},{24,16},{28,20},{1,9},{5... | collective-permute-start | bytes 3080 | tf_op jit(solution)/shard_map/ppermute | solution.py:579
  147.2 4.9 %collective-permute-done.11 = f32[8,32]{1,0:T(8,128)S(1)} collective-permute-done((f32[8,32]{1,0:T(8,128)S(1)}, f32[8,32]{1,0:T(8,128)S(1)}, u32[]{:S(2)}, u32[]{:S(2)}) %collective-permute-start.11) | collective-permute-done | bytes 1056 | tf_op jit(solution)/shard_map/ppermute | solution.py:579
  153.5 2.1 %collective-permute-done.12 = f32[8,32]{1,0:T(8,128)S(1)} collective-permute-done((f32[8,32]{1,0:T(8,128)S(1)}, f32[8,32]{1,0:T(8,128)S(1)}, u32[]{:S(2)}, u32[]{:S(2)}) %collective-permute-start.12) | collective-permute-done | bytes 1056 | tf_op jit(solution)/shard_map/ppermute | solution.py:579
  (61 shorter events, 22.7 us)
Async XLA Ops:
  0.6 9.1 %copy-start.2 = (f32[4,2,16,2048]{3,2,1,0:T(8,128)S(1)}, f32[4,2,16,2048]{3,2,1,0:T(8,128)}, u32[]{:S(2)}) copy-start(f32[4,2,16,2048]{3,2,1,0:T(8,128)} %refs_0_.2) | copy-start | bytes 3145732
  3.5 15.4 %collective-permute-start = (f32[768,128]{1,0:T(8,128)S(1)}, f32[768,128]{1,0:T(8,128)S(1)}, u32[]{:S(2)}, u32[]{:S(2)}) collective-permute-start(f32[768,128]{1,0:T(8,128)S(1)} %get-tuple-element.45), channel_id=1, source_target_pairs={{0,1},{1,2},{2,3},{4,5},{5,6},{6,7},{8,9},{9,10},{10,11},{12,13},{... | collective-permute-start | bytes 1179656 | tf_op jit(solution)/shard_map/ppermute | solution.py:459
  8.4 12.5 %collective-permute-start.1 = (f32[768,128]{1,0:T(8,128)S(1)}, f32[768,128]{1,0:T(8,128)S(1)}, u32[]{:S(2)}, u32[]{:S(2)}) collective-permute-start(f32[768,128]{1,0:T(8,128)S(1)} %get-tuple-element.46), channel_id=1, source_target_pairs={{1,0},{2,1},{3,2},{5,4},{6,5},{7,6},{9,8},{10,9},{11,10},{13,12},{... | collective-permute-start | bytes 1179656 | tf_op jit(solution)/shard_map/ppermute | solution.py:460
  11.3 9.6 %copy-start.1 = (f32[2,4,2,16,2048]{4,3,2,1,0:T(8,128)S(1)}, f32[2,4,2,16,2048]{4,3,2,1,0:T(8,128)}, u32[]{:S(2)}) copy-start(f32[2,4,2,16,2048]{4,3,2,1,0:T(8,128)} %n_ref) | copy-start | bytes 6291460
  13.0 12.3 %collective-permute-start.2 = (f32[768,128]{1,0:T(8,128)S(1)}, f32[768,128]{1,0:T(8,128)S(1)}, u32[]{:S(2)}, u32[]{:S(2)}) collective-permute-start(f32[768,128]{1,0:T(8,128)S(1)} %get-tuple-element.48), channel_id=1, source_target_pairs={{0,1},{1,2},{2,3},{4,5},{5,6},{6,7},{8,9},{9,10},{10,11},{12,13},{... | collective-permute-start | bytes 1179656 | tf_op jit(solution)/shard_map/ppermute | solution.py:462
  17.5 12.0 %collective-permute-start.3 = (f32[768,128]{1,0:T(8,128)S(1)}, f32[768,128]{1,0:T(8,128)}, u32[]{:S(2)}, u32[]{:S(2)}) collective-permute-start(f32[768,128]{1,0:T(8,128)S(1)} %get-tuple-element.49), channel_id=1, source_target_pairs={{1,0},{2,1},{3,2},{5,4},{6,5},{7,6},{9,8},{10,9},{11,10},{13,12},{... | collective-permute-start | bytes 1179656 | tf_op jit(solution)/shard_map/ppermute | solution.py:463
  29.6 20.5 %all-to-all-start = ((f32[8,4,9,8,128]{4,3,2,1,0:T(8,128)}), f32[8,4,9,8,128]{4,3,2,1,0:T(8,128)S(1)}, u32[]{:S(2)}, u32[]{:S(2)}) async-start(f32[8,4,9,8,128]{4,3,2,1,0:T(8,128)} %pack_noise.1), calls=%async_computation | async-start | bytes 2359296 | tf_op jit(solution)/shard_map/all_to_all | solution.py:478
  70.3 20.4 %all-to-all-start.2 = ((f32[8,4,9,8,128]{4,3,2,1,0:T(8,128)}), f32[8,4,9,8,128]{4,3,2,1,0:T(8,128)S(1)}, u32[]{:S(2)}, u32[]{:S(2)}) async-start(f32[8,4,9,8,128]{4,3,2,1,0:T(8,128)} %get-tuple-element.58), calls=%async_computation.2 | async-start | bytes 2359296 | tf_op jit(solution)/shard_map/all_to_all | solution.py:501
  78.8 28.5 %collective-permute-start.5 = (f32[832,128]{1,0:T(8,128)}, f32[832,128]{1,0:T(8,128)S(1)}, u32[]{:S(2)}, u32[]{:S(2)}) collective-permute-start(f32[832,128]{1,0:T(8,128)} %get-tuple-element.68), channel_id=1, source_target_pairs={{0,1},{1,2},{2,3},{4,5},{5,6},{6,7},{8,9},{9,10},{10,11},{12,13},{... | collective-permute-start | bytes 1277960 | tf_op jit(solution)/shard_map/ppermute | solution.py:514
  82.3 25.1 %collective-permute-start.7 = (f32[832,128]{1,0:T(8,128)}, f32[832,128]{1,0:T(8,128)S(1)}, u32[]{:S(2)}, u32[]{:S(2)}) collective-permute-start(f32[832,128]{1,0:T(8,128)} %get-tuple-element.70), channel_id=1, source_target_pairs={{1,0},{2,1},{3,2},{5,4},{6,5},{7,6},{9,8},{10,9},{11,10},{13,12},{... | collective-permute-start | bytes 1277960 | tf_op jit(solution)/shard_map/ppermute | solution.py:515
  90.8 7.4 %copy-start.5 = (f32[2,512,128]{2,1,0:T(8,128)S(1)}, f32[2,512,128]{2,1,0:T(8,128)}, u32[]{:S(2)}) copy-start(f32[2,512,128]{2,1,0:T(8,128)} %get-tuple-element.63.z_ref) | copy-start | bytes 1572868
  90.8 7.4 %copy-start.7 = (f32[2,2,1024]{2,1,0:T(2,128)S(1)}, f32[2,2,1024]{2,1,0:T(2,128)}, u32[]{:S(2)}) copy-start(f32[2,2,1024]{2,1,0:T(2,128)} %o_ref.3) | copy-start | bytes 49156
  90.8 7.4 %copy-start.8 = (f32[2,2,1024]{2,1,0:T(2,128)S(1)}, f32[2,2,1024]{2,1,0:T(2,128)}, u32[]{:S(2)}) copy-start(f32[2,2,1024]{2,1,0:T(2,128)} %w_ref.3) | copy-start | bytes 49156
  90.8 7.4 %copy-start.9 = (s32[2,2]{1,0:T(2,128)S(1)}, s32[2,2]{1,0:T(2,128)}, u32[]{:S(2)}) copy-start(s32[2,2]{1,0:T(2,128)} %rows_ref.3) | copy-start | bytes 52
  93.3 14.0 %collective-permute-start.4 = (f32[832,128]{1,0:T(8,128)S(1)}, f32[832,128]{1,0:T(8,128)S(1)}, u32[]{:S(2)}, u32[]{:S(2)}) collective-permute-start(f32[832,128]{1,0:T(8,128)S(1)} %get-tuple-element.67), channel_id=1, source_target_pairs={{0,1},{1,2},{2,3},{4,5},{5,6},{6,7},{8,9},{9,10},{10,11},{12,13},{... | collective-permute-start | bytes 1277960 | tf_op jit(solution)/shard_map/ppermute | solution.py:514
  96.8 10.5 %collective-permute-start.6 = (f32[832,128]{1,0:T(8,128)S(1)}, f32[832,128]{1,0:T(8,128)S(1)}, u32[]{:S(2)}, u32[]{:S(2)}) collective-permute-start(f32[832,128]{1,0:T(8,128)S(1)} %get-tuple-element.69), channel_id=1, source_target_pairs={{1,0},{2,1},{3,2},{5,4},{6,5},{7,6},{9,8},{10,9},{11,10},{13,12},{... | collective-permute-start | bytes 1277960 | tf_op jit(solution)/shard_map/ppermute | solution.py:515
  98.2 9.2 %copy-start.3 = (f32[2048,128]{1,0:T(8,128)S(1)}, f32[2048,128]{1,0:T(8,128)}, u32[]{:S(2)}) copy-start(f32[2048,128]{1,0:T(8,128)} %get-tuple-element.64.p_main) | copy-start | bytes 3145732
  98.2 9.2 %copy-start.6 = (f32[256,128]{1,0:T(8,128)S(1)}, f32[256,128]{1,0:T(8,128)}, u32[]{:S(2)}) copy-start(f32[256,128]{1,0:T(8,128)} %get-tuple-element.66.p_edge) | copy-start | bytes 393220
  121.6 35.0 %all-to-all-start.3 = ((f32[8,4,128,128]{3,2,1,0:T(8,128)}), f32[8,4,128,128]{3,2,1,0:T(8,128)S(1)}, u32[]{:S(2)}, u32[]{:S(2)}) async-start(f32[8,4,128,128]{3,2,1,0:T(8,128)} %bitcast.12), calls=%async_computation.3 | async-start | bytes 4194304 | tf_op jit(solution)/shard_map/all_to_all | solution.py:565
  135.3 4.0 %collective-permute-start.8 = (f32[8,32]{1,0:T(8,128)S(1)}, f32[8,32]{1,0:T(8,128)S(1)}, u32[]{:S(2)}, u32[]{:S(2)}) collective-permute-start(f32[8,32]{1,0:T(8,128)S(1)} %score.3), channel_id=1, source_target_pairs={{0,1},{1,0},{2,3},{3,2},{4,5},{5,4},{6,7},{7,6},{8,9},{9,8},{10,11... | collective-permute-start | bytes 3080 | tf_op jit(solution)/shard_map/ppermute | solution.py:579
  139.3 4.6 %collective-permute-start.9 = (f32[8,32]{1,0:T(8,128)S(1)}, f32[8,32]{1,0:T(8,128)S(1)}, u32[]{:S(2)}, u32[]{:S(2)}) collective-permute-start(f32[8,32]{1,0:T(8,128)S(1)} %add.15), channel_id=1, source_target_pairs={{0,2},{1,3},{2,0},{3,1},{4,6},{5,7},{6,4},{7,5},{8,10},{9,11},{10,... | collective-permute-start | bytes 3080 | tf_op jit(solution)/shard_map/ppermute | solution.py:579
  143.9 1.2 collective-permute-start.10
  145.1 7.0 %collective-permute-start.11 = (f32[8,32]{1,0:T(8,128)S(1)}, f32[8,32]{1,0:T(8,128)S(1)}, u32[]{:S(2)}, u32[]{:S(2)}) collective-permute-start(f32[8,32]{1,0:T(8,128)S(1)} %add.17), channel_id=1, source_target_pairs={{0,8},{4,12},{8,0},{12,4},{16,24},{20,28},{24,16},{28,20},{1,9},{5... | collective-permute-start | bytes 3080 | tf_op jit(solution)/shard_map/ppermute | solution.py:579
  152.1 3.6 %collective-permute-start.12 = (f32[8,32]{1,0:T(8,128)S(1)}, f32[8,32]{1,0:T(8,128)S(1)}, u32[]{:S(2)}, u32[]{:S(2)}) collective-permute-start(f32[8,32]{1,0:T(8,128)S(1)} %add.18), channel_id=1, source_target_pairs={{0,16},{4,20},{8,24},{12,28},{16,0},{20,4},{24,8},{28,12},{1,17},{... | collective-permute-start | bytes 3080 | tf_op jit(solution)/shard_map/ppermute | solution.py:579
  (6 other events, 14.3 us)

commit v6 on v5

--- a/solution.py
+++ b/solution.py
@@ -575,9 +575,15 @@
     for axis, size in (("tile", tiles), ("dom", groups)):
         hop = 1
         while hop < size:
-            pairs = [(i, i ^ hop) for i in range(size)]
-            loglik = loglik + lax.ppermute(loglik, axis, pairs)
-            hop *= 2
+            def beside(step, value=loglik, axis=axis, size=size):
+                return lax.ppermute(value, axis, [(i, i ^ step) for i in range(size)])
+
+            if hop == 1 and (size.bit_length() - 1) % 2:
+                loglik = loglik + beside(1)
+                hop = 2
+            else:
+                loglik = (loglik + beside(hop)) + (beside(2 * hop) + beside(3 * hop))
+                hop *= 4
     loglik = loglik[:CYCLES]
     total_obs = observed.size * groups * tiles
     mean_loglik = loglik / total_obs

time: 159 us -> 156 us (0.981)
    ppermute x5 -> x7, waiting for transfers between devices: 11.3 us -> 9.92 us  [beside(): return lax.ppermute(value, axis, [(i, i ^ step) for i in range(size)])]
    ppermute x5 -> x7, starting transfers between devices: 9.06 us -> 7.89 us  [beside(): return lax.ppermute(value, axis, [(i, i ^ step) for i in range(size)])]
  transfers between devices with their start and end apart: 16 -> 18, of which waited for: 10 -> 11; matrix products, arithmetic and copies ran while one was open for 1% -> 1% of each run, Pallas kernels for 28% -> 28%
where the time goes in v6:
time: 156 us
  Pallas kernels  61.3 us (39%)
  starting transfers between devices  41.5 us (27%)
  waiting for transfers between devices  26.6 us (17%)
  blocking collectives  20.2 us (13%)
  local copies, waits for them, and re-layouts  3.69 us (2%)
    pallas_call x5, Pallas kernels, run(): pl.pallas_call(kernel, out_shape=[pltpu.HBM(o.shape, F32) if i in far els...  37.6 us
    all_to_all x1, blocking collectives, spread(): owned = lax.all_to_all(sent, 'dom', split_axis=0, concat_axis=0, tiled=True)  20.2 us
    pallas_call x2, Pallas kernels, likelihood(): pl.pallas_call(functools.partial(score, members=members, cycle=cycle), gr...  18.2 us
    ppermute x7, waiting for transfers between devices, beside(): return lax.ppermute(value, axis, [(i, i ^ step) for i in range(size)])  9.92 us
    ppermute x7, starting transfers between devices, beside(): return lax.ppermute(value, axis, [(i, i ^ step) for i in range(size)])  7.89 us
    all_to_all x1, waiting for transfers between devices, spread(): owned = lax.all_to_all(sent, 'dom', split_axis=0, concat_axis=0, tiled=True)  7.21 us
    ppermute x2, starting transfers between devices, exchange(): below = lax.ppermute(to_up, 'tile', up)  6.92 us
    ppermute x1, starting transfers between devices, shards(): p_below = lax.ppermute(p_up, 'tile', up)  4.95 us
  transfers between devices with their start and end apart: 18, of which 11 were waited for; matrix products, arithmetic and copies ran while one was open for 1% of the time, Pallas kernels for 28%

profile of v6, /device:TPU:0, one launch (start us, length us, event | category | flops | bytes accessed | tf_op | source)
XLA Modules:
  0.0 155.6 jit_solution(7972158689272948372)
XLA Ops:
  3.5 5.0 %collective-permute-start = (f32[768,128]{1,0:T(8,128)S(1)}, f32[768,128]{1,0:T(8,128)S(1)}, u32[]{:S(2)}, u32[]{:S(2)}) collective-permute-start(f32[768,128]{1,0:T(8,128)S(1)} %get-tuple-element.45), channel_id=1, source_target_pairs={{0,1},{1,2},{2,3},{4,5},{5,6},{6,7},{8,9},{9,10},{10,11},{12,13},{... | collective-permute-start | bytes 1179656 | tf_op jit(solution)/shard_map/ppermute | solution.py:459
  13.0 4.6 %collective-permute-start.2 = (f32[768,128]{1,0:T(8,128)S(1)}, f32[768,128]{1,0:T(8,128)S(1)}, u32[]{:S(2)}, u32[]{:S(2)}) collective-permute-start(f32[768,128]{1,0:T(8,128)S(1)} %get-tuple-element.48), channel_id=1, source_target_pairs={{0,1},{1,2},{2,3},{4,5},{5,6},{6,7},{8,9},{9,10},{10,11},{12,13},{... | collective-permute-start | bytes 1179656 | tf_op jit(solution)/shard_map/ppermute | solution.py:462
  18.9 2.0 %collective-permute-done.1.p_down = f32[768,128]{1,0:T(8,128)S(1)} collective-permute-done((f32[768,128]{1,0:T(8,128)S(1)}, f32[768,128]{1,0:T(8,128)S(1)}, u32[]{:S(2)}, u32[]{:S(2)}) %collective-permute-start.1) | collective-permute-done | bytes 393248 | tf_op jit(solution)/shard_map/ppermute | solution.py:460
  20.9 2.4 %pack_noise.1 = f32[8,4,9,8,128]{4,3,2,1,0:T(8,128)} custom-call(f32[2,4,2,16,2048]{4,3,2,1,0:T(8,128)S(1)} %copy-done.1), custom_call_target="tpu_custom_call" | custom-call | flops 1000 | bytes 1000 | tf_op jit(solution)/shard_map/pack_noise/pallas_call | solution.py:466
  23.4 2.0 %collective-permute-done.2.q_up = f32[768,128]{1,0:T(8,128)S(1)} collective-permute-done((f32[768,128]{1,0:T(8,128)S(1)}, f32[768,128]{1,0:T(8,128)S(1)}, u32[]{:S(2)}, u32[]{:S(2)}) %collective-permute-start.2) | collective-permute-done | bytes 393248 | tf_op jit(solution)/shard_map/ppermute | solution.py:462
  26.1 3.5 %collective-permute-done.3.q_down = f32[768,128]{1,0:T(8,128)} collective-permute-done((f32[768,128]{1,0:T(8,128)S(1)}, f32[768,128]{1,0:T(8,128)}, u32[]{:S(2)}, u32[]{:S(2)}) %collective-permute-start.3) | collective-permute-done | bytes 393248 | tf_op jit(solution)/shard_map/ppermute | solution.py:463
  29.6 3.7 %all-to-all-start = ((f32[8,4,9,8,128]{4,3,2,1,0:T(8,128)}), f32[8,4,9,8,128]{4,3,2,1,0:T(8,128)S(1)}, u32[]{:S(2)}, u32[]{:S(2)}) async-start(f32[8,4,9,8,128]{4,3,2,1,0:T(8,128)} %pack_noise.1), calls=%async_computation | async-start | bytes 2359296 | tf_op jit(solution)/shard_map/all_to_all | solution.py:478
  33.4 14.8 %advance_members.1 = (f32[8,4,9,8,128]{4,3,2,1,0:T(8,128)}, f32[8,4,9,8,128]{4,3,2,1,0:T(8,128)}) custom-call(s32[2]{0:T(128)S(1)} %pad_add_fusion.edge, f32[2048,128]{1,0:T(8,128)S(1)} %get-tuple-element.43.q_main, f32[2048,128]{1,0:T(8,128)S(1)} %get-tuple-element.44.p_main, f32[768,128]{1,0:T(8,128)} %copy-done.12, f32[768,128]{1,0:T(8,128)} %copy-done.10, ...), custom_call_target="tpu_custom_call" | custom-call | flops 1000 | bytes 1000 | tf_op jit(solution)/shard_map/advance_members/pallas_call | solution.py:404
  48.2 1.9 %all-to-all-done = f32[8,4,9,8,128]{4,3,2,1,0:T(8,128)S(1)} async-done(((f32[8,4,9,8,128]{4,3,2,1,0:T(8,128)}), f32[8,4,9,8,128]{4,3,2,1,0:T(8,128)S(1)}, u32[]{:S(2)}, u32[]{:S(2)}) %all-to-all-start) | async-done | bytes 1179680 | tf_op jit(solution)/shard_map/all_to_all | solution.py:478
  50.1 20.2 %all_to_all.20 = f32[8,4,9,8,128]{4,3,2,1,0:T(8,128)S(1)} all-to-all(f32[8,4,9,8,128]{4,3,2,1,0:T(8,128)} %get-tuple-element.57), channel_id=1, replica_groups=mesh['dom'=8,'tile'=4] {'dom'}, dimensions={0} | all-to-all | bytes 2359296 | tf_op jit(solution)/shard_map/all_to_all | solution.py:501
  70.3 3.7 %all-to-all-start.2 = ((f32[8,4,9,8,128]{4,3,2,1,0:T(8,128)}), f32[8,4,9,8,128]{4,3,2,1,0:T(8,128)S(1)}, u32[]{:S(2)}, u32[]{:S(2)}) async-start(f32[8,4,9,8,128]{4,3,2,1,0:T(8,128)} %get-tuple-element.58), calls=%async_computation.2 | async-start | bytes 2359296 | tf_op jit(solution)/shard_map/all_to_all | solution.py:501
  74.4 4.4 %resample_psi.1 = (f32[2048,128]{1,0:T(8,128)}, f32[256,128]{1,0:T(8,128)}, f32[832,128]{1,0:T(8,128)}, f32[832,128]{1,0:T(8,128)}, f32[2,512,128]{2,1,0:T(8,128)}) custom-call(s32[32]{0:T(128)S(1)} %get-tuple-element.78.parent, f32[32,72,128]{2,1,0:T(8,128)S(1)} %bitcast.11), custom_call_target="tpu_custom_call" | custom-call | flops 1000 | bytes 1000 | tf_op jit(solution)/shard_map/resample_psi/pallas_call | solution.py:404
  78.8 3.5 %collective-permute-start.5 = (f32[832,128]{1,0:T(8,128)}, f32[832,128]{1,0:T(8,128)S(1)}, u32[]{:S(2)}, u32[]{:S(2)}) collective-permute-start(f32[832,128]{1,0:T(8,128)} %get-tuple-element.68), channel_id=1, source_target_pairs={{0,1},{1,2},{2,3},{4,5},{5,6},{6,7},{8,9},{9,10},{10,11},{12,13},{... | collective-permute-start | bytes 1277960 | tf_op jit(solution)/shard_map/ppermute | solution.py:514
  83.6 7.2 %all-to-all-done.2 = f32[8,4,9,8,128]{4,3,2,1,0:T(8,128)S(1)} async-done(((f32[8,4,9,8,128]{4,3,2,1,0:T(8,128)}), f32[8,4,9,8,128]{4,3,2,1,0:T(8,128)S(1)}, u32[]{:S(2)}, u32[]{:S(2)}) %all-to-all-start.2) | async-done | bytes 1179680 | tf_op jit(solution)/shard_map/all_to_all | solution.py:501
  90.8 2.6 %resample_q.1 = (f32[2048,128]{1,0:T(8,128)S(1)}, f32[256,128]{1,0:T(8,128)S(1)}, f32[832,128]{1,0:T(8,128)S(1)}, f32[832,128]{1,0:T(8,128)S(1)}) custom-call(s32[32]{0:T(128)S(1)} %get-tuple-element.78.parent, f32[32,72,128]{2,1,0:T(8,128)S(1)} %bitcast.10, f32[32,72,128]{2,1,0:T(8,128)S(1)} %bitcast.9), custom_call_target="tpu_custom_call" | custom-call | flops 1000 | bytes 1000 | tf_op jit(solution)/shard_map/resample_q/pallas_call | solution.py:404
  93.3 3.5 %collective-permute-start.4 = (f32[832,128]{1,0:T(8,128)S(1)}, f32[832,128]{1,0:T(8,128)S(1)}, u32[]{:S(2)}, u32[]{:S(2)}) collective-permute-start(f32[832,128]{1,0:T(8,128)S(1)} %get-tuple-element.67), channel_id=1, source_target_pairs={{0,1},{1,2},{2,3},{4,5},{5,6},{6,7},{8,9},{9,10},{10,11},{12,13},{... | collective-permute-start | bytes 1277960 | tf_op jit(solution)/shard_map/ppermute | solution.py:514
  98.2 9.1 %score.2.first_ref = f32[8,32]{1,0:T(8,128)S(1)} custom-call(s32[2,2]{1,0:T(2,128)S(1)} %copy-done.9, f32[2,512,128]{2,1,0:T(8,128)S(1)} %copy-done.5, f32[2,2,1024,1024]{3,2,1,0:T(8,128)} %f_ref.3, f32[2,2,1024]{2,1,0:T(2,128)S(1)} %copy-done.7, f32[2,2,1024]{2,1,0:T(2,128)S(1)} %copy-done.8, f32[8,32]{1,0:T(8,128)S(1)} %broadcast_in_dim.2.first_ref), custom_call_target="tpu_custom_call" | custom-call | flops 1000 | bytes 1000 | tf_op jit(solution)/shard_map/score/pallas_call | solution.py:530
  107.4 14.2 %advance_columns.1 = (f32[32,16,8,128]{3,2,1,0:T(8,128)}, f32[2,512,128]{2,1,0:T(8,128)S(1)}) custom-call(s32[2]{0:T(128)S(1)} %pad_add_fusion.edge, s32[32]{0:T(128)S(1)} %get-tuple-element.79.parent, f32[2048,128]{1,0:T(8,128)S(1)} %get-tuple-element.60.q_main, f32[2048,128]{1,0:T(8,128)S(1)} %copy-done.3, f32[256,128]{1,0:T(8,128)S(1)} %get-tuple-element.65.q_edge, ...), custom_call_target="tpu_custom_call" | custom-call | flops 1000 | bytes 1000 | tf_op jit(solution)/shard_map/advance_columns/pallas_call | solution.py:404
  121.6 4.6 %all-to-all-start.3 = ((f32[8,4,128,128]{3,2,1,0:T(8,128)}), f32[8,4,128,128]{3,2,1,0:T(8,128)S(1)}, u32[]{:S(2)}, u32[]{:S(2)}) async-start(f32[8,4,128,128]{3,2,1,0:T(8,128)} %bitcast.12), calls=%async_computation.3 | async-start | bytes 4194304 | tf_op jit(solution)/shard_map/all_to_all | solution.py:565
  126.2 9.0 %score.3 = f32[8,32]{1,0:T(8,128)S(1)} custom-call(s32[2,2]{1,0:T(2,128)S(1)} %copy-done.9, f32[2,512,128]{2,1,0:T(8,128)S(1)} %get-tuple-element.74.z_ref, f32[2,2,1024,1024]{3,2,1,0:T(8,128)} %f_ref.3, f32[2,2,1024]{2,1,0:T(2,128)S(1)} %copy-done.7, f32[2,2,1024]{2,1,0:T(2,128)S(1)} %copy-done.8, f32[8,32]{1,0:T(8,128)S(1)} %score.2.first_ref), custom_call_target="tpu_custom_call" | custom-call | flops 1000 | bytes 1000 | tf_op jit(solution)/shard_map/score/pallas_call | solution.py:530
  135.3 2.2 %collective-permute-start.10 = (f32[8,32]{1,0:T(8,128)S(1)}, f32[8,32]{1,0:T(8,128)S(1)}, u32[]{:S(2)}, u32[]{:S(2)}) collective-permute-start(f32[8,32]{1,0:T(8,128)S(1)} %score.3), channel_id=1, source_target_pairs={{0,3},{1,2},{2,1},{3,0},{4,7},{5,6},{6,5},{7,4},{8,11},{9,10},{10,... | collective-permute-start | bytes 3080 | tf_op jit(solution)/shard_map/ppermute | solution.py:579
  141.0 2.8 %collective-permute-done.9 = f32[8,32]{1,0:T(8,128)S(1)} collective-permute-done((f32[8,32]{1,0:T(8,128)S(1)}, f32[8,32]{1,0:T(8,128)S(1)}, u32[]{:S(2)}, u32[]{:S(2)}) %collective-permute-start.9) | collective-permute-done | bytes 1056 | tf_op jit(solution)/shard_map/ppermute | solution.py:579
  145.0 1.9 %collective-permute-start.12 = (f32[8,32]{1,0:T(8,128)S(1)}, f32[8,32]{1,0:T(8,128)S(1)}, u32[]{:S(2)}, u32[]{:S(2)}) collective-permute-start(f32[8,32]{1,0:T(8,128)S(1)} %add.24), channel_id=1, source_target_pairs={{0,8},{4,12},{8,0},{12,4},{16,24},{20,28},{24,16},{28,20},{1,9},{5... | collective-permute-start | bytes 3080 | tf_op jit(solution)/shard_map/ppermute | solution.py:579
  148.5 3.6 %collective-permute-done.12 = f32[8,32]{1,0:T(8,128)S(1)} collective-permute-done((f32[8,32]{1,0:T(8,128)S(1)}, f32[8,32]{1,0:T(8,128)S(1)}, u32[]{:S(2)}, u32[]{:S(2)}) %collective-permute-start.12) | collective-permute-done | bytes 1056 | tf_op jit(solution)/shard_map/ppermute | solution.py:579
  (63 shorter events, 22.3 us)
Async XLA Ops:
  0.6 9.1 %copy-start.2 = (f32[4,2,16,2048]{3,2,1,0:T(8,128)S(1)}, f32[4,2,16,2048]{3,2,1,0:T(8,128)}, u32[]{:S(2)}) copy-start(f32[4,2,16,2048]{3,2,1,0:T(8,128)} %refs_0_.2) | copy-start | bytes 3145732
  3.5 15.4 %collective-permute-start = (f32[768,128]{1,0:T(8,128)S(1)}, f32[768,128]{1,0:T(8,128)S(1)}, u32[]{:S(2)}, u32[]{:S(2)}) collective-permute-start(f32[768,128]{1,0:T(8,128)S(1)} %get-tuple-element.45), channel_id=1, source_target_pairs={{0,1},{1,2},{2,3},{4,5},{5,6},{6,7},{8,9},{9,10},{10,11},{12,13},{... | collective-permute-start | bytes 1179656 | tf_op jit(solution)/shard_map/ppermute | solution.py:459
  8.4 12.5 %collective-permute-start.1 = (f32[768,128]{1,0:T(8,128)S(1)}, f32[768,128]{1,0:T(8,128)S(1)}, u32[]{:S(2)}, u32[]{:S(2)}) collective-permute-start(f32[768,128]{1,0:T(8,128)S(1)} %get-tuple-element.46), channel_id=1, source_target_pairs={{1,0},{2,1},{3,2},{5,4},{6,5},{7,6},{9,8},{10,9},{11,10},{13,12},{... | collective-permute-start | bytes 1179656 | tf_op jit(solution)/shard_map/ppermute | solution.py:460
  11.3 9.6 %copy-start.1 = (f32[2,4,2,16,2048]{4,3,2,1,0:T(8,128)S(1)}, f32[2,4,2,16,2048]{4,3,2,1,0:T(8,128)}, u32[]{:S(2)}) copy-start(f32[2,4,2,16,2048]{4,3,2,1,0:T(8,128)} %n_ref) | copy-start | bytes 6291460
  13.0 12.3 %collective-permute-start.2 = (f32[768,128]{1,0:T(8,128)S(1)}, f32[768,128]{1,0:T(8,128)S(1)}, u32[]{:S(2)}, u32[]{:S(2)}) collective-permute-start(f32[768,128]{1,0:T(8,128)S(1)} %get-tuple-element.48), channel_id=1, source_target_pairs={{0,1},{1,2},{2,3},{4,5},{5,6},{6,7},{8,9},{9,10},{10,11},{12,13},{... | collective-permute-start | bytes 1179656 | tf_op jit(solution)/shard_map/ppermute | solution.py:462
  17.5 12.0 %collective-permute-start.3 = (f32[768,128]{1,0:T(8,128)S(1)}, f32[768,128]{1,0:T(8,128)}, u32[]{:S(2)}, u32[]{:S(2)}) collective-permute-start(f32[768,128]{1,0:T(8,128)S(1)} %get-tuple-element.49), channel_id=1, source_target_pairs={{1,0},{2,1},{3,2},{5,4},{6,5},{7,6},{9,8},{10,9},{11,10},{13,12},{... | collective-permute-start | bytes 1179656 | tf_op jit(solution)/shard_map/ppermute | solution.py:463
  29.6 20.5 %all-to-all-start = ((f32[8,4,9,8,128]{4,3,2,1,0:T(8,128)}), f32[8,4,9,8,128]{4,3,2,1,0:T(8,128)S(1)}, u32[]{:S(2)}, u32[]{:S(2)}) async-start(f32[8,4,9,8,128]{4,3,2,1,0:T(8,128)} %pack_noise.1), calls=%async_computation | async-start | bytes 2359296 | tf_op jit(solution)/shard_map/all_to_all | solution.py:478
  70.3 20.4 %all-to-all-start.2 = ((f32[8,4,9,8,128]{4,3,2,1,0:T(8,128)}), f32[8,4,9,8,128]{4,3,2,1,0:T(8,128)S(1)}, u32[]{:S(2)}, u32[]{:S(2)}) async-start(f32[8,4,9,8,128]{4,3,2,1,0:T(8,128)} %get-tuple-element.58), calls=%async_computation.2 | async-start | bytes 2359296 | tf_op jit(solution)/shard_map/all_to_all | solution.py:501
  78.8 28.5 %collective-permute-start.5 = (f32[832,128]{1,0:T(8,128)}, f32[832,128]{1,0:T(8,128)S(1)}, u32[]{:S(2)}, u32[]{:S(2)}) collective-permute-start(f32[832,128]{1,0:T(8,128)} %get-tuple-element.68), channel_id=1, source_target_pairs={{0,1},{1,2},{2,3},{4,5},{5,6},{6,7},{8,9},{9,10},{10,11},{12,13},{... | collective-permute-start | bytes 1277960 | tf_op jit(solution)/shard_map/ppermute | solution.py:514
  82.3 25.1 %collective-permute-start.7 = (f32[832,128]{1,0:T(8,128)}, f32[832,128]{1,0:T(8,128)S(1)}, u32[]{:S(2)}, u32[]{:S(2)}) collective-permute-start(f32[832,128]{1,0:T(8,128)} %get-tuple-element.70), channel_id=1, source_target_pairs={{1,0},{2,1},{3,2},{5,4},{6,5},{7,6},{9,8},{10,9},{11,10},{13,12},{... | collective-permute-start | bytes 1277960 | tf_op jit(solution)/shard_map/ppermute | solution.py:515
  90.8 7.4 %copy-start.8 = (f32[2,2,1024]{2,1,0:T(2,128)S(1)}, f32[2,2,1024]{2,1,0:T(2,128)}, u32[]{:S(2)}) copy-start(f32[2,2,1024]{2,1,0:T(2,128)} %w_ref.3) | copy-start | bytes 49156
  90.8 7.4 %copy-start.9 = (s32[2,2]{1,0:T(2,128)S(1)}, s32[2,2]{1,0:T(2,128)}, u32[]{:S(2)}) copy-start(s32[2,2]{1,0:T(2,128)} %rows_ref.3) | copy-start | bytes 52
  93.3 14.0 %collective-permute-start.4 = (f32[832,128]{1,0:T(8,128)S(1)}, f32[832,128]{1,0:T(8,128)S(1)}, u32[]{:S(2)}, u32[]{:S(2)}) collective-permute-start(f32[832,128]{1,0:T(8,128)S(1)} %get-tuple-element.67), channel_id=1, source_target_pairs={{0,1},{1,2},{2,3},{4,5},{5,6},{6,7},{8,9},{9,10},{10,11},{12,13},{... | collective-permute-start | bytes 1277960 | tf_op jit(solution)/shard_map/ppermute | solution.py:514
  96.8 10.5 %collective-permute-start.6 = (f32[832,128]{1,0:T(8,128)S(1)}, f32[832,128]{1,0:T(8,128)S(1)}, u32[]{:S(2)}, u32[]{:S(2)}) collective-permute-start(f32[832,128]{1,0:T(8,128)S(1)} %get-tuple-element.69), channel_id=1, source_target_pairs={{1,0},{2,1},{3,2},{5,4},{6,5},{7,6},{9,8},{10,9},{11,10},{13,12},{... | collective-permute-start | bytes 1277960 | tf_op jit(solution)/shard_map/ppermute | solution.py:515
  98.2 9.2 %copy-start.3 = (f32[2048,128]{1,0:T(8,128)S(1)}, f32[2048,128]{1,0:T(8,128)}, u32[]{:S(2)}) copy-start(f32[2048,128]{1,0:T(8,128)} %get-tuple-element.64.p_main) | copy-start | bytes 3145732
  98.2 9.2 %copy-start.6 = (f32[256,128]{1,0:T(8,128)S(1)}, f32[256,128]{1,0:T(8,128)}, u32[]{:S(2)}) copy-start(f32[256,128]{1,0:T(8,128)} %get-tuple-element.66.p_edge) | copy-start | bytes 393220
  121.6 32.4 %all-to-all-start.3 = ((f32[8,4,128,128]{3,2,1,0:T(8,128)}), f32[8,4,128,128]{3,2,1,0:T(8,128)S(1)}, u32[]{:S(2)}, u32[]{:S(2)}) async-start(f32[8,4,128,128]{3,2,1,0:T(8,128)} %bitcast.12), calls=%async_computation.3 | async-start | bytes 4194304 | tf_op jit(solution)/shard_map/all_to_all | solution.py:565
  135.3 5.4 %collective-permute-start.10 = (f32[8,32]{1,0:T(8,128)S(1)}, f32[8,32]{1,0:T(8,128)S(1)}, u32[]{:S(2)}, u32[]{:S(2)}) collective-permute-start(f32[8,32]{1,0:T(8,128)S(1)} %score.3), channel_id=1, source_target_pairs={{0,3},{1,2},{2,1},{3,0},{4,7},{5,6},{6,5},{7,4},{8,11},{9,10},{10,... | collective-permute-start | bytes 3080 | tf_op jit(solution)/shard_map/ppermute | solution.py:579
  137.4 3.6 %collective-permute-start.8 = (f32[8,32]{1,0:T(8,128)S(1)}, f32[8,32]{1,0:T(8,128)S(1)}, u32[]{:S(2)}, u32[]{:S(2)}) collective-permute-start(f32[8,32]{1,0:T(8,128)S(1)} %score.3), channel_id=1, source_target_pairs={{0,1},{1,0},{2,3},{3,2},{4,5},{5,4},{6,7},{7,6},{8,9},{9,8},{10,11... | collective-permute-start | bytes 3080 | tf_op jit(solution)/shard_map/ppermute | solution.py:579
  139.3 4.5 %collective-permute-start.9 = (f32[8,32]{1,0:T(8,128)S(1)}, f32[8,32]{1,0:T(8,128)S(1)}, u32[]{:S(2)}, u32[]{:S(2)}) collective-permute-start(f32[8,32]{1,0:T(8,128)S(1)} %score.3), channel_id=1, source_target_pairs={{0,2},{1,3},{2,0},{3,1},{4,6},{5,7},{6,4},{7,5},{8,10},{9,11},{10,... | collective-permute-start | bytes 3080 | tf_op jit(solution)/shard_map/ppermute | solution.py:579
  143.8 1.2 collective-permute-start.11
  145.0 7.1 %collective-permute-start.12 = (f32[8,32]{1,0:T(8,128)S(1)}, f32[8,32]{1,0:T(8,128)S(1)}, u32[]{:S(2)}, u32[]{:S(2)}) collective-permute-start(f32[8,32]{1,0:T(8,128)S(1)} %add.24), channel_id=1, source_target_pairs={{0,8},{4,12},{8,0},{12,4},{16,24},{20,28},{24,16},{28,20},{1,9},{5... | collective-permute-start | bytes 3080 | tf_op jit(solution)/shard_map/ppermute | solution.py:579
  146.9 5.2 %collective-permute-start.13 = (f32[8,32]{1,0:T(8,128)S(1)}, f32[8,32]{1,0:T(8,128)S(1)}, u32[]{:S(2)}, u32[]{:S(2)}) collective-permute-start(f32[8,32]{1,0:T(8,128)S(1)} %add.24), channel_id=1, source_target_pairs={{0,16},{4,20},{8,24},{12,28},{16,0},{20,4},{24,8},{28,12},{1,17},{... | collective-permute-start | bytes 3080 | tf_op jit(solution)/shard_map/ppermute | solution.py:579
  148.4 4.7 %collective-permute-start.14 = (f32[8,32]{1,0:T(8,128)S(1)}, f32[8,32]{1,0:T(8,128)S(1)}, u32[]{:S(2)}, u32[]{:S(2)}) collective-permute-start(f32[8,32]{1,0:T(8,128)S(1)} %add.24), channel_id=1, source_target_pairs={{0,24},{4,28},{8,16},{12,20},{16,8},{20,12},{24,0},{28,4},{1,25},{... | collective-permute-start | bytes 3080 | tf_op jit(solution)/shard_map/ppermute | solution.py:579
  (8 other events, 29.0 us)
